TPU v7x, 32 devices: a whole 2x2x4 slice. The times are simulated.
32 devices in a mesh: grp: 2 (over y), depth: 4 (over z), rows: 4 (over x, core).
Axes of the slice: x: 2, y: 2, z: 4, core: 2. Of those that a mesh axis runs over, the one named last changes fastest.
Arguments:
- volume: bfloat16 [16, 64, 256, 128], P(('grp', 'depth'), None, 'rows'), parts along dimension 0, may hold values from -6 to 6
- conv_one: bfloat16 [3, 3, 128, 128], replicated, may hold values from -0.1875 to 0.1875
- bias_one: float32 [128], replicated, may hold values from -3 to 3
- conv_two: bfloat16 [3, 3, 128, 128], replicated, may hold values from -0.1875 to 0.1875
- bias_two: float32 [128], replicated, may hold values from -3 to 3
- opacity_weight: float32 [128], replicated, may hold values from -0.5 to 0.5
- opacity_bias: float32 [8], P('depth'), may hold values from -5 to -2.5
Outputs:
- image: float32 [128, 256, 128], P(('grp', 'depth'), 'rows'), parts along dimension 0
There are 2 independent parts, one for each index of `grp`. A program takes and returns all parts, laid end to end along the dimension named above; an argument that names none is the same for every part. Nothing has to cross between parts.
All inputs are finite; a program needn't handle non-finite values.
Results may differ from a plain program's by a relative error of at most 0.0016.
Values may be sent and summed in bfloat16 or wider, within the bound.
No kernel may reach another device: no remote copies, remote signals or barrier semaphores. Data moves between devices by JAX's collectives and lax.ppermute only.
A program may use at most 64 MiB of HBM per device.

v0:
```python
import jax
import jax.numpy as jnp
from jax import lax
from jax.sharding import PartitionSpec as P


def padded_2(array, sides, width):
    for axis, dim in sides:
        size, length = (lax.axis_size(axis), array.shape[dim])
        up = [(i, (i + 1) % size) for i in range(size - 1)]
        down = [(j, i) for i, j in up]
        last = lax.slice_in_dim(array, length - width, length, axis=dim)
        leading = lax.slice_in_dim(array, 0, width, axis=dim)
        before = lax.ppermute(last, axis, up)
        after = lax.ppermute(leading, axis, down)
        array = jnp.concatenate([before, array, after], axis=dim)
    return array


def from_partner(value, axis, stride):
    mask = 2**stride
    pairs = [(source, source ^ mask) for source in range(lax.axis_size(axis))]
    return lax.ppermute(value, axis, pairs)


def convolve_rows(block, kernel, bias):
    out = lax.conv_general_dilated(
        block,
        kernel,
        (1, 1),
        ((1, 1), (0, 0)),
        dimension_numbers=("NHWC", "HWIO", "NHWC"),
        preferred_element_type=jnp.float32,
    )
    return out + bias


def pick_half(array, remaining, bit_set):
    shaped = array.reshape((remaining // 2, 2, -1) + array.shape[1:])
    first_half = shaped[:, 0].reshape((-1,) + array.shape[1:])
    second_half = shaped[:, 1].reshape((-1,) + array.shape[1:])
    keep = jnp.where(bit_set, second_half, first_half)
    other = jnp.where(bit_set, first_half, second_half)
    return (keep, other)


def per_device(volume, conv_one, bias_one, conv_two, bias_two, opacity_weight, opacity_bias):
    padded = padded_2(volume, (("rows", 2),), 1)
    hidden = jax.nn.gelu(convolve_rows(padded, conv_one, bias_one)).astype(jnp.bfloat16)
    hidden_pad = padded_2(hidden, (("rows", 2),), 1)
    features = jax.nn.gelu(convolve_rows(hidden_pad, conv_two, bias_two))
    logits = jnp.sum(features * opacity_weight, axis=-1) + opacity_bias[:, None, None]
    alpha = jax.nn.sigmoid(logits)
    color = jnp.zeros(features.shape[1:], jnp.float32)
    trans = jnp.ones(alpha.shape[1:], jnp.float32)
    for plane in range(features.shape[0]):
        color = color + (trans * alpha[plane])[..., None] * features[plane]
        trans = trans * (1.0 - alpha[plane])
    position = lax.axis_index("depth")
    slabs = lax.axis_size("depth")
    for level in range(slabs.bit_length() - 1):
        remaining = slabs >> level
        bit_set = jnp.right_shift(position, level) % 2 == 1
        keep_color, send_color = pick_half(color, remaining, bit_set)
        keep_trans, send_trans = pick_half(trans, remaining, bit_set)
        got_color, got_trans = from_partner((send_color, send_trans), "depth", level)
        color = jnp.where(
            bit_set,
            got_color + got_trans[..., None] * keep_color,
            keep_color + keep_trans[..., None] * got_color,
        )
        trans = keep_trans * got_trans
    return color


def solution(mesh):
    in_specs = (P(("grp", "depth"), None, "rows", None), P(), P(), P(), P(), P(), P("depth"))
    out_specs = P(("grp", "depth"), "rows", None)
    return jax.shard_map(
        per_device, mesh=mesh, in_specs=in_specs, out_specs=out_specs, check_vma=False
    )
```

profile of v0, /device:TPU:1, one launch (start us, length us, event | category | flops | bytes accessed | tf_op | source)
XLA Modules:
  0.0 108.9 jit_solution(14130880989977997727)
XLA Ops:
  0.0 3.0 %copy.34 = bf16[2,64,64,128]{3,1,2,0:T(8,128)(2,1)S(1)} copy(bf16[2,64,64,128]{3,2,1,0:T(8,128)(2,1)} %param.7) | data formatting | bytes 4194304 | tf_op args[0]
  3.0 4.5 %collective-permute-start = (bf16[2,64,1,128]{3,1,2,0:T(8,128)(2,1)S(1)}, bf16[2,64,1,128]{3,1,2,0:T(8,128)(2,1)S(1)}, u32[]{:S(2)}, u32[]{:S(2)}) collective-permute-start(bf16[2,64,1,128]{3,1,2,0:T(8,128)(2,1)S(1)} %get-tuple-element.11), channel_id=1, source_target_pairs={{0,1},{1,2},{2,3},{4,5},{5,6},{6,7},{8,9},{9,10},{10,11},{12,13},{... | collective-permute-start | bytes 98312 | tf_op jit(solution)/shard_map/ppermute | solution.py:14
  7.5 1.9 %collective-permute-start.1 = (bf16[2,64,1,128]{3,1,2,0:T(8,128)(2,1)S(1)}, bf16[2,64,1,128]{3,1,2,0:T(8,128)(2,1)S(1)}, u32[]{:S(2)}, u32[]{:S(2)}) collective-permute-start(bf16[2,64,1,128]{3,1,2,0:T(8,128)(2,1)S(1)} %get-tuple-element.12), channel_id=1, source_target_pairs={{1,0},{2,1},{3,2},{5,4},{6,5},{7,6},{9,8},{10,9},{11,10},{13,12},{... | collective-permute-start | bytes 98312 | tf_op jit(solution)/shard_map/ppermute | solution.py:15
  9.5 3.3 %collective-permute-done.1 = bf16[2,64,1,128]{3,1,2,0:T(8,128)(2,1)S(1)} collective-permute-done((bf16[2,64,1,128]{3,1,2,0:T(8,128)(2,1)S(1)}, bf16[2,64,1,128]{3,1,2,0:T(8,128)(2,1)S(1)}, u32[]{:S(2)}, u32[]{:S(2)}) %collective-permute-start.1) | collective-permute-done | bytes 32800 | tf_op jit(solution)/shard_map/ppermute | solution.py:15
  12.8 0.3 maximum_bitcast_fusion
  13.0 0.5 pad
  13.6 0.8 fusion.17
  14.5 10.6 %fusion.9 = bf16[64,16,9,128]{3,1,2,0:T(8,128)(2,1)S(1)} fusion(f32[128]{0:T(128)S(1)} %copy-done.3, pred[16,9]{0,1:T(8,128)(4,1)S(1)} %copy-done.6, bf16[3,3,128,128]{3,2,1,0:T(8,128)(2,1)S(1)} %copy-done.2, bf16[64,2,8,11,128]{4,0,3,2,1:T(8,128)(2,1)S(1)} %fusion.17), kind=kOutput, calls=%fused_computation.12 | convolution fusion | flops 2702573568 | bytes 5538448 | tf_op jit(solution)/shard_map/conv_general_dilated | solution.py:27
  25.1 0.6 copy.38
  25.7 0.2 slice_bitcast_fusion.1
  25.9 1.9 %collective-permute-start.2 = (bf16[2,64,1,128]{3,1,2,0:T(8,128)(2,1)S(1)}, bf16[2,64,1,128]{3,1,2,0:T(8,128)(2,1)S(1)}, u32[]{:S(2)}, u32[]{:S(2)}) collective-permute-start(bf16[2,64,1,128]{3,1,2,0:T(8,128)(2,1)S(1)} %get-tuple-element.9), channel_id=1, source_target_pairs={{0,1},{1,2},{2,3},{4,5},{5,6},{6,7},{8,9},{9,10},{10,11},{12,13},{... | collective-permute-start | bytes 98312 | tf_op jit(solution)/shard_map/ppermute | solution.py:14
  27.9 2.4 %collective-permute-start.3 = (bf16[2,64,1,128]{3,1,2,0:T(8,128)(2,1)S(1)}, bf16[2,64,1,128]{3,1,2,0:T(8,128)(2,1)S(1)}, u32[]{:S(2)}, u32[]{:S(2)}) collective-permute-start(bf16[2,64,1,128]{3,1,2,0:T(8,128)(2,1)S(1)} %get-tuple-element.10), channel_id=1, source_target_pairs={{1,0},{2,1},{3,2},{5,4},{6,5},{7,6},{9,8},{10,9},{11,10},{13,12},{... | collective-permute-start | bytes 98312 | tf_op jit(solution)/shard_map/ppermute | solution.py:15
  30.4 2.7 %collective-permute-done.3 = bf16[2,64,1,128]{3,1,2,0:T(8,128)(2,1)S(1)} collective-permute-done((bf16[2,64,1,128]{3,1,2,0:T(8,128)(2,1)S(1)}, bf16[2,64,1,128]{3,1,2,0:T(8,128)(2,1)S(1)}, u32[]{:S(2)}, u32[]{:S(2)}) %collective-permute-start.3) | collective-permute-done | bytes 32800 | tf_op jit(solution)/shard_map/ppermute | solution.py:15
  33.1 0.3 maximum_bitcast_fusion.1
  33.4 0.5 pad.2
  33.9 0.8 fusion.18
  34.7 12.4 %multiply_reduce_fusion = (f32[64,16,9]{1,2,0:T(8,128)S(1)}, f32[64,16,9,128]{3,1,2,0:T(8,128)}) fusion(f32[128]{0:T(128)S(1)} %copy-done.4, f32[128]{0:T(128)S(1)} %copy-done.5, bf16[3,3,128,128]{3,2,1,0:T(8,128)(2,1)S(1)} %copy-done, bf16[64,2,8,11,128]{4,0,3,2,1:T(8,128)(2,1)S(1)} %fusion.18, pred[16,9]{0,1:T(8,128)(4,1)S(1)} %copy-done.6), kind=kOutput, calls=%fused_computation.20 | convolution fusion | flops 2703744000 | bytes 7935120 | tf_op jit(solution)/shard_map/conv_general_dilated | solution.py:27
  47.2 0.2 copy.40
  47.6 3.9 %copy.44 = f32[64,16,9,128]{3,0,2,1:T(8,128)S(1)} copy(f32[64,16,9,128]{3,1,2,0:T(8,128)} %get-tuple-element.22) | data formatting | bytes 9437184 | tf_op jit(solution)/shard_map/mul | solution.py:51
  51.5 0.6 slice_bitcast_fusion
  52.1 0.3 fusion.37
  52.4 1.2 %copy.45 = f32[1,64,64,128]{3,2,1,0:T(8,128)S(1)} copy(f32[1,64,64,128]{3,1,2,0:T(8,128)S(1)} %get-tuple-element.5) | data formatting | bytes 4194304 | tf_op jit(solution)/shard_map/slice | solution.py:57
  53.6 1.2 %copy.47 = f32[1,64,64,128]{3,2,1,0:T(8,128)S(1)} copy(f32[1,64,64,128]{3,1,2,0:T(8,128)S(1)} %get-tuple-element.6) | data formatting | bytes 4194304 | tf_op jit(solution)/shard_map/slice | solution.py:57
  54.9 1.3 %multiply_add_fusion = f32[2,2,16,64,128]{4,3,2,1,0:T(8,128)S(1)} fusion(f32[2,2,16,64,128]{4,3,2,1,0:T(8,128)S(1)} %bitcast.75, f32[2,2,16,64,128]{4,3,2,1,0:T(8,128)S(1)} %bitcast.74, f32[2,2,16,64]{3,2,1,0:T(8,128)S(1)} %get-tuple-element.14, f32[2,2,16,64]{3,2,1,0:T(8,128)S(1)} %bitcast.78), kind=kLoop, calls=%fused_computation.33 | loop fusion | flops 1572864 | bytes 6324224 | tf_op jit(solution)/shard_map/add | solution.py:57
  56.1 0.3 slice_select_fusion
  56.4 1.4 %collective-permute-start.4 = (f32[32,64,128]{2,1,0:T(8,128)S(1)}, f32[32,64,128]{2,1,0:T(8,128)S(1)}, u32[]{:S(2)}, u32[]{:S(2)}) collective-permute-start(f32[32,64,128]{2,1,0:T(8,128)S(1)} %bitcast.76), channel_id=1, source_target_pairs={{0,4},{4,0},{8,12},{12,8},{1,5},{5,1},{9,13},{13,9},{2,6},{6,2},{1... | collective-permute-start | bytes 3145736 | tf_op jit(solution)/shard_map/ppermute | solution.py:23
  57.8 0.2 collective-permute-start.5
  58.0 22.6 %collective-permute-done.5 = f32[32,64]{1,0:T(8,128)S(1)} collective-permute-done((f32[32,64]{1,0:T(8,128)S(1)}, f32[32,64]{1,0:T(8,128)S(1)}, u32[]{:S(2)}, u32[]{:S(2)}) %collective-permute-start.5) | collective-permute-done | bytes 8224 | tf_op jit(solution)/shard_map/ppermute | solution.py:23
  80.5 0.8 fusion.30
  81.4 2.4 %collective-permute-start.6 = (f32[16,64,128]{2,1,0:T(8,128)S(1)}, f32[16,64,128]{2,1,0:T(8,128)S(1)}, u32[]{:S(2)}, u32[]{:S(2)}) collective-permute-start(f32[16,64,128]{2,1,0:T(8,128)S(1)} %select_bitcast_fusion), channel_id=1, source_target_pairs={{0,8},{4,12},{8,0},{12,4},{1,9},{5,13},{9,1},{13,5},{2,10},{6,14},... | collective-permute-start | bytes 1572872 | tf_op jit(solution)/shard_map/ppermute | solution.py:23
  83.9 23.9 %collective-permute-done.7 = f32[16,64]{1,0:T(8,128)S(1)} collective-permute-done((f32[16,64]{1,0:T(8,128)S(1)}, f32[16,64]{1,0:T(8,128)S(1)}, u32[]{:S(2)}, u32[]{:S(2)}) %collective-permute-start.7) | collective-permute-done | bytes 4128 | tf_op jit(solution)/shard_map/ppermute | solution.py:23
  107.8 1.1 %fusion.32 = f32[16,64,128]{2,1,0:T(8,128)} fusion(f32[16,64,128]{2,1,0:T(8,128)S(1)} %collective-permute-done.6, f32[1,2,16,64,128]{4,3,2,1,0:T(8,128)S(1)} %bitcast.72, f32[16,64]{1,0:T(8,128)S(1)} %get-tuple-element.20, f32[16,64]{1,0:T(8,128)S(1)} %collective-permute-done.7, pred[]{:T(512)S(6)} %eq.9), kind=kLoop, calls=%fused_computation.43 | loop fusion | flops 786432 | bytes 2106368 | tf_op jit(solution)/shard_map/jit(_where)/select_n | solution.py:67
  (37 shorter events, 0.8 us)
Async XLA Ops:
  0.0 34.7 %copy-start = (bf16[3,3,128,128]{3,2,1,0:T(8,128)(2,1)S(1)}, bf16[3,3,128,128]{3,2,1,0:T(8,128)(2,1)}, u32[]{:S(2)}) copy-start(bf16[3,3,128,128]{3,2,1,0:T(8,128)(2,1)} %param.10) | copy-start | bytes 884740
  3.0 6.4 %collective-permute-start = (bf16[2,64,1,128]{3,1,2,0:T(8,128)(2,1)S(1)}, bf16[2,64,1,128]{3,1,2,0:T(8,128)(2,1)S(1)}, u32[]{:S(2)}, u32[]{:S(2)}) collective-permute-start(bf16[2,64,1,128]{3,1,2,0:T(8,128)(2,1)S(1)} %get-tuple-element.11), channel_id=1, source_target_pairs={{0,1},{1,2},{2,3},{4,5},{5,6},{6,7},{8,9},{9,10},{10,11},{12,13},{... | collective-permute-start | bytes 98312 | tf_op jit(solution)/shard_map/ppermute | solution.py:14
  7.5 5.2 %collective-permute-start.1 = (bf16[2,64,1,128]{3,1,2,0:T(8,128)(2,1)S(1)}, bf16[2,64,1,128]{3,1,2,0:T(8,128)(2,1)S(1)}, u32[]{:S(2)}, u32[]{:S(2)}) collective-permute-start(bf16[2,64,1,128]{3,1,2,0:T(8,128)(2,1)S(1)} %get-tuple-element.12), channel_id=1, source_target_pairs={{1,0},{2,1},{3,2},{5,4},{6,5},{7,6},{9,8},{10,9},{11,10},{13,12},{... | collective-permute-start | bytes 98312 | tf_op jit(solution)/shard_map/ppermute | solution.py:15
  13.6 1.0 copy-start.2
  13.6 1.0 copy-start.3
  13.6 0.9 copy-start.6
  25.7 4.6 %copy-start.1 = (f32[2]{0:T(128)S(1)}, f32[2]{0:T(128)}, u32[]{:S(2)}) copy-start(f32[2]{0:T(128)} %param.13) | copy-start | bytes 28
  25.9 4.5 %collective-permute-start.2 = (bf16[2,64,1,128]{3,1,2,0:T(8,128)(2,1)S(1)}, bf16[2,64,1,128]{3,1,2,0:T(8,128)(2,1)S(1)}, u32[]{:S(2)}, u32[]{:S(2)}) collective-permute-start(bf16[2,64,1,128]{3,1,2,0:T(8,128)(2,1)S(1)} %get-tuple-element.9), channel_id=1, source_target_pairs={{0,1},{1,2},{2,3},{4,5},{5,6},{6,7},{8,9},{9,10},{10,11},{12,13},{... | collective-permute-start | bytes 98312 | tf_op jit(solution)/shard_map/ppermute | solution.py:14
  27.9 5.2 %collective-permute-start.3 = (bf16[2,64,1,128]{3,1,2,0:T(8,128)(2,1)S(1)}, bf16[2,64,1,128]{3,1,2,0:T(8,128)(2,1)S(1)}, u32[]{:S(2)}, u32[]{:S(2)}) collective-permute-start(bf16[2,64,1,128]{3,1,2,0:T(8,128)(2,1)S(1)} %get-tuple-element.10), channel_id=1, source_target_pairs={{1,0},{2,1},{3,2},{5,4},{6,5},{7,6},{9,8},{10,9},{11,10},{13,12},{... | collective-permute-start | bytes 98312 | tf_op jit(solution)/shard_map/ppermute | solution.py:15
  33.9 0.8 copy-start.4
  33.9 0.8 copy-start.5
  56.4 24.1 %collective-permute-start.4 = (f32[32,64,128]{2,1,0:T(8,128)S(1)}, f32[32,64,128]{2,1,0:T(8,128)S(1)}, u32[]{:S(2)}, u32[]{:S(2)}) collective-permute-start(f32[32,64,128]{2,1,0:T(8,128)S(1)} %bitcast.76), channel_id=1, source_target_pairs={{0,4},{4,0},{8,12},{12,8},{1,5},{5,1},{9,13},{13,9},{2,6},{6,2},{1... | collective-permute-start | bytes 3145736 | tf_op jit(solution)/shard_map/ppermute | solution.py:23
  57.8 22.8 %collective-permute-start.5 = (f32[32,64]{1,0:T(8,128)S(1)}, f32[32,64]{1,0:T(8,128)S(1)}, u32[]{:S(2)}, u32[]{:S(2)}) collective-permute-start(f32[32,64]{1,0:T(8,128)S(1)} %bitcast.82), channel_id=1, source_target_pairs={{0,4},{4,0},{8,12},{12,8},{1,5},{5,1},{9,13},{13,9},{2,6},{6,2},{1... | collective-permute-start | bytes 24584 | tf_op jit(solution)/shard_map/ppermute | solution.py:23
  81.4 26.4 %collective-permute-start.6 = (f32[16,64,128]{2,1,0:T(8,128)S(1)}, f32[16,64,128]{2,1,0:T(8,128)S(1)}, u32[]{:S(2)}, u32[]{:S(2)}) collective-permute-start(f32[16,64,128]{2,1,0:T(8,128)S(1)} %select_bitcast_fusion), channel_id=1, source_target_pairs={{0,8},{4,12},{8,0},{12,4},{1,9},{5,13},{9,1},{13,5},{2,10},{6,14},... | collective-permute-start | bytes 1572872 | tf_op jit(solution)/shard_map/ppermute | solution.py:23
  83.8 24.0 %collective-permute-start.7 = (f32[16,64]{1,0:T(8,128)S(1)}, f32[16,64]{1,0:T(8,128)S(1)}, u32[]{:S(2)}, u32[]{:S(2)}) collective-permute-start(f32[16,64]{1,0:T(8,128)S(1)} %get-tuple-element.19), channel_id=1, source_target_pairs={{0,8},{4,12},{8,0},{12,4},{1,9},{5,13},{9,1},{13,5},{2,10},{6,14},... | collective-permute-start | bytes 12296 | tf_op jit(solution)/shard_map/ppermute | solution.py:23
where the time goes:
time: 110 us; the launch traced here: 109 us
  waiting for transfers between devices  52.5 us (48%)
  matrix products  23 us (21%)
  starting transfers between devices  14.8 us (13%)
  local copies, waits for them, and re-layouts  12.7 us (12%)
  other arithmetic  5.68 us (5%)
    ppermute x4, waiting for transfers between devices, from_partner(): return lax.ppermute(value, axis, pairs)  46.5 us
    conv_general_dilated x2, matrix products, convolve_rows(): lax.conv_general_dilated(block, kernel, (1, 1), ((1, 1), (0, 0)), dimensi...  23 us
    ppermute x2, starting transfers between devices, padded_2(): before = lax.ppermute(last, axis, up)  6.43 us
    ppermute x2, waiting for transfers between devices, padded_2(): after = lax.ppermute(leading, axis, down)  5.99 us
    mul x2, local copies, waits for them, and re-layouts, per_device(): features = jax.nn.gelu(convolve_rows(hidden_pad, conv_two, bias_two))  4.45 us
    ppermute x2, starting transfers between devices, padded_2(): after = lax.ppermute(leading, axis, down)  4.32 us
    ppermute x4, starting transfers between devices, from_partner(): return lax.ppermute(value, axis, pairs)  4.02 us
    unnamed x16, local copies, waits for them, and re-layouts  3.36 us
  transfers between devices with their start and end apart: 8, of which 4 were waited for; matrix products, arithmetic and copies ran while one was open for 0% of the time, Pallas kernels for 0%

commit v1 on v0

v1 whole, which is shorter than its diff:
```python
import functools

import jax
import jax.numpy as jnp
from jax import lax
from jax.experimental import pallas as pl
from jax.experimental.pallas import tpu as pltpu
from jax.sharding import PartitionSpec as P

VM = pl.BlockSpec(memory_space=pltpu.VMEM)
ANY = pl.BlockSpec(memory_space=pl.ANY)
F32 = jnp.float32
BF16 = jnp.bfloat16


def gelu(x):
    c = 0.7978845608028654
    half = 0.5 * x
    return half + half * jnp.tanh(x * (c + (c * 0.044715) * (x * x)))


def pair_weights(w_ref):
    zero = jnp.zeros((w_ref.shape[2], w_ref.shape[3]), w_ref.dtype)
    blocks = []
    for j in range(4):
        for d in range(3):
            first = w_ref[j, d] if j < 3 else zero
            second = w_ref[j - 1, d] if j > 0 else zero
            blocks.append(jnp.concatenate([first, second], axis=1))
    return jnp.concatenate(blocks, axis=0)


def edges_kernel(x_hbm, top_ref, bot_ref, buf, sem):
    rows = x_hbm.shape[2]
    a = pltpu.make_async_copy(x_hbm.at[:, :, pl.ds(0, 8)], buf.at[0], sem.at[0])
    b = pltpu.make_async_copy(x_hbm.at[:, :, pl.ds(rows - 8, 8)], buf.at[1], sem.at[1])
    a.start()
    b.start()
    a.wait()
    top_ref[...] = buf[0, :, :, 0:2]
    b.wait()
    bot_ref[...] = buf[1, :, :, 6:8]


def edges(x):
    planes, cols, rows, ch = x.shape
    shape = jax.ShapeDtypeStruct((planes, cols, 2, ch), x.dtype)
    return pl.pallas_call(
        edges_kernel,
        out_shape=(shape, shape),
        in_specs=[ANY],
        out_specs=(VM, VM),
        scratch_shapes=[
            pltpu.VMEM((2, planes, cols, 8, ch), x.dtype),
            pltpu.SemaphoreType.DMA((2,)),
        ],
        compiler_params=pltpu.CompilerParams(vmem_limit_bytes=8 << 20),
    )(x)


def chunk_kernel(pick, packed, x_ref, above_ref, below_ref, w1_ref, w2_ref, par_ref, *refs):
    if packed:
        out_ref, f_ref, xs, f2_ref, hs, fs = refs
    else:
        out_ref, trans_ref, f_ref, xs, f2_ref, hs, fs = refs
    planes, cols, rows, ch = x_ref.shape
    ext = rows + 16
    nc = fs.shape[1]
    slots = f_ref.shape[0]
    c0 = pick() * nc
    for i in range(planes * (nc + 4)):
        p, c = divmod(i, nc + 4)
        at = c0 - 2 + c
        inside = jnp.logical_and(at >= 0, at < cols)
        at = jnp.clip(at, 0, cols - 1)
        keep = jnp.where(inside, 1.0, 0.0)
        f = f_ref.at[i % slots]
        f[16 : 16 + rows] = x_ref[p, at].astype(F32) * keep
        f[14:16] = above_ref[p, at].astype(F32) * keep
        f[16 + rows : 18 + rows] = below_ref[p, at].astype(F32) * keep
        for d in range(3):
            xs[d, p, c] = f[7 + d : 7 + d + ext].astype(BF16)
    here = lax.axis_index("rows")
    above = jnp.where(here == 0, 0.0, 1.0)
    below = jnp.where(here == lax.axis_size("rows") - 1, 0.0, 1.0)
    bias_one = par_ref[0:1]
    bias_two = par_ref[1:2]
    opacity = par_ref[2:3]
    weights = pair_weights(w1_ref)
    for p in range(planes):
        taps = []
        for j in range(4):
            for d in range(3):
                taps.append(jnp.concatenate([xs[d, p, g + j] for g in range(0, nc + 2, 2)], axis=0))
        y = jnp.dot(jnp.concatenate(taps, axis=1), weights, preferred_element_type=F32)
        for c in range(nc + 2):
            g, o = divmod(c, 2)
            v = gelu(y[g * ext : (g + 1) * ext, o * ch : (o + 1) * ch] + bias_one)
            if c == 0:
                v = v * jnp.where(c0 > 0, 1.0, 0.0)
            if c == nc + 1:
                v = v * jnp.where(c0 + nc < cols, 1.0, 0.0)
            f2 = f2_ref.at[p, c]
            f2[...] = v
            f2[7:8] = f2[7:8] * above
            f2[8 + rows : 9 + rows] = f2[8 + rows : 9 + rows] * below
            for d in range(3):
                hs[d, p, c] = f2[7 + d : 7 + d + rows].astype(BF16)
    lane = lax.broadcasted_iota(jnp.int32, (rows, ch), 1)
    weights = pair_weights(w2_ref)
    logits = [jnp.zeros((rows, ch), F32) for _ in range(planes)]
    taps = []
    for j in range(4):
        for d in range(3):
            taps.append(
                jnp.concatenate(
                    [hs[d, p, g + j] for g in range(0, nc, 2) for p in range(planes)], axis=0
                )
            )
    y = jnp.dot(jnp.concatenate(taps, axis=1), weights, preferred_element_type=F32)
    for c in range(nc):
        g, o = divmod(c, 2)
        for p in range(planes):
            r0 = (g * planes + p) * rows
            f = gelu(y[r0 : r0 + rows, o * ch : (o + 1) * ch] + bias_two)
            total = jnp.sum(f * opacity, axis=1, keepdims=True)
            logits[p] = jnp.where(lane == c, total, logits[p])
            fs[p, c] = f
    parts = []
    trans = None
    for p in range(planes):
        alpha = 1.0 / (1.0 + jnp.exp(-(logits[p] + par_ref[3 + p : 4 + p])))
        if p == 0:
            parts.append(alpha)
            trans = 1.0 - alpha
        else:
            parts.append(trans * alpha)
            trans = trans * (1.0 - alpha)
    for c in range(nc):
        color = sum(parts[p][:, c : c + 1] * fs[p, c] for p in range(planes))
        out_ref[c] = color.astype(out_ref.dtype)
    if packed:
        high = trans.astype(BF16).astype(F32)
        low = pltpu.roll(trans - high, nc, axis=1)
        out_ref[nc] = jnp.where(lane < nc, high, low).astype(out_ref.dtype)
    else:
        trans_ref[...] = trans


def chunk(pick, nc, packed, x, above, below, w1, w2, par):
    planes, cols, rows, ch = x.shape
    ext = rows + 16
    if packed:
        out_shape = jax.ShapeDtypeStruct((nc + 1, rows, ch), BF16)
        out_specs = VM
    else:
        out_shape = (
            jax.ShapeDtypeStruct((nc, rows, ch), F32),
            jax.ShapeDtypeStruct((rows, ch), F32),
        )
        out_specs = (VM, VM)
    return pl.pallas_call(
        functools.partial(chunk_kernel, pick, packed),
        out_shape=out_shape,
        in_specs=[VM] * 6,
        out_specs=out_specs,
        scratch_shapes=[
            pltpu.VMEM((8, rows + 32, ch), F32),
            pltpu.VMEM((3, planes, nc + 4, ext, ch), BF16),
            pltpu.VMEM((planes, nc + 2, ext, ch), F32),
            pltpu.VMEM((3, planes, nc + 2, rows, ch), BF16),
            pltpu.VMEM((planes, nc, rows, ch), F32),
        ],
        compiler_params=pltpu.CompilerParams(vmem_limit_bytes=16 << 20),
    )(x, above, below, w1, w2, par)


def combine_kernel(own_ref, trans_ref, *refs):
    *got_refs, out_ref = refs
    nc, rows, ch = own_ref.shape
    here = lax.axis_index("depth")
    trans = [trans_ref[...]]
    for ref in got_refs:
        t = ref[nc].astype(F32)
        trans.append(t + pltpu.roll(t, ch - nc, axis=1))
    scale = []
    for k in range(len(trans)):
        w = None
        for m in range(len(trans)):
            if m != k:
                front = jnp.bitwise_xor(here, m) < jnp.bitwise_xor(here, k)
                term = jnp.where(front, trans[m], 1.0)
                w = term if w is None else w * term
        scale.append(w)
    for c in range(nc):
        total = scale[0][:, c : c + 1] * own_ref[c]
        for k, ref in enumerate(got_refs):
            total = total + scale[k + 1][:, c : c + 1] * ref[c].astype(F32)
        out_ref[c] = total


def combine(own, trans, got):
    return pl.pallas_call(
        combine_kernel,
        out_shape=jax.ShapeDtypeStruct(own.shape, F32),
        in_specs=[VM] * (2 + len(got)),
        out_specs=VM,
        compiler_params=pltpu.CompilerParams(vmem_limit_bytes=8 << 20),
    )(own, trans, *got)


def exchange(value, axis, mask):
    pairs = [(i, i ^ mask) for i in range(lax.axis_size(axis))]
    return lax.ppermute(value, axis, pairs)


def pick_half(array, remaining, bit_set):
    shaped = array.reshape((remaining // 2, 2, -1) + array.shape[1:])
    first_half = shaped[:, 0].reshape((-1,) + array.shape[1:])
    second_half = shaped[:, 1].reshape((-1,) + array.shape[1:])
    keep = jnp.where(bit_set, second_half, first_half)
    other = jnp.where(bit_set, first_half, second_half)
    return (keep, other)


def butterfly(color, trans):
    position = lax.axis_index("depth")
    slabs = lax.axis_size("depth")
    for level in range(slabs.bit_length() - 1):
        remaining = slabs >> level
        bit_set = jnp.right_shift(position, level) % 2 == 1
        keep_color, send_color = pick_half(color, remaining, bit_set)
        keep_trans, send_trans = pick_half(trans, remaining, bit_set)
        got_color = exchange(send_color, "depth", 2**level)
        got_trans = exchange(send_trans, "depth", 2**level)
        color = jnp.where(
            bit_set,
            got_color + got_trans[..., None] * keep_color,
            keep_color + keep_trans[..., None] * got_color,
        )
        trans = keep_trans * got_trans
    return color


def per_device(volume, conv_one, bias_one, conv_two, bias_two, opacity_weight, opacity_bias):
    planes, cols, rows, ch = volume.shape
    slabs = lax.axis_size("depth")
    size = lax.axis_size("rows")
    par = jnp.concatenate(
        [
            jnp.stack([bias_one, bias_two, opacity_weight]),
            jnp.broadcast_to(opacity_bias[:, None], (planes, ch)),
        ]
    )
    top, bot = edges(volume)
    above = lax.ppermute(bot, "rows", [(i, i + 1) for i in range(size - 1)])
    below = lax.ppermute(top, "rows", [(i + 1, i) for i in range(size - 1)])
    args = (volume, above, below, conv_one, conv_two, par)
    if slabs > 4:
        nc = 16
        done = [
            chunk(functools.partial(jnp.int32, i), nc, False, *args) for i in range(cols // nc)
        ]
        color = jnp.concatenate([c for c, _ in done])
        trans = jnp.concatenate([jnp.transpose(t[:, :nc]) for _, t in done])
        return butterfly(color, trans)
    nc = cols // slabs

    def pick(k):
        return lambda: jnp.bitwise_xor(lax.axis_index("depth"), k)

    got = {}
    for k in [k for k in (2, 3, 1) if k < slabs]:
        got[k] = exchange(chunk(pick(k), nc, True, *args), "depth", k)
    own, trans = chunk(pick(0), nc, False, *args)
    return combine(own, trans, [got[k] for k in sorted(got)])


def solution(mesh):
    in_specs = (P(("grp", "depth"), None, "rows", None), P(), P(), P(), P(), P(), P("depth"))
    out_specs = P(("grp", "depth"), "rows", None)
    return jax.shard_map(
        per_device, mesh=mesh, in_specs=in_specs, out_specs=out_specs, check_vma=False
    )
```

time: 110 us -> 48 us (0.44)
  the two profiles are of different devices: /device:TPU:1 before, /device:TPU:21 now
where the time goes in v1:
time: 48 us; the launch traced here: 47.7 us
  waiting for transfers between devices  19.6 us (41%)
  Pallas kernels  15.8 us (33%)
  starting transfers between devices  8.58 us (18%)
  local copies, waits for them, and re-layouts  3.61 us (8%)
    ppermute x3, waiting for transfers between devices, exchange(): return lax.ppermute(value, axis, pairs)  16.1 us
    pallas_call x4, Pallas kernels, chunk(): pl.pallas_call(functools.partial(chunk_kernel, pick, packed), out_shape=o...  14 us
    ppermute x1, starting transfers between devices, per_device(): above = lax.ppermute(bot, 'rows', [(i, i + 1) for i in range(size - 1)])  3.81 us
    unnamed x16, local copies, waits for them, and re-layouts  3.53 us
    ppermute x1, waiting for transfers between devices, per_device(): below = lax.ppermute(top, 'rows', [(i + 1, i) for i in range(size - 1)])  3.49 us
    ppermute x3, starting transfers between devices, exchange(): return lax.ppermute(value, axis, pairs)  2.85 us
    ppermute x1, starting transfers between devices, per_device(): below = lax.ppermute(top, 'rows', [(i + 1, i) for i in range(size - 1)])  1.92 us
    pallas_call x1, Pallas kernels, combine(): pl.pallas_call(combine_kernel, out_shape=jax.ShapeDtypeStruct(own.shape,...  1.51 us
  transfers between devices with their start and end apart: 5, of which 3 were waited for; matrix products, arithmetic and copies ran while one was open for 0% of the time, Pallas kernels for 22%

profile of v1, /device:TPU:21, one launch (start us, length us, event | category | flops | bytes accessed | tf_op | source)
XLA Modules:
  0.0 47.7 jit_solution(6033946045255123240)
XLA Ops:
  0.0 0.0 copy-start
  0.0 1.6 %copy-done = bf16[2,64,64,128]{3,2,1,0:T(8,128)(2,1)S(1)} copy-done((bf16[2,64,64,128]{3,2,1,0:T(8,128)(2,1)S(1)}, bf16[2,64,64,128]{3,2,1,0:T(8,128)(2,1)}, u32[]{:S(2)}) %copy-start) | copy-done | bytes 2097176
  1.6 0.0 copy-start.7
  1.6 0.0 copy-start.4
  1.6 0.0 copy-start.5
  1.6 0.0 copy-start.6
  1.6 0.0 copy-start.1
  1.6 0.3 shard_map.73
  1.9 3.8 %collective-permute-start = (bf16[2,64,2,128]{3,2,1,0:T(2,128)(2,1)S(1)}, bf16[2,64,2,128]{3,2,1,0:T(2,128)(2,1)S(1)}, u32[]{:S(2)}, u32[]{:S(2)}) collective-permute-start(bf16[2,64,2,128]{3,2,1,0:T(2,128)(2,1)S(1)} %get-tuple-element.9), channel_id=1, source_target_pairs={{0,1},{1,2},{2,3},{4,5},{5,6},{6,7},{8,9},{9,10},{10,11},{12,13},{... | collective-permute-start | bytes 196616 | tf_op jit(solution)/shard_map/ppermute | solution.py:256
  5.7 1.9 %collective-permute-start.1 = (bf16[2,64,2,128]{3,2,1,0:T(2,128)(2,1)S(1)}, bf16[2,64,2,128]{3,2,1,0:T(2,128)(2,1)S(1)}, u32[]{:S(2)}, u32[]{:S(2)}) collective-permute-start(bf16[2,64,2,128]{3,2,1,0:T(2,128)(2,1)S(1)} %get-tuple-element.10), channel_id=1, source_target_pairs={{1,0},{2,1},{3,2},{5,4},{6,5},{7,6},{9,8},{10,9},{11,10},{13,12},{... | collective-permute-start | bytes 196616 | tf_op jit(solution)/shard_map/ppermute | solution.py:257
  7.6 0.0 copy-done.7
  7.7 0.1 pad.3.clone
  7.7 0.0 copy-done.4
  7.7 0.0 copy-done.5
  7.7 0.0 copy-done.6
  7.7 0.1 maximum_maximum_fusion.par_ref
  7.8 0.0 collective-permute-done.above_ref
  7.8 3.5 %collective-permute-done.1.below_ref = bf16[2,64,2,128]{3,2,1,0:T(2,128)(2,1)S(1)} collective-permute-done((bf16[2,64,2,128]{3,2,1,0:T(2,128)(2,1)S(1)}, bf16[2,64,2,128]{3,2,1,0:T(2,128)(2,1)S(1)}, u32[]{:S(2)}, u32[]{:S(2)}) %collective-permute-start.1) | collective-permute-done | bytes 65568 | tf_op jit(solution)/shard_map/ppermute | solution.py:257
  11.3 0.0 copy-done.1
  11.3 1.0 %copy-done.2 = bf16[3,3,128,128]{3,2,1,0:T(8,128)(2,1)S(1)} copy-done((bf16[3,3,128,128]{3,2,1,0:T(8,128)(2,1)S(1)}, bf16[3,3,128,128]{3,2,1,0:T(8,128)(2,1)}, u32[]{:S(2)}) %copy-start.2) | copy-done | bytes 294936
  12.3 1.0 %copy-done.3 = bf16[3,3,128,128]{3,2,1,0:T(8,128)(2,1)S(1)} copy-done((bf16[3,3,128,128]{3,2,1,0:T(8,128)(2,1)S(1)}, bf16[3,3,128,128]{3,2,1,0:T(8,128)(2,1)}, u32[]{:S(2)}) %copy-start.3) | copy-done | bytes 294936
  13.2 3.5 %shard_map.75 = bf16[17,64,128]{2,1,0:T(8,128)(2,1)S(1)} custom-call(bf16[2,64,64,128]{3,2,1,0:T(8,128)(2,1)S(1)} %copy-done.1, bf16[2,64,2,128]{3,2,1,0:T(2,128)(2,1)S(1)} %collective-permute-done.above_ref, bf16[2,64,2,128]{3,2,1,0:T(2,128)(2,1)S(1)} %collective-permute-done.1.below_ref, bf16[3,3,128,128]{3,2,1,0:T(8,128)(2,1)S(1)} %copy-done.2, ...), custom_call_target="tpu_custom_call" | custom-call | tf_op jit(solution)/shard_map/pallas_call | solution.py:162
  16.7 1.4 %collective-permute-start.2 = (bf16[17,64,128]{2,1,0:T(8,128)(2,1)S(1)}, bf16[17,64,128]{2,1,0:T(8,128)(2,1)S(1)}, u32[]{:S(2)}, u32[]{:S(2)}) collective-permute-start(bf16[17,64,128]{2,1,0:T(8,128)(2,1)S(1)} %shard_map.75), channel_id=1, source_target_pairs={{0,4},{4,0},{8,12},{12,8},{1,5},{5,1},{9,13},{13,9},{2,6},{6,2},{1... | collective-permute-start | bytes 835592 | tf_op jit(solution)/shard_map/ppermute | solution.py:214
  18.1 3.5 %shard_map.76 = bf16[17,64,128]{2,1,0:T(8,128)(2,1)S(1)} custom-call(bf16[2,64,64,128]{3,2,1,0:T(8,128)(2,1)S(1)} %copy-done.1, bf16[2,64,2,128]{3,2,1,0:T(2,128)(2,1)S(1)} %collective-permute-done.above_ref, bf16[2,64,2,128]{3,2,1,0:T(2,128)(2,1)S(1)} %collective-permute-done.1.below_ref, bf16[3,3,128,128]{3,2,1,0:T(8,128)(2,1)S(1)} %copy-done.2, ...), custom_call_target="tpu_custom_call" | custom-call | tf_op jit(solution)/shard_map/pallas_call | solution.py:162
  21.6 0.1 collective-permute-start.3
  21.7 3.5 %shard_map.77 = bf16[17,64,128]{2,1,0:T(8,128)(2,1)S(1)} custom-call(bf16[2,64,64,128]{3,2,1,0:T(8,128)(2,1)S(1)} %copy-done.1, bf16[2,64,2,128]{3,2,1,0:T(2,128)(2,1)S(1)} %collective-permute-done.above_ref, bf16[2,64,2,128]{3,2,1,0:T(2,128)(2,1)S(1)} %collective-permute-done.1.below_ref, bf16[3,3,128,128]{3,2,1,0:T(8,128)(2,1)S(1)} %copy-done.2, ...), custom_call_target="tpu_custom_call" | custom-call | tf_op jit(solution)/shard_map/pallas_call | solution.py:162
  25.2 1.4 %collective-permute-start.4 = (bf16[17,64,128]{2,1,0:T(8,128)(2,1)S(1)}, bf16[17,64,128]{2,1,0:T(8,128)(2,1)S(1)}, u32[]{:S(2)}, u32[]{:S(2)}) collective-permute-start(bf16[17,64,128]{2,1,0:T(8,128)(2,1)S(1)} %shard_map.77), channel_id=1, source_target_pairs={{0,12},{4,8},{8,4},{12,0},{1,13},{5,9},{9,5},{13,1},{2,14},{6,10},... | collective-permute-start | bytes 835592 | tf_op jit(solution)/shard_map/ppermute | solution.py:214
  26.6 3.5 %shard_map.74 = (f32[16,64,128]{2,1,0:T(8,128)S(1)}, f32[64,128]{1,0:T(8,128)S(1)}) custom-call(bf16[2,64,64,128]{3,2,1,0:T(8,128)(2,1)S(1)} %copy-done.1, bf16[2,64,2,128]{3,2,1,0:T(2,128)(2,1)S(1)} %collective-permute-done.above_ref, bf16[2,64,2,128]{3,2,1,0:T(2,128)(2,1)S(1)} %collective-permute-done.1.below_ref, bf16[3,3,128,128]{3,2,1,0:T(8,128)(2,1)S(1)} %copy-done.2, ...), custom_call_target="tpu_custom_call" | custom-call | tf_op jit(solution)/shard_map/pallas_call | solution.py:162
  30.1 0.0 collective-permute-done.2.refs_0_
  30.1 9.2 %collective-permute-done.3.refs_1_ = bf16[17,64,128]{2,1,0:T(8,128)(2,1)S(1)} collective-permute-done((bf16[17,64,128]{2,1,0:T(8,128)(2,1)S(1)}, bf16[17,64,128]{2,1,0:T(8,128)(2,1)S(1)}, u32[]{:S(2)}, u32[]{:S(2)}) %collective-permute-start.3) | collective-permute-done | bytes 278560 | tf_op jit(solution)/shard_map/ppermute | solution.py:214
  39.3 6.9 %collective-permute-done.4.refs_2_ = bf16[17,64,128]{2,1,0:T(8,128)(2,1)S(1)} collective-permute-done((bf16[17,64,128]{2,1,0:T(8,128)(2,1)S(1)}, bf16[17,64,128]{2,1,0:T(8,128)(2,1)S(1)}, u32[]{:S(2)}, u32[]{:S(2)}) %collective-permute-start.4) | collective-permute-done | bytes 278560 | tf_op jit(solution)/shard_map/ppermute | solution.py:214
  46.2 1.5 %shard_map.78 = f32[16,64,128]{2,1,0:T(8,128)} custom-call(f32[16,64,128]{2,1,0:T(8,128)S(1)} %get-tuple-element.11.own_ref, f32[64,128]{1,0:T(8,128)S(1)} %get-tuple-element.12.trans_ref, bf16[17,64,128]{2,1,0:T(8,128)(2,1)S(1)} %collective-permute-done.2.refs_0_, bf16[17,64,128]{2,1,0:T(8,128)(2,1)S(1)} %collective-permute-done.3.refs_1_, ...), custom_call_target="tpu_custom_call" | custom-call | tf_op jit(solution)/shard_map/pallas_call | solution.py:203
  (2 shorter events, 0.0 us)
Async XLA Ops:
  0.0 1.6 %copy-start = (bf16[2,64,64,128]{3,2,1,0:T(8,128)(2,1)S(1)}, bf16[2,64,64,128]{3,2,1,0:T(8,128)(2,1)}, u32[]{:S(2)}) copy-start(bf16[2,64,64,128]{3,2,1,0:T(8,128)(2,1)} %x_ref.7) | copy-start | bytes 6291460
  1.6 6.1 %copy-start.7 = (f32[2]{0:T(128)S(1)}, f32[2]{0:T(128)}, u32[]{:S(2)}) copy-start(f32[2]{0:T(128)} %param.13) | copy-start | bytes 28
  1.6 6.1 %copy-start.4 = (f32[128]{0:T(128)S(1)}, f32[128]{0:T(128)}, u32[]{:S(2)}) copy-start(f32[128]{0:T(128)} %param.12) | copy-start | bytes 1540
  1.6 6.1 %copy-start.5 = (f32[128]{0:T(128)S(1)}, f32[128]{0:T(128)}, u32[]{:S(2)}) copy-start(f32[128]{0:T(128)} %param.11) | copy-start | bytes 1540
  1.6 6.1 %copy-start.6 = (f32[128]{0:T(128)S(1)}, f32[128]{0:T(128)}, u32[]{:S(2)}) copy-start(f32[128]{0:T(128)} %param.9) | copy-start | bytes 1540
  1.6 9.7 %copy-start.1 = (bf16[2,64,64,128]{3,2,1,0:T(8,128)(2,1)S(1)}, bf16[2,64,64,128]{3,2,1,0:T(8,128)(2,1)}, u32[]{:S(2)}) copy-start(bf16[2,64,64,128]{3,2,1,0:T(8,128)(2,1)} %x_ref.7) | copy-start | bytes 6291460
  1.9 5.9 %collective-permute-start = (bf16[2,64,2,128]{3,2,1,0:T(2,128)(2,1)S(1)}, bf16[2,64,2,128]{3,2,1,0:T(2,128)(2,1)S(1)}, u32[]{:S(2)}, u32[]{:S(2)}) collective-permute-start(bf16[2,64,2,128]{3,2,1,0:T(2,128)(2,1)S(1)} %get-tuple-element.9), channel_id=1, source_target_pairs={{0,1},{1,2},{2,3},{4,5},{5,6},{6,7},{8,9},{9,10},{10,11},{12,13},{... | collective-permute-start | bytes 196616 | tf_op jit(solution)/shard_map/ppermute | solution.py:256
  5.7 5.6 %collective-permute-start.1 = (bf16[2,64,2,128]{3,2,1,0:T(2,128)(2,1)S(1)}, bf16[2,64,2,128]{3,2,1,0:T(2,128)(2,1)S(1)}, u32[]{:S(2)}, u32[]{:S(2)}) collective-permute-start(bf16[2,64,2,128]{3,2,1,0:T(2,128)(2,1)S(1)} %get-tuple-element.10), channel_id=1, source_target_pairs={{1,0},{2,1},{3,2},{5,4},{6,5},{7,6},{9,8},{10,9},{11,10},{13,12},{... | collective-permute-start | bytes 196616 | tf_op jit(solution)/shard_map/ppermute | solution.py:257
  11.3 1.0 %copy-start.2 = (bf16[3,3,128,128]{3,2,1,0:T(8,128)(2,1)S(1)}, bf16[3,3,128,128]{3,2,1,0:T(8,128)(2,1)}, u32[]{:S(2)}) copy-start(bf16[3,3,128,128]{3,2,1,0:T(8,128)(2,1)} %w1_ref.7) | copy-start | bytes 884740
  12.3 1.0 %copy-start.3 = (bf16[3,3,128,128]{3,2,1,0:T(8,128)(2,1)S(1)}, bf16[3,3,128,128]{3,2,1,0:T(8,128)(2,1)}, u32[]{:S(2)}) copy-start(bf16[3,3,128,128]{3,2,1,0:T(8,128)(2,1)} %w2_ref.7) | copy-start | bytes 884740
  16.7 13.3 %collective-permute-start.2 = (bf16[17,64,128]{2,1,0:T(8,128)(2,1)S(1)}, bf16[17,64,128]{2,1,0:T(8,128)(2,1)S(1)}, u32[]{:S(2)}, u32[]{:S(2)}) collective-permute-start(bf16[17,64,128]{2,1,0:T(8,128)(2,1)S(1)} %shard_map.75), channel_id=1, source_target_pairs={{0,4},{4,0},{8,12},{12,8},{1,5},{5,1},{9,13},{13,9},{2,6},{6,2},{1... | collective-permute-start | bytes 835592 | tf_op jit(solution)/shard_map/ppermute | solution.py:214
  21.6 17.7 %collective-permute-start.3 = (bf16[17,64,128]{2,1,0:T(8,128)(2,1)S(1)}, bf16[17,64,128]{2,1,0:T(8,128)(2,1)S(1)}, u32[]{:S(2)}, u32[]{:S(2)}) collective-permute-start(bf16[17,64,128]{2,1,0:T(8,128)(2,1)S(1)} %shard_map.76), channel_id=1, source_target_pairs={{0,8},{4,12},{8,0},{12,4},{1,9},{5,13},{9,1},{13,5},{2,10},{6,14},... | collective-permute-start | bytes 835592 | tf_op jit(solution)/shard_map/ppermute | solution.py:214
  25.2 21.0 %collective-permute-start.4 = (bf16[17,64,128]{2,1,0:T(8,128)(2,1)S(1)}, bf16[17,64,128]{2,1,0:T(8,128)(2,1)S(1)}, u32[]{:S(2)}, u32[]{:S(2)}) collective-permute-start(bf16[17,64,128]{2,1,0:T(8,128)(2,1)S(1)} %shard_map.77), channel_id=1, source_target_pairs={{0,12},{4,8},{8,4},{12,0},{1,13},{5,9},{9,5},{13,1},{2,14},{6,10},... | collective-permute-start | bytes 835592 | tf_op jit(solution)/shard_map/ppermute | solution.py:214

commit v2 on v1

--- a/solution.py
+++ b/solution.py
@@ -8,7 +8,7 @@
 from jax.sharding import PartitionSpec as P
 
 VM = pl.BlockSpec(memory_space=pltpu.VMEM)
-ANY = pl.BlockSpec(memory_space=pl.ANY)
+HBM = pl.BlockSpec(memory_space=pltpu.HBM)
 F32 = jnp.float32
 BF16 = jnp.bfloat16
 
@@ -48,7 +48,7 @@
     return pl.pallas_call(
         edges_kernel,
         out_shape=(shape, shape),
-        in_specs=[ANY],
+        in_specs=[HBM],
         out_specs=(VM, VM),
         scratch_shapes=[
             pltpu.VMEM((2, planes, cols, 8, ch), x.dtype),
@@ -58,14 +58,74 @@
     )(x)
 
 
-def chunk_kernel(pick, packed, x_ref, above_ref, below_ref, w1_ref, w2_ref, par_ref, *refs):
-    if packed:
-        out_ref, f_ref, xs, f2_ref, hs, fs = refs
-    else:
-        out_ref, trans_ref, f_ref, xs, f2_ref, hs, fs = refs
+def load_shifted(part, x_ref, p, at, keep, f, xs, c, halo):
+    rows = x_ref.shape[2]
+    if part == "strips":
+        above_ref, below_ref = halo
+        f[8:24] = x_ref[p, at, 0:16].astype(F32) * keep
+        f[6:8] = above_ref[p, at].astype(F32) * keep
+        f[40:56] = x_ref[p, at, rows - 16 : rows].astype(F32) * keep
+        f[56:58] = below_ref[p, at].astype(F32) * keep
+        for d in range(3):
+            xs[d, p, c, 0:16] = f[3 + d : 19 + d].astype(BF16)
+            xs[d, p, c, 16:32] = f[43 + d : 59 + d].astype(BF16)
+        return
+    lead = 8 if part == "whole" else 0
+    f[16 : 16 + rows] = x_ref[p, at].astype(F32) * keep
+    if part == "whole":
+        above_ref, below_ref = halo
+        f[14:16] = above_ref[p, at].astype(F32) * keep
+        f[16 + rows : 18 + rows] = below_ref[p, at].astype(F32) * keep
+    for d in range(3):
+        first = 15 - lead + d
+        xs[d, p, c] = f[first : first + xs.shape[3]].astype(BF16)
+
+
+def store_shifted(part, f2, hs, p, c, above, below):
+    if part == "strips":
+        f2[3:4] = f2[3:4] * above
+        f2[28:29] = f2[28:29] * below
+        for d in range(3):
+            both = jnp.concatenate([f2[3 + d : 11 + d], f2[19 + d : 27 + d]], axis=0)
+            hs[d, p, c] = both.astype(BF16)
+        return
+    nr = hs.shape[3]
+    if part == "whole":
+        f2[7:8] = f2[7:8] * above
+        f2[8 + nr : 9 + nr] = f2[8 + nr : 9 + nr] * below
+    for d in range(3):
+        hs[d, p, c] = f2[7 + d : 7 + d + nr].astype(BF16)
+
+
+def chunk_kernel(pick, part, packed, first, *refs):
+    refs = list(refs)
+    x_ref = refs.pop(0)
+    halo = () if part == "inner" else (refs.pop(0), refs.pop(0))
+    w1_ref, w2_ref, par_ref = refs[:3]
+    refs = refs[3:]
+    out_ref = refs.pop(0)
+    trans_ref = None if packed else refs.pop(0)
+    if first:
+        x_hbm, w1_hbm, w2_hbm = x_ref, w1_ref, w2_ref
+        x_ref, w1_ref, w2_ref = refs[:3]
+        sem = refs.pop()
+        copies = [
+            pltpu.make_async_copy(x_hbm, x_ref, sem.at[0]),
+            pltpu.make_async_copy(w1_hbm, w1_ref, sem.at[1]),
+            pltpu.make_async_copy(w2_hbm, w2_ref, sem.at[2]),
+        ]
+        top_ref, bot_ref = refs[3:5]
+        refs = refs[5:]
+        for copy in copies:
+            copy.start()
+        for copy in copies:
+            copy.wait()
+        top_ref[...] = x_ref[:, :, 0:2]
+        bot_ref[...] = x_ref[:, :, x_ref.shape[2] - 2 :]
+    f_ref, xs, f2_ref, hs, fs = refs
     planes, cols, rows, ch = x_ref.shape
-    ext = rows + 16
-    nc = fs.shape[1]
+    nc, nr = fs.shape[1:3]
+    ext = xs.shape[3]
     slots = f_ref.shape[0]
     c0 = pick() * nc
     for i in range(planes * (nc + 4)):
@@ -74,12 +134,7 @@
         inside = jnp.logical_and(at >= 0, at < cols)
         at = jnp.clip(at, 0, cols - 1)
         keep = jnp.where(inside, 1.0, 0.0)
-        f = f_ref.at[i % slots]
-        f[16 : 16 + rows] = x_ref[p, at].astype(F32) * keep
-        f[14:16] = above_ref[p, at].astype(F32) * keep
-        f[16 + rows : 18 + rows] = below_ref[p, at].astype(F32) * keep
-        for d in range(3):
-            xs[d, p, c] = f[7 + d : 7 + d + ext].astype(BF16)
+        load_shifted(part, x_ref, p, at, keep, f_ref.at[i % slots], xs, c, halo)
     here = lax.axis_index("rows")
     above = jnp.where(here == 0, 0.0, 1.0)
     below = jnp.where(here == lax.axis_size("rows") - 1, 0.0, 1.0)
@@ -102,13 +157,10 @@
                 v = v * jnp.where(c0 + nc < cols, 1.0, 0.0)
             f2 = f2_ref.at[p, c]
             f2[...] = v
-            f2[7:8] = f2[7:8] * above
-            f2[8 + rows : 9 + rows] = f2[8 + rows : 9 + rows] * below
-            for d in range(3):
-                hs[d, p, c] = f2[7 + d : 7 + d + rows].astype(BF16)
-    lane = lax.broadcasted_iota(jnp.int32, (rows, ch), 1)
+            store_shifted(part, f2, hs, p, c, above, below)
+    lane = lax.broadcasted_iota(jnp.int32, (nr, ch), 1)
     weights = pair_weights(w2_ref)
-    logits = [jnp.zeros((rows, ch), F32) for _ in range(planes)]
+    logits = [jnp.zeros((nr, ch), F32) for _ in range(planes)]
     taps = []
     for j in range(4):
         for d in range(3):
@@ -121,8 +173,8 @@
     for c in range(nc):
         g, o = divmod(c, 2)
         for p in range(planes):
-            r0 = (g * planes + p) * rows
-            f = gelu(y[r0 : r0 + rows, o * ch : (o + 1) * ch] + bias_two)
+            r0 = (g * planes + p) * nr
+            f = gelu(y[r0 : r0 + nr, o * ch : (o + 1) * ch] + bias_two)
             total = jnp.sum(f * opacity, axis=1, keepdims=True)
             logits[p] = jnp.where(lane == c, total, logits[p])
             fs[p, c] = f
@@ -147,66 +199,94 @@
         trans_ref[...] = trans
 
 
-def chunk(pick, nc, packed, x, above, below, w1, w2, par):
+def chunk(pick, nc, part, packed, first, x, halo, w1, w2, par):
     planes, cols, rows, ch = x.shape
-    ext = rows + 16
+    ext, nr = {"whole": (rows + 16, rows), "inner": (rows, rows - 16), "strips": (32, 16)}[part]
     if packed:
-        out_shape = jax.ShapeDtypeStruct((nc + 1, rows, ch), BF16)
-        out_specs = VM
+        out_shape = [jax.ShapeDtypeStruct((nc + 1, nr, ch), BF16)]
     else:
-        out_shape = (
-            jax.ShapeDtypeStruct((nc, rows, ch), F32),
-            jax.ShapeDtypeStruct((rows, ch), F32),
-        )
-        out_specs = (VM, VM)
+        out_shape = [
+            jax.ShapeDtypeStruct((nc, nr, ch), F32),
+            jax.ShapeDtypeStruct((nr, ch), F32),
+        ]
+    scratch = [
+        pltpu.VMEM((8, rows + 32, ch), F32),
+        pltpu.VMEM((3, planes, nc + 4, ext, ch), BF16),
+        pltpu.VMEM((planes, nc + 2, ext, ch), F32),
+        pltpu.VMEM((3, planes, nc + 2, nr, ch), BF16),
+        pltpu.VMEM((planes, nc, nr, ch), F32),
+    ]
+    if part == "inner":
+        halo = ()
+    big = HBM if first else VM
+    if first:
+        edge = jax.ShapeDtypeStruct((planes, cols, 2, ch), x.dtype)
+        out_shape += [jax.ShapeDtypeStruct(a.shape, a.dtype) for a in (x, w1, w2)] + [edge] * 2
+        x, w1, w2 = (pltpu.with_memory_space_constraint(a, pltpu.HBM) for a in (x, w1, w2))
+        scratch.append(pltpu.SemaphoreType.DMA((3,)))
     return pl.pallas_call(
-        functools.partial(chunk_kernel, pick, packed),
+        functools.partial(chunk_kernel, pick, part, packed, first),
         out_shape=out_shape,
-        in_specs=[VM] * 6,
-        out_specs=out_specs,
-        scratch_shapes=[
-            pltpu.VMEM((8, rows + 32, ch), F32),
-            pltpu.VMEM((3, planes, nc + 4, ext, ch), BF16),
-            pltpu.VMEM((planes, nc + 2, ext, ch), F32),
-            pltpu.VMEM((3, planes, nc + 2, rows, ch), BF16),
-            pltpu.VMEM((planes, nc, rows, ch), F32),
-        ],
+        in_specs=[big] + [VM] * len(halo) + [big, big, VM],
+        out_specs=[VM] * len(out_shape),
+        scratch_shapes=scratch,
         compiler_params=pltpu.CompilerParams(vmem_limit_bytes=16 << 20),
-    )(x, above, below, w1, w2, par)
-
-
-def combine_kernel(own_ref, trans_ref, *refs):
-    *got_refs, out_ref = refs
+        cost_estimate=pl.CostEstimate(flops=5 * 10**9, transcendentals=0, bytes_accessed=10**6),
+    )(x, *halo, w1, w2, par)
+
+
+def combine_kernel(splits, own_ref, trans_ref, *refs):
+    refs = list(refs)
+    out_ref = refs.pop()
     nc, rows, ch = own_ref.shape
+    slabs = lax.axis_size("depth")
     here = lax.axis_index("depth")
-    trans = [trans_ref[...]]
-    for ref in got_refs:
-        t = ref[nc].astype(F32)
-        trans.append(t + pltpu.roll(t, ch - nc, axis=1))
-    scale = []
-    for k in range(len(trans)):
-        w = None
-        for m in range(len(trans)):
-            if m != k:
-                front = jnp.bitwise_xor(here, m) < jnp.bitwise_xor(here, k)
-                term = jnp.where(front, trans[m], 1.0)
-                w = term if w is None else w * term
-        scale.append(w)
-    for c in range(nc):
-        total = scale[0][:, c : c + 1] * own_ref[c]
-        for k, ref in enumerate(got_refs):
-            total = total + scale[k + 1][:, c : c + 1] * ref[c].astype(F32)
-        out_ref[c] = total
+    order = [here] + [lax.rem(here + slabs - s, slabs) for s in range(1, slabs)]
+    groups = []
+    for split in splits:
+        groups.append([refs.pop(0) for _ in range(2 if split else 1)])
+    for r0, nr in ((0, 8), (8, rows - 16), (rows - 8, 8)):
+        views = []
+        for group in groups:
+            if len(group) == 1:
+                views.append((group[0], r0))
+            elif nr == 8:
+                views.append((group[1], 0 if r0 == 0 else 8))
+            else:
+                views.append((group[0], 0))
+        trans = [trans_ref[r0 : r0 + nr]]
+        for ref, v0 in views:
+            t = ref[nc, v0 : v0 + nr].astype(F32)
+            trans.append(t + pltpu.roll(t, ch - nc, axis=1))
+        scale = []
+        for k in range(slabs):
+            w = None
+            for m in range(slabs):
+                if m != k:
+                    term = jnp.where(order[m] < order[k], trans[m], 1.0)
+                    w = term if w is None else w * term
+            scale.append(w)
+        for c in range(nc):
+            total = scale[0][:, c : c + 1] * own_ref[c, r0 : r0 + nr]
+            for k, (ref, v0) in enumerate(views):
+                total = total + scale[k + 1][:, c : c + 1] * ref[c, v0 : v0 + nr].astype(F32)
+            out_ref[c, r0 : r0 + nr] = total
 
 
 def combine(own, trans, got):
+    flat = [a for group in got for a in group]
     return pl.pallas_call(
-        combine_kernel,
+        functools.partial(combine_kernel, [len(group) == 2 for group in got]),
         out_shape=jax.ShapeDtypeStruct(own.shape, F32),
-        in_specs=[VM] * (2 + len(got)),
+        in_specs=[VM] * (2 + len(flat)),
         out_specs=VM,
         compiler_params=pltpu.CompilerParams(vmem_limit_bytes=8 << 20),
-    )(own, trans, *got)
+    )(own, trans, *flat)
+
+
+def send_on(value, step):
+    slabs = lax.axis_size("depth")
+    return lax.ppermute(value, "depth", [(i, (i + step) % slabs) for i in range(slabs)])
 
 
 def exchange(value, axis, mask):
@@ -252,28 +332,43 @@
             jnp.broadcast_to(opacity_bias[:, None], (planes, ch)),
         ]
     )
-    top, bot = edges(volume)
-    above = lax.ppermute(bot, "rows", [(i, i + 1) for i in range(size - 1)])
-    below = lax.ppermute(top, "rows", [(i + 1, i) for i in range(size - 1)])
-    args = (volume, above, below, conv_one, conv_two, par)
-    if slabs > 4:
+    up = [(i, i + 1) for i in range(size - 1)]
+    down = [(i + 1, i) for i in range(size - 1)]
+    if slabs != 4:
+        top, bot = edges(volume)
+        halo = (lax.ppermute(bot, "rows", up), lax.ppermute(top, "rows", down))
         nc = 16
-        done = [
-            chunk(functools.partial(jnp.int32, i), nc, False, *args) for i in range(cols // nc)
-        ]
+        args = (nc, "whole", False, False, volume, halo, conv_one, conv_two, par)
+        done = [chunk(functools.partial(jnp.int32, i), *args) for i in range(cols // nc)]
         color = jnp.concatenate([c for c, _ in done])
         trans = jnp.concatenate([jnp.transpose(t[:, :nc]) for _, t in done])
         return butterfly(color, trans)
     nc = cols // slabs
 
-    def pick(k):
-        return lambda: jnp.bitwise_xor(lax.axis_index("depth"), k)
-
-    got = {}
-    for k in [k for k in (2, 3, 1) if k < slabs]:
-        got[k] = exchange(chunk(pick(k), nc, True, *args), "depth", k)
-    own, trans = chunk(pick(0), nc, False, *args)
-    return combine(own, trans, [got[k] for k in sorted(got)])
+    def to(step):
+        return lambda: lax.rem(lax.axis_index("depth") + step, slabs)
+
+    one, x, w1, w2, top, bot = chunk(
+        to(1), nc, "inner", True, True, volume, (), conv_one, conv_two, par
+    )
+    got_one = send_on(one, 1)
+    above = lax.ppermute(bot, "rows", up)
+    below = lax.ppermute(top, "rows", down)
+    (two,) = chunk(to(2), nc, "inner", True, False, x, (), w1, w2, par)
+    got_two = send_on(two, 2)
+    x, above, below, two, got_one = lax.optimization_barrier((x, above, below, two, got_one))
+    halo = (above, below)
+    (one_strips,) = chunk(to(1), nc, "strips", True, False, x, halo, w1, w2, par)
+    got_one_strips = send_on(one_strips, 1)
+    x, one_strips = lax.optimization_barrier((x, one_strips))
+    (two_strips,) = chunk(to(2), nc, "strips", True, False, x, halo, w1, w2, par)
+    got_two_strips = send_on(two_strips, 2)
+    x, two_strips = lax.optimization_barrier((x, two_strips))
+    (three,) = chunk(to(3), nc, "whole", True, False, x, halo, w1, w2, par)
+    got_three = send_on(three, 3)
+    x, three = lax.optimization_barrier((x, three))
+    own, trans = chunk(to(0), nc, "whole", False, False, x, halo, w1, w2, par)
+    return combine(own, trans, [(got_one, got_one_strips), (got_two, got_two_strips), (got_three,)])
 
 
 def solution(mesh):

time: 48 us -> 41.8 us (0.87)
  the two profiles are of different devices: /device:TPU:21 before, /device:TPU:1 now
where the time goes in v2:
time: 41.8 us; the launch traced here: 41.2 us
  Pallas kernels  19.6 us (47%)
  starting transfers between devices  14.9 us (36%)
  waiting for transfers between devices  5.11 us (12%)
  other arithmetic  0.76 us (2%)
  local copies, waits for them, and re-layouts  0.73 us (2%)
    pallas_call x6, Pallas kernels, chunk(): pl.pallas_call(functools.partial(chunk_kernel, pick, part, packed, first)...  17.6 us
    ppermute x5, starting transfers between devices, send_on(): lax.ppermute(value, 'depth', [(i, (i + step) % slabs) for i in range(slab...  8.49 us
    ppermute x5, waiting for transfers between devices, send_on(): lax.ppermute(value, 'depth', [(i, (i + step) % slabs) for i in range(slab...  5.1 us
    ppermute x1, starting transfers between devices, per_device(): above = lax.ppermute(bot, 'rows', up)  4.51 us
    pallas_call x1, Pallas kernels, combine(): pl.pallas_call(functools.partial(combine_kernel, [len(group) == 2 for gro...  2.07 us
    ppermute x1, starting transfers between devices, per_device(): below = lax.ppermute(top, 'rows', down)  1.92 us
  transfers between devices with their start and end apart: 7, of which 2 were waited for; matrix products, arithmetic and copies ran while one was open for 0% of the time, Pallas kernels for 32%

profile of v2, /device:TPU:1, one launch (start us, length us, event | category | flops | bytes accessed | tf_op | source)
XLA Modules:
  0.0 41.2 jit_solution(12158056350488353139)
XLA Ops:
  0.0 0.7 %pad.3.clone = f32[5]{0:T(128)S(1)} pad(f32[2]{0:T(128)} %param.13, f32[]{:T(128)} %constant.2), padding=3_0 | pad | bytes 32 | tf_op jit(solution)/shard_map/concatenate | solution.py:329
  0.7 0.8 %maximum_maximum_fusion.refs_3_.refs_5_ = f32[5,128]{1,0:T(8,128)S(1)} fusion(f32[1,128]{1,0:T(1,128)} %bitcast.3, f32[1,128]{1,0:T(1,128)} %bitcast.4, f32[1,128]{1,0:T(1,128)} %bitcast.5, f32[5]{0:T(128)S(1)} %pad.3.clone), kind=kLoop, calls=%fused_computation | loop fusion | flops 1920 | bytes 4116 | tf_op jit(solution)/shard_map/concatenate | solution.py:329
  1.5 4.5 %shard_map.73 = (bf16[17,48,128]{2,1,0:T(8,128)(2,1)S(1)}, bf16[2,64,64,128]{3,2,1,0:T(8,128)(2,1)S(1)}, bf16[3,3,128,128]{3,2,1,0:T(8,128)(2,1)S(1)}, bf16[3,3,...) custom-call(bf16[2,64,64,128]{3,2,1,0:T(8,128)(2,1)} %refs_0_.1, ...), custom_call_target="tpu_custom_call" | custom-call | flops 5000000000 | bytes 1000000 | tf_op jit(solution)/shard_map/pallas_call | solution.py:227
  6.0 4.5 %collective-permute-start = (bf16[2,64,2,128]{3,2,1,0:T(2,128)(2,1)S(1)}, bf16[2,64,2,128]{3,2,1,0:T(2,128)(2,1)S(1)}, u32[]{:S(2)}, u32[]{:S(2)}) collective-permute-start(bf16[2,64,2,128]{3,2,1,0:T(2,128)(2,1)S(1)} %get-tuple-element.21), channel_id=1, source_target_pairs={{0,1},{1,2},{2,3},{4,5},{5,6},{6,7},{8,9},{9,10},{10,11},{12,13},{... | collective-permute-start | bytes 196616 | tf_op jit(solution)/shard_map/ppermute | solution.py:355
  10.5 1.9 %collective-permute-start.1 = (bf16[2,64,2,128]{3,2,1,0:T(2,128)(2,1)S(1)}, bf16[2,64,2,128]{3,2,1,0:T(2,128)(2,1)S(1)}, u32[]{:S(2)}, u32[]{:S(2)}) collective-permute-start(bf16[2,64,2,128]{3,2,1,0:T(2,128)(2,1)S(1)} %get-tuple-element.22), channel_id=1, source_target_pairs={{1,0},{2,1},{3,2},{5,4},{6,5},{7,6},{9,8},{10,9},{11,10},{13,12},{... | collective-permute-start | bytes 196616 | tf_op jit(solution)/shard_map/ppermute | solution.py:356
  12.5 1.3 %collective-permute-start.2 = (bf16[17,48,128]{2,1,0:T(8,128)(2,1)S(1)}, bf16[17,48,128]{2,1,0:T(8,128)(2,1)S(1)}, u32[]{:S(2)}, u32[]{:S(2)}) collective-permute-start(bf16[17,48,128]{2,1,0:T(8,128)(2,1)S(1)} %get-tuple-element.25), channel_id=1, source_target_pairs={{0,4},{4,8},{8,12},{12,0},{1,5},{5,9},{9,13},{13,1},{2,6},{6,10},{... | collective-permute-start | bytes 626696 | tf_op jit(solution)/shard_map/ppermute | solution.py:289
  13.8 2.8 %shard_map.74 = bf16[17,48,128]{2,1,0:T(8,128)(2,1)S(1)} custom-call(bf16[2,64,64,128]{3,2,1,0:T(8,128)(2,1)S(1)} %get-tuple-element.31.refs_0_, bf16[3,3,128,128]{3,2,1,0:T(8,128)(2,1)S(1)} %get-tuple-element.23.refs_1_.refs_3_, bf16[3,3,128,128]{3,2,1,0:T(8,128)(2,1)S(1)} %get-tuple-element.24.refs_2_.refs_4_, f32[5,128]{1,0:T(8,128)S(1)} %maximum_maximum_fusion.refs_3_.refs_5_), custom_call_target="tpu_custom_call" | custom-call | flops 5000000000 | bytes 1000000 | tf_op jit(solution)/shard_map/pallas_call | solution.py:227
  16.6 2.4 %collective-permute-start.4 = (bf16[17,48,128]{2,1,0:T(8,128)(2,1)S(1)}, bf16[17,48,128]{2,1,0:T(8,128)(2,1)S(1)}, u32[]{:S(2)}, u32[]{:S(2)}) collective-permute-start(bf16[17,48,128]{2,1,0:T(8,128)(2,1)S(1)} %shard_map.74), channel_id=1, source_target_pairs={{0,8},{4,12},{8,0},{12,4},{1,9},{5,13},{9,1},{13,5},{2,10},{6,14},... | collective-permute-start | bytes 626696 | tf_op jit(solution)/shard_map/ppermute | solution.py:289
  19.0 0.0 collective-permute-done.refs_1_
  19.0 0.0 collective-permute-done.1.refs_2_
  19.0 0.7 %collective-permute-done.2.refs_0_ = bf16[17,48,128]{2,1,0:T(8,128)(2,1)S(1)} collective-permute-done((bf16[17,48,128]{2,1,0:T(8,128)(2,1)S(1)}, bf16[17,48,128]{2,1,0:T(8,128)(2,1)S(1)}, u32[]{:S(2)}, u32[]{:S(2)}) %collective-permute-start.2) | collective-permute-done | bytes 208928 | tf_op jit(solution)/shard_map/ppermute | solution.py:289
  19.6 1.6 %shard_map.75 = bf16[17,16,128]{2,1,0:T(8,128)(2,1)S(1)} custom-call(bf16[2,64,64,128]{3,2,1,0:T(8,128)(2,1)S(1)} %get-tuple-element.31.refs_0_, bf16[2,64,2,128]{3,2,1,0:T(2,128)(2,1)S(1)} %collective-permute-done.refs_1_, bf16[2,64,2,128]{3,2,1,0:T(2,128)(2,1)S(1)} %collective-permute-done.1.refs_2_, ...), custom_call_target="tpu_custom_call" | custom-call | flops 5000000000 | bytes 1000000 | tf_op jit(solution)/shard_map/pallas_call | solution.py:227
  21.3 1.7 %shard_map.76 = bf16[17,16,128]{2,1,0:T(8,128)(2,1)S(1)} custom-call(bf16[2,64,64,128]{3,2,1,0:T(8,128)(2,1)S(1)} %get-tuple-element.31.refs_0_, bf16[2,64,2,128]{3,2,1,0:T(2,128)(2,1)S(1)} %collective-permute-done.refs_1_, bf16[2,64,2,128]{3,2,1,0:T(2,128)(2,1)S(1)} %collective-permute-done.1.refs_2_, ...), custom_call_target="tpu_custom_call" | custom-call | flops 5000000000 | bytes 1000000 | tf_op jit(solution)/shard_map/pallas_call | solution.py:227
  22.9 1.3 %collective-permute-start.5 = (bf16[17,16,128]{2,1,0:T(8,128)(2,1)S(1)}, bf16[17,16,128]{2,1,0:T(8,128)(2,1)S(1)}, u32[]{:S(2)}, u32[]{:S(2)}) collective-permute-start(bf16[17,16,128]{2,1,0:T(8,128)(2,1)S(1)} %shard_map.76), channel_id=1, source_target_pairs={{0,8},{4,12},{8,0},{12,4},{1,9},{5,13},{9,1},{13,5},{2,10},{6,14},... | collective-permute-start | bytes 208904 | tf_op jit(solution)/shard_map/ppermute | solution.py:289
  24.2 2.0 %collective-permute-start.3 = (bf16[17,16,128]{2,1,0:T(8,128)(2,1)S(1)}, bf16[17,16,128]{2,1,0:T(8,128)(2,1)S(1)}, u32[]{:S(2)}, u32[]{:S(2)}) collective-permute-start(bf16[17,16,128]{2,1,0:T(8,128)(2,1)S(1)} %shard_map.75), channel_id=1, source_target_pairs={{0,4},{4,8},{8,12},{12,0},{1,5},{5,9},{9,13},{13,1},{2,6},{6,10},{... | collective-permute-start | bytes 208904 | tf_op jit(solution)/shard_map/ppermute | solution.py:289
  26.2 3.5 %shard_map.77 = bf16[17,64,128]{2,1,0:T(8,128)(2,1)S(1)} custom-call(bf16[2,64,64,128]{3,2,1,0:T(8,128)(2,1)S(1)} %get-tuple-element.31.refs_0_, bf16[2,64,2,128]{3,2,1,0:T(2,128)(2,1)S(1)} %collective-permute-done.refs_1_, bf16[2,64,2,128]{3,2,1,0:T(2,128)(2,1)S(1)} %collective-permute-done.1.refs_2_, ...), custom_call_target="tpu_custom_call" | custom-call | flops 5000000000 | bytes 1000000 | tf_op jit(solution)/shard_map/pallas_call | solution.py:227
  29.7 1.5 %collective-permute-start.6 = (bf16[17,64,128]{2,1,0:T(8,128)(2,1)S(1)}, bf16[17,64,128]{2,1,0:T(8,128)(2,1)S(1)}, u32[]{:S(2)}, u32[]{:S(2)}) collective-permute-start(bf16[17,64,128]{2,1,0:T(8,128)(2,1)S(1)} %shard_map.77), channel_id=1, source_target_pairs={{0,12},{4,0},{8,4},{12,8},{1,13},{5,1},{9,5},{13,9},{2,14},{6,2},{... | collective-permute-start | bytes 835592 | tf_op jit(solution)/shard_map/ppermute | solution.py:289
  31.2 3.5 %shard_map.78 = (f32[16,64,128]{2,1,0:T(8,128)S(1)}, f32[64,128]{1,0:T(8,128)S(1)}) custom-call(bf16[2,64,64,128]{3,2,1,0:T(8,128)(2,1)S(1)} %get-tuple-element.31.refs_0_, bf16[2,64,2,128]{3,2,1,0:T(2,128)(2,1)S(1)} %collective-permute-done.refs_1_, bf16[2,64,2,128]{3,2,1,0:T(2,128)(2,1)S(1)} %collective-permute-done.1.refs_2_, ...), custom_call_target="tpu_custom_call" | custom-call | flops 5000000000 | bytes 1000000 | tf_op jit(solution)/shard_map/pallas_call | solution.py:227
  34.7 0.0 collective-permute-done.4.refs_2_
  34.7 0.0 collective-permute-done.5.refs_3_
  34.7 0.0 collective-permute-done.3.refs_1_
  34.7 4.4 %collective-permute-done.6.refs_4_ = bf16[17,64,128]{2,1,0:T(8,128)(2,1)S(1)} collective-permute-done((bf16[17,64,128]{2,1,0:T(8,128)(2,1)S(1)}, bf16[17,64,128]{2,1,0:T(8,128)(2,1)S(1)}, u32[]{:S(2)}, u32[]{:S(2)}) %collective-permute-start.6) | collective-permute-done | bytes 278560 | tf_op jit(solution)/shard_map/ppermute | solution.py:289
  39.2 2.1 %shard_map.79 = f32[16,64,128]{2,1,0:T(8,128)} custom-call(f32[16,64,128]{2,1,0:T(8,128)S(1)} %get-tuple-element.32.own_ref, f32[64,128]{1,0:T(8,128)S(1)} %get-tuple-element.33.trans_ref, bf16[17,48,128]{2,1,0:T(8,128)(2,1)S(1)} %collective-permute-done.2.refs_0_, bf16[17,16,128]{2,1,0:T(8,128)(2,1)S(1)} %collective-permute-done.3.refs_1_, ...), custom_call_target="tpu_custom_call" | custom-call | tf_op jit(solution)/shard_map/pallas_call | solution.py:278
Async XLA Ops:
  6.0 12.9 %collective-permute-start = (bf16[2,64,2,128]{3,2,1,0:T(2,128)(2,1)S(1)}, bf16[2,64,2,128]{3,2,1,0:T(2,128)(2,1)S(1)}, u32[]{:S(2)}, u32[]{:S(2)}) collective-permute-start(bf16[2,64,2,128]{3,2,1,0:T(2,128)(2,1)S(1)} %get-tuple-element.21), channel_id=1, source_target_pairs={{0,1},{1,2},{2,3},{4,5},{5,6},{6,7},{8,9},{9,10},{10,11},{12,13},{... | collective-permute-start | bytes 196616 | tf_op jit(solution)/shard_map/ppermute | solution.py:355
  10.5 8.4 %collective-permute-start.1 = (bf16[2,64,2,128]{3,2,1,0:T(2,128)(2,1)S(1)}, bf16[2,64,2,128]{3,2,1,0:T(2,128)(2,1)S(1)}, u32[]{:S(2)}, u32[]{:S(2)}) collective-permute-start(bf16[2,64,2,128]{3,2,1,0:T(2,128)(2,1)S(1)} %get-tuple-element.22), channel_id=1, source_target_pairs={{1,0},{2,1},{3,2},{5,4},{6,5},{7,6},{9,8},{10,9},{11,10},{13,12},{... | collective-permute-start | bytes 196616 | tf_op jit(solution)/shard_map/ppermute | solution.py:356
  12.5 7.2 %collective-permute-start.2 = (bf16[17,48,128]{2,1,0:T(8,128)(2,1)S(1)}, bf16[17,48,128]{2,1,0:T(8,128)(2,1)S(1)}, u32[]{:S(2)}, u32[]{:S(2)}) collective-permute-start(bf16[17,48,128]{2,1,0:T(8,128)(2,1)S(1)} %get-tuple-element.25), channel_id=1, source_target_pairs={{0,4},{4,8},{8,12},{12,0},{1,5},{5,9},{9,13},{13,1},{2,6},{6,10},{... | collective-permute-start | bytes 626696 | tf_op jit(solution)/shard_map/ppermute | solution.py:289
  16.6 18.1 %collective-permute-start.4 = (bf16[17,48,128]{2,1,0:T(8,128)(2,1)S(1)}, bf16[17,48,128]{2,1,0:T(8,128)(2,1)S(1)}, u32[]{:S(2)}, u32[]{:S(2)}) collective-permute-start(bf16[17,48,128]{2,1,0:T(8,128)(2,1)S(1)} %shard_map.74), channel_id=1, source_target_pairs={{0,8},{4,12},{8,0},{12,4},{1,9},{5,13},{9,1},{13,5},{2,10},{6,14},... | collective-permute-start | bytes 626696 | tf_op jit(solution)/shard_map/ppermute | solution.py:289
  22.9 11.8 %collective-permute-start.5 = (bf16[17,16,128]{2,1,0:T(8,128)(2,1)S(1)}, bf16[17,16,128]{2,1,0:T(8,128)(2,1)S(1)}, u32[]{:S(2)}, u32[]{:S(2)}) collective-permute-start(bf16[17,16,128]{2,1,0:T(8,128)(2,1)S(1)} %shard_map.76), channel_id=1, source_target_pairs={{0,8},{4,12},{8,0},{12,4},{1,9},{5,13},{9,1},{13,5},{2,10},{6,14},... | collective-permute-start | bytes 208904 | tf_op jit(solution)/shard_map/ppermute | solution.py:289
  24.2 10.5 %collective-permute-start.3 = (bf16[17,16,128]{2,1,0:T(8,128)(2,1)S(1)}, bf16[17,16,128]{2,1,0:T(8,128)(2,1)S(1)}, u32[]{:S(2)}, u32[]{:S(2)}) collective-permute-start(bf16[17,16,128]{2,1,0:T(8,128)(2,1)S(1)} %shard_map.75), channel_id=1, source_target_pairs={{0,4},{4,8},{8,12},{12,0},{1,5},{5,9},{9,13},{13,1},{2,6},{6,10},{... | collective-permute-start | bytes 208904 | tf_op jit(solution)/shard_map/ppermute | solution.py:289
  29.7 9.4 %collective-permute-start.6 = (bf16[17,64,128]{2,1,0:T(8,128)(2,1)S(1)}, bf16[17,64,128]{2,1,0:T(8,128)(2,1)S(1)}, u32[]{:S(2)}, u32[]{:S(2)}) collective-permute-start(bf16[17,64,128]{2,1,0:T(8,128)(2,1)S(1)} %shard_map.77), channel_id=1, source_target_pairs={{0,12},{4,0},{8,4},{12,8},{1,13},{5,1},{9,5},{13,9},{2,14},{6,2},{... | collective-permute-start | bytes 835592 | tf_op jit(solution)/shard_map/ppermute | solution.py:289

commit v3 on v1

--- a/solution.py
+++ b/solution.py
@@ -8,9 +8,17 @@
 from jax.sharding import PartitionSpec as P
 
 VM = pl.BlockSpec(memory_space=pltpu.VMEM)
-ANY = pl.BlockSpec(memory_space=pl.ANY)
+HBM = pl.BlockSpec(memory_space=pltpu.HBM)
 F32 = jnp.float32
 BF16 = jnp.bfloat16
+
+PIECE = ((3, 2, 1, 0), (2, 0, 3, 1), (1, 3, 0, 2), (0, 1, 2, 3))
+FAR = [(0, 1), (3, 2)]
+NEAR = [(1, 2), (2, 1)]
+SECOND = [(0, 2), (3, 1), (1, 0), (2, 3)]
+THIRD = [(0, 1), (3, 2), (1, 3), (2, 0)]
+MERGE = (0, 1, 2, 0)
+KEYS = ((0, 1, 2, 3), (9, 2, 1, 9), (1, 3, 0, 2), (2, 0, 3, 0))
 
 
 def gelu(x):
@@ -30,16 +38,28 @@
     return jnp.concatenate(blocks, axis=0)
 
 
-def edges_kernel(x_hbm, top_ref, bot_ref, buf, sem):
+def odd_row():
+    return lax.rem(lax.axis_index("rows"), 2) == 1
+
+
+def edges_kernel(x_hbm, one_ref, two_ref, buf, sem):
     rows = x_hbm.shape[2]
     a = pltpu.make_async_copy(x_hbm.at[:, :, pl.ds(0, 8)], buf.at[0], sem.at[0])
     b = pltpu.make_async_copy(x_hbm.at[:, :, pl.ds(rows - 8, 8)], buf.at[1], sem.at[1])
     a.start()
     b.start()
     a.wait()
-    top_ref[...] = buf[0, :, :, 0:2]
     b.wait()
-    bot_ref[...] = buf[1, :, :, 6:8]
+
+    @pl.when(odd_row())
+    def _():
+        one_ref[...] = buf[0, :, :, 0:2]
+        two_ref[...] = buf[1, :, :, 6:8]
+
+    @pl.when(jnp.logical_not(odd_row()))
+    def _():
+        one_ref[...] = buf[1, :, :, 6:8]
+        two_ref[...] = buf[0, :, :, 0:2]
 
 
 def edges(x):
@@ -48,26 +68,64 @@
     return pl.pallas_call(
         edges_kernel,
         out_shape=(shape, shape),
-        in_specs=[ANY],
+        in_specs=[HBM],
         out_specs=(VM, VM),
         scratch_shapes=[
             pltpu.VMEM((2, planes, cols, 8, ch), x.dtype),
             pltpu.SemaphoreType.DMA((2,)),
         ],
         compiler_params=pltpu.CompilerParams(vmem_limit_bytes=8 << 20),
-    )(x)
-
-
-def chunk_kernel(pick, packed, x_ref, above_ref, below_ref, w1_ref, w2_ref, par_ref, *refs):
-    if packed:
-        out_ref, f_ref, xs, f2_ref, hs, fs = refs
-    else:
-        out_ref, trans_ref, f_ref, xs, f2_ref, hs, fs = refs
+    )(pltpu.with_memory_space_constraint(x, pltpu.HBM))
+
+
+def load_kernel(x_hbm, w1_hbm, w2_hbm, b1_hbm, b2_hbm, ow_hbm, ob_ref, x_ref, w1_ref, w2_ref, par_ref, sem):
+    pieces = 4
+    step = x_ref.shape[1] // pieces
+    pairs = [
+        (w1_hbm, w1_ref),
+        (w2_hbm, w2_ref),
+        (b1_hbm, par_ref.at[0]),
+        (b2_hbm, par_ref.at[1]),
+        (ow_hbm, par_ref.at[2]),
+    ]
+    for i in range(pieces):
+        at = (slice(None), pl.ds(i * step, step))
+        pairs.append((x_hbm.at[at], x_ref.at[at]))
+    copies = [pltpu.make_async_copy(src, dst, sem.at[i]) for i, (src, dst) in enumerate(pairs)]
+    for copy in copies:
+        copy.start()
+    for p in range(x_ref.shape[0]):
+        par_ref[3 + p : 4 + p] = jnp.full((1, x_ref.shape[3]), ob_ref[p])
+    for copy in copies:
+        copy.wait()
+
+
+def load(x, w1, w2, b1, b2, ow, ob):
+    args = [pltpu.with_memory_space_constraint(a, pltpu.HBM) for a in (x, w1, w2, b1, b2, ow)]
+    out_shape = [jax.ShapeDtypeStruct(a.shape, a.dtype) for a in (x, w1, w2)]
+    out_shape.append(jax.ShapeDtypeStruct((3 + x.shape[0], x.shape[3]), F32))
+    return pl.pallas_call(
+        load_kernel,
+        out_shape=out_shape,
+        in_specs=[HBM] * 6 + [pl.BlockSpec(memory_space=pltpu.SMEM)],
+        out_specs=[VM] * 4,
+        scratch_shapes=[pltpu.SemaphoreType.DMA((9,))],
+        compiler_params=pltpu.CompilerParams(vmem_limit_bytes=8 << 20),
+        cost_estimate=pl.CostEstimate(flops=10**9, transcendentals=0, bytes_accessed=10**6),
+    )(*args, ob)
+
+
+def chunk_kernel(pick, packed, x_ref, one_ref, two_ref, w1_ref, w2_ref, par_ref, *refs):
+    refs = list(refs)
+    out_ref = refs.pop(0)
+    trans_ref = None if packed else refs.pop(0)
+    f_ref, xs, f2_ref, hs, fs = refs
     planes, cols, rows, ch = x_ref.shape
-    ext = rows + 16
-    nc = fs.shape[1]
+    nc, nr = fs.shape[1:3]
+    ext = xs.shape[3]
     slots = f_ref.shape[0]
     c0 = pick() * nc
+    odd = odd_row()
     for i in range(planes * (nc + 4)):
         p, c = divmod(i, nc + 4)
         at = c0 - 2 + c
@@ -75,9 +133,11 @@
         at = jnp.clip(at, 0, cols - 1)
         keep = jnp.where(inside, 1.0, 0.0)
         f = f_ref.at[i % slots]
+        one = one_ref[p, at].astype(F32)
+        two = two_ref[p, at].astype(F32)
         f[16 : 16 + rows] = x_ref[p, at].astype(F32) * keep
-        f[14:16] = above_ref[p, at].astype(F32) * keep
-        f[16 + rows : 18 + rows] = below_ref[p, at].astype(F32) * keep
+        f[14:16] = jnp.where(odd, one, two) * keep
+        f[16 + rows : 18 + rows] = jnp.where(odd, two, one) * keep
         for d in range(3):
             xs[d, p, c] = f[7 + d : 7 + d + ext].astype(BF16)
     here = lax.axis_index("rows")
@@ -106,9 +166,9 @@
             f2[8 + rows : 9 + rows] = f2[8 + rows : 9 + rows] * below
             for d in range(3):
                 hs[d, p, c] = f2[7 + d : 7 + d + rows].astype(BF16)
-    lane = lax.broadcasted_iota(jnp.int32, (rows, ch), 1)
+    lane = lax.broadcasted_iota(jnp.int32, (nr, ch), 1)
     weights = pair_weights(w2_ref)
-    logits = [jnp.zeros((rows, ch), F32) for _ in range(planes)]
+    logits = [jnp.zeros((nr, ch), F32) for _ in range(planes)]
     taps = []
     for j in range(4):
         for d in range(3):
@@ -121,8 +181,8 @@
     for c in range(nc):
         g, o = divmod(c, 2)
         for p in range(planes):
-            r0 = (g * planes + p) * rows
-            f = gelu(y[r0 : r0 + rows, o * ch : (o + 1) * ch] + bias_two)
+            r0 = (g * planes + p) * nr
+            f = gelu(y[r0 : r0 + nr, o * ch : (o + 1) * ch] + bias_two)
             total = jnp.sum(f * opacity, axis=1, keepdims=True)
             logits[p] = jnp.where(lane == c, total, logits[p])
             fs[p, c] = f
@@ -140,30 +200,26 @@
         color = sum(parts[p][:, c : c + 1] * fs[p, c] for p in range(planes))
         out_ref[c] = color.astype(out_ref.dtype)
     if packed:
-        high = trans.astype(BF16).astype(F32)
-        low = pltpu.roll(trans - high, nc, axis=1)
-        out_ref[nc] = jnp.where(lane < nc, high, low).astype(out_ref.dtype)
+        out_ref[nc] = pack_trans(trans, nc)
     else:
         trans_ref[...] = trans
 
 
-def chunk(pick, nc, packed, x, above, below, w1, w2, par):
+def chunk(pick, nc, packed, x, one, two, w1, w2, par):
     planes, cols, rows, ch = x.shape
     ext = rows + 16
     if packed:
-        out_shape = jax.ShapeDtypeStruct((nc + 1, rows, ch), BF16)
-        out_specs = VM
+        out_shape = [jax.ShapeDtypeStruct((nc + 1, rows, ch), BF16)]
     else:
-        out_shape = (
+        out_shape = [
             jax.ShapeDtypeStruct((nc, rows, ch), F32),
             jax.ShapeDtypeStruct((rows, ch), F32),
-        )
-        out_specs = (VM, VM)
+        ]
     return pl.pallas_call(
         functools.partial(chunk_kernel, pick, packed),
         out_shape=out_shape,
         in_specs=[VM] * 6,
-        out_specs=out_specs,
+        out_specs=[VM] * len(out_shape),
         scratch_shapes=[
             pltpu.VMEM((8, rows + 32, ch), F32),
             pltpu.VMEM((3, planes, nc + 4, ext, ch), BF16),
@@ -172,24 +228,67 @@
             pltpu.VMEM((planes, nc, rows, ch), F32),
         ],
         compiler_params=pltpu.CompilerParams(vmem_limit_bytes=16 << 20),
-    )(x, above, below, w1, w2, par)
+        cost_estimate=pl.CostEstimate(flops=5 * 10**9, transcendentals=0, bytes_accessed=10**6),
+    )(x, one, two, w1, w2, par)
+
+
+def lookup(table):
+    here = lax.axis_index("depth")
+    value = jnp.int32(table[-1])
+    for i in range(len(table) - 1):
+        value = jnp.where(here == i, table[i], value)
+    return value
+
+
+def unpack_trans(packed):
+    nc = packed.shape[0] - 1
+    t = packed[nc].astype(F32)
+    return t + pltpu.roll(t, t.shape[1] - nc, axis=1)
+
+
+def pack_trans(trans, nc):
+    lane = lax.broadcasted_iota(jnp.int32, trans.shape, 1)
+    high = trans.astype(BF16).astype(F32)
+    low = pltpu.roll(trans - high, nc, axis=1)
+    return jnp.where(lane < nc, high, low).astype(BF16)
+
+
+def merge_kernel(own_ref, trans_ref, got_ref, out_ref):
+    nc = own_ref.shape[0]
+    mine = trans_ref[...]
+    theirs = unpack_trans(got_ref)
+    role = lookup(MERGE)
+    scale_own = jnp.where(role == 1, theirs, 1.0)
+    scale_got = jnp.where(role == 2, mine, jnp.where(role == 1, 1.0, 0.0))
+    for c in range(nc):
+        color = scale_own[:, c : c + 1] * own_ref[c]
+        color = color + scale_got[:, c : c + 1] * got_ref[c].astype(F32)
+        out_ref[c] = color.astype(BF16)
+    out_ref[nc] = pack_trans(jnp.where(role == 0, mine, mine * theirs), nc)
+
+
+def merge(own, trans, got):
+    return pl.pallas_call(
+        merge_kernel,
+        out_shape=jax.ShapeDtypeStruct(got.shape, BF16),
+        in_specs=[VM] * 3,
+        out_specs=VM,
+        compiler_params=pltpu.CompilerParams(vmem_limit_bytes=8 << 20),
+        cost_estimate=pl.CostEstimate(flops=10**9, transcendentals=0, bytes_accessed=10**6),
+    )(own, trans, got)
 
 
 def combine_kernel(own_ref, trans_ref, *refs):
     *got_refs, out_ref = refs
-    nc, rows, ch = own_ref.shape
-    here = lax.axis_index("depth")
-    trans = [trans_ref[...]]
-    for ref in got_refs:
-        t = ref[nc].astype(F32)
-        trans.append(t + pltpu.roll(t, ch - nc, axis=1))
+    nc = own_ref.shape[0]
+    keys = [lookup(table) for table in KEYS]
+    trans = [trans_ref[...]] + [unpack_trans(ref) for ref in got_refs]
     scale = []
     for k in range(len(trans)):
         w = None
         for m in range(len(trans)):
             if m != k:
-                front = jnp.bitwise_xor(here, m) < jnp.bitwise_xor(here, k)
-                term = jnp.where(front, trans[m], 1.0)
+                term = jnp.where(keys[m] < keys[k], trans[m], 1.0)
                 w = term if w is None else w * term
         scale.append(w)
     for c in range(nc):
@@ -246,34 +345,34 @@
     planes, cols, rows, ch = volume.shape
     slabs = lax.axis_size("depth")
     size = lax.axis_size("rows")
-    par = jnp.concatenate(
-        [
-            jnp.stack([bias_one, bias_two, opacity_weight]),
-            jnp.broadcast_to(opacity_bias[:, None], (planes, ch)),
-        ]
+    one, two = edges(volume)
+    one = lax.ppermute(one, "rows", [(i, i ^ 1) for i in range(size)])
+    inner = [(i, i + 1) for i in range(1, size - 1, 2)]
+    two = lax.ppermute(two, "rows", inner + [(j, i) for i, j in inner])
+    x, w1, w2, par = load(
+        volume, conv_one, conv_two, bias_one, bias_two, opacity_weight, opacity_bias
     )
-    top, bot = edges(volume)
-    above = lax.ppermute(bot, "rows", [(i, i + 1) for i in range(size - 1)])
-    below = lax.ppermute(top, "rows", [(i + 1, i) for i in range(size - 1)])
-    args = (volume, above, below, conv_one, conv_two, par)
-    if slabs > 4:
+    args = (x, one, two, w1, w2, par)
+    if slabs != 4:
         nc = 16
-        done = [
-            chunk(functools.partial(jnp.int32, i), nc, False, *args) for i in range(cols // nc)
-        ]
+        done = [chunk(functools.partial(jnp.int32, i), nc, False, *args) for i in range(cols // nc)]
         color = jnp.concatenate([c for c, _ in done])
         trans = jnp.concatenate([jnp.transpose(t[:, :nc]) for _, t in done])
         return butterfly(color, trans)
     nc = cols // slabs
 
-    def pick(k):
-        return lambda: jnp.bitwise_xor(lax.axis_index("depth"), k)
-
-    got = {}
-    for k in [k for k in (2, 3, 1) if k < slabs]:
-        got[k] = exchange(chunk(pick(k), nc, True, *args), "depth", k)
-    own, trans = chunk(pick(0), nc, False, *args)
-    return combine(own, trans, [got[k] for k in sorted(got)])
+    def piece(slot, packed):
+        pick = functools.partial(lookup, [order[slot] for order in PIECE])
+        return chunk(pick, nc, packed, x, one, two, w1, w2, par)
+
+    (first,) = piece(0, True)
+    far = lax.ppermute(first, "depth", FAR)
+    near = lax.ppermute(first, "depth", NEAR)
+    (second,) = piece(1, True)
+    second = lax.ppermute(second, "depth", SECOND)
+    third = lax.ppermute(merge(*piece(2, False), far), "depth", THIRD)
+    own, trans = piece(3, False)
+    return combine(own, trans, [near, second, third])
 
 
 def solution(mesh):

time: 48 us -> 36.3 us (0.76)
  the two profiles are of different devices: /device:TPU:21 before, /device:TPU:1 now
where the time goes in v3:
time: 36.3 us; the launch traced here: 36.1 us
  Pallas kernels  19.3 us (53%)
  starting transfers between devices  10.8 us (30%)
  waiting for transfers between devices  5.83 us (16%)
    pallas_call x4, Pallas kernels, chunk(): pl.pallas_call(functools.partial(chunk_kernel, pick, packed), out_shape=o...  13.9 us
    ppermute x1, waiting for transfers between devices, per_device(): third = lax.ppermute(merge(*piece(2, False), far), 'depth', THIRD)  5.82 us
    ppermute x1, starting transfers between devices, per_device(): two = lax.ppermute(two, 'rows', inner + [(j, i) for i, j in inner])  4.47 us
    ppermute x1, starting transfers between devices, per_device(): far = lax.ppermute(first, 'depth', FAR)  3.36 us
    pallas_call x1, Pallas kernels, load(): pl.pallas_call(load_kernel, out_shape=out_shape, in_specs=[HBM] * 6 + [pl...  2.37 us
    ppermute x1, starting transfers between devices, per_device(): second = lax.ppermute(second, 'depth', SECOND)  1.83 us
    pallas_call x1, Pallas kernels, combine(): pl.pallas_call(combine_kernel, out_shape=jax.ShapeDtypeStruct(own.shape,...  1.51 us
    pallas_call x1, Pallas kernels, edges(): pl.pallas_call(edges_kernel, out_shape=(shape, shape), in_specs=[HBM], ou...  1.19 us
  transfers between devices with their start and end apart: 6, of which 1 were waited for; matrix products, arithmetic and copies ran while one was open for 0% of the time, Pallas kernels for 36%

profile of v3, /device:TPU:1, one launch (start us, length us, event | category | flops | bytes accessed | tf_op | source)
XLA Modules:
  0.0 36.1 jit_solution(4348886805376260235)
XLA Ops:
  0.0 0.0 copy-start
  0.0 1.2 %shard_map.74 = (bf16[2,64,2,128]{3,2,1,0:T(2,128)(2,1)S(1)}, bf16[2,64,2,128]{3,2,1,0:T(2,128)(2,1)S(1)}) custom-call(bf16[2,64,64,128]{3,2,1,0:T(8,128)(2,1)} %x_hbm.3), custom_call_target="tpu_custom_call" | custom-call | tf_op jit(solution)/shard_map/pallas_call | solution.py:68
  1.2 0.1 collective-permute-start
  1.3 4.5 %collective-permute-start.1 = (bf16[2,64,2,128]{3,2,1,0:T(2,128)(2,1)S(1)}, bf16[2,64,2,128]{3,2,1,0:T(2,128)(2,1)S(1)}, u32[]{:S(2)}, u32[]{:S(2)}) collective-permute-start(bf16[2,64,2,128]{3,2,1,0:T(2,128)(2,1)S(1)} %get-tuple-element.17), channel_id=1, source_target_pairs={{1,2},{2,1},{5,6},{6,5},{9,10},{10,9},{13,14},{14,13},{17,18},{18,... | collective-permute-start | bytes 196616 | tf_op jit(solution)/shard_map/ppermute | solution.py:351
  5.8 0.0 copy-done
  5.8 2.4 %shard_map.73 = (bf16[2,64,64,128]{3,2,1,0:T(8,128)(2,1)S(1)}, bf16[3,3,128,128]{3,2,1,0:T(8,128)(2,1)S(1)}, bf16[3,3,128,128]{3,2,1,0:T(8,128)(2,1)S(1)}, f32[5,128]{1,0:T(8,128)S(1)}) custom-call(bf16[2,64,64,128]{3,2,1,0:T(8,128)(2,1)} %x_hbm.3, bf16[3,3,128,128]{3,2,1,0:T(8,128)(2,1)} %w1_hbm.1, bf16[3,3,128,128]{3,2,1,0:T(8,128)(2,1)} %w2_hbm.1, ...), custom_call_target="tpu_custom_call" | custom-call | flops 1000000000 | bytes 1000000 | tf_op jit(solution)/shard_map/pallas_call | solution.py:107
  8.2 0.0 collective-permute-done.one_ref
  8.2 0.0 collective-permute-done.1.two_ref
  8.2 3.5 %shard_map.76 = bf16[17,64,128]{2,1,0:T(8,128)(2,1)S(1)} custom-call(bf16[2,64,64,128]{3,2,1,0:T(8,128)(2,1)S(1)} %get-tuple-element.15.x_ref, bf16[2,64,2,128]{3,2,1,0:T(2,128)(2,1)S(1)} %collective-permute-done.one_ref, bf16[2,64,2,128]{3,2,1,0:T(2,128)(2,1)S(1)} %collective-permute-done.1.two_ref, bf16[3,3,128,128]{3,2,1,0:T(8,128)(2,1)S(1)} %get-tuple-element.18.w1_ref, ...), custom_call_target="tpu_custom_call" | custom-call | flops 5000000000 | bytes 1000000 | tf_op jit(solution)/shard_map/pallas_call | solution.py:218
  11.7 3.4 %collective-permute-start.4 = (bf16[17,64,128]{2,1,0:T(8,128)(2,1)S(1)}, bf16[17,64,128]{2,1,0:T(8,128)(2,1)S(1)}, u32[]{:S(2)}, u32[]{:S(2)}) collective-permute-start(bf16[17,64,128]{2,1,0:T(8,128)(2,1)S(1)} %shard_map.76), channel_id=1, source_target_pairs={{0,4},{12,8},{1,5},{13,9},{2,6},{14,10},{3,7},{15,11},{16,20},{28,... | collective-permute-start | bytes 835592 | tf_op jit(solution)/shard_map/ppermute | solution.py:369
  15.0 0.7 %collective-permute-start.2 = (bf16[17,64,128]{2,1,0:T(8,128)(2,1)S(1)}, bf16[17,64,128]{2,1,0:T(8,128)(2,1)S(1)}, u32[]{:S(2)}, u32[]{:S(2)}) collective-permute-start(bf16[17,64,128]{2,1,0:T(8,128)(2,1)S(1)} %shard_map.76), channel_id=1, source_target_pairs={{4,8},{8,4},{5,9},{9,5},{6,10},{10,6},{7,11},{11,7},{20,24},{24,20... | collective-permute-start | bytes 835592 | tf_op jit(solution)/shard_map/ppermute | solution.py:370
  15.7 3.5 %shard_map.77 = bf16[17,64,128]{2,1,0:T(8,128)(2,1)S(1)} custom-call(bf16[2,64,64,128]{3,2,1,0:T(8,128)(2,1)S(1)} %get-tuple-element.15.x_ref, bf16[2,64,2,128]{3,2,1,0:T(2,128)(2,1)S(1)} %collective-permute-done.one_ref, bf16[2,64,2,128]{3,2,1,0:T(2,128)(2,1)S(1)} %collective-permute-done.1.two_ref, bf16[3,3,128,128]{3,2,1,0:T(8,128)(2,1)S(1)} %get-tuple-element.18.w1_ref, ...), custom_call_target="tpu_custom_call" | custom-call | flops 5000000000 | bytes 1000000 | tf_op jit(solution)/shard_map/pallas_call | solution.py:218
  19.2 1.8 %collective-permute-start.3 = (bf16[17,64,128]{2,1,0:T(8,128)(2,1)S(1)}, bf16[17,64,128]{2,1,0:T(8,128)(2,1)S(1)}, u32[]{:S(2)}, u32[]{:S(2)}) collective-permute-start(bf16[17,64,128]{2,1,0:T(8,128)(2,1)S(1)} %shard_map.77), channel_id=1, source_target_pairs={{0,8},{12,4},{4,0},{8,12},{1,9},{13,5},{5,1},{9,13},{2,10},{14,6},... | collective-permute-start | bytes 835592 | tf_op jit(solution)/shard_map/ppermute | solution.py:372
  21.0 3.4 %shard_map.78 = (f32[16,64,128]{2,1,0:T(8,128)S(1)}, f32[64,128]{1,0:T(8,128)S(1)}) custom-call(bf16[2,64,64,128]{3,2,1,0:T(8,128)(2,1)S(1)} %get-tuple-element.15.x_ref, bf16[2,64,2,128]{3,2,1,0:T(2,128)(2,1)S(1)} %collective-permute-done.one_ref, bf16[2,64,2,128]{3,2,1,0:T(2,128)(2,1)S(1)} %collective-permute-done.1.two_ref, ...), custom_call_target="tpu_custom_call" | custom-call | flops 5000000000 | bytes 1000000 | tf_op jit(solution)/shard_map/pallas_call | solution.py:218
  24.5 0.0 collective-permute-done.4.got_ref
  24.5 0.4 %shard_map.79 = bf16[17,64,128]{2,1,0:T(8,128)(2,1)S(1)} custom-call(f32[16,64,128]{2,1,0:T(8,128)S(1)} %get-tuple-element.23.own_ref, f32[64,128]{1,0:T(8,128)S(1)} %get-tuple-element.24.trans_ref, bf16[17,64,128]{2,1,0:T(8,128)(2,1)S(1)} %collective-permute-done.4.got_ref), custom_call_target="tpu_custom_call" | custom-call | flops 1000000000 | bytes 1000000 | tf_op jit(solution)/shard_map/pallas_call | solution.py:271
  24.9 0.4 %collective-permute-start.5 = (bf16[17,64,128]{2,1,0:T(8,128)(2,1)S(1)}, bf16[17,64,128]{2,1,0:T(8,128)(2,1)S(1)}, u32[]{:S(2)}, u32[]{:S(2)}) collective-permute-start(bf16[17,64,128]{2,1,0:T(8,128)(2,1)S(1)} %shard_map.79), channel_id=1, source_target_pairs={{0,4},{12,8},{4,12},{8,0},{1,5},{13,9},{5,13},{9,1},{2,6},{14,10},... | collective-permute-start | bytes 835592 | tf_op jit(solution)/shard_map/ppermute | solution.py:373
  25.3 3.5 %shard_map.75 = (f32[16,64,128]{2,1,0:T(8,128)S(1)}, f32[64,128]{1,0:T(8,128)S(1)}) custom-call(bf16[2,64,64,128]{3,2,1,0:T(8,128)(2,1)S(1)} %get-tuple-element.15.x_ref, bf16[2,64,2,128]{3,2,1,0:T(2,128)(2,1)S(1)} %collective-permute-done.one_ref, bf16[2,64,2,128]{3,2,1,0:T(2,128)(2,1)S(1)} %collective-permute-done.1.two_ref, ...), custom_call_target="tpu_custom_call" | custom-call | flops 5000000000 | bytes 1000000 | tf_op jit(solution)/shard_map/pallas_call | solution.py:218
  28.7 0.0 collective-permute-done.2.refs_0_
  28.8 0.0 collective-permute-done.3.refs_1_
  28.8 5.8 %collective-permute-done.5.refs_2_ = bf16[17,64,128]{2,1,0:T(8,128)(2,1)S(1)} collective-permute-done((bf16[17,64,128]{2,1,0:T(8,128)(2,1)S(1)}, bf16[17,64,128]{2,1,0:T(8,128)(2,1)S(1)}, u32[]{:S(2)}, u32[]{:S(2)}) %collective-permute-start.5) | collective-permute-done | bytes 278560 | tf_op jit(solution)/shard_map/ppermute | solution.py:373
  34.6 1.5 %shard_map.80 = f32[16,64,128]{2,1,0:T(8,128)} custom-call(f32[16,64,128]{2,1,0:T(8,128)S(1)} %get-tuple-element.21.own_ref, f32[64,128]{1,0:T(8,128)S(1)} %get-tuple-element.22.trans_ref, bf16[17,64,128]{2,1,0:T(8,128)(2,1)S(1)} %collective-permute-done.2.refs_0_, bf16[17,64,128]{2,1,0:T(8,128)(2,1)S(1)} %collective-permute-done.3.refs_1_, ...), custom_call_target="tpu_custom_call" | custom-call | tf_op jit(solution)/shard_map/pallas_call | solution.py:302
Async XLA Ops:
  0.0 5.8 %copy-start = (f32[2]{0:T(128)S(1)}, f32[2]{0:T(128)}, u32[]{:S(2)}) copy-start(f32[2]{0:T(128)} %ob_ref.1) | copy-start | bytes 28
  1.2 7.0 %collective-permute-start = (bf16[2,64,2,128]{3,2,1,0:T(2,128)(2,1)S(1)}, bf16[2,64,2,128]{3,2,1,0:T(2,128)(2,1)S(1)}, u32[]{:S(2)}, u32[]{:S(2)}) collective-permute-start(bf16[2,64,2,128]{3,2,1,0:T(2,128)(2,1)S(1)} %get-tuple-element.16), channel_id=1, source_target_pairs={{0,1},{1,0},{2,3},{3,2},{4,5},{5,4},{6,7},{7,6},{8,9},{9,8},{10,11... | collective-permute-start | bytes 196616 | tf_op jit(solution)/shard_map/ppermute | solution.py:349
  1.3 6.9 %collective-permute-start.1 = (bf16[2,64,2,128]{3,2,1,0:T(2,128)(2,1)S(1)}, bf16[2,64,2,128]{3,2,1,0:T(2,128)(2,1)S(1)}, u32[]{:S(2)}, u32[]{:S(2)}) collective-permute-start(bf16[2,64,2,128]{3,2,1,0:T(2,128)(2,1)S(1)} %get-tuple-element.17), channel_id=1, source_target_pairs={{1,2},{2,1},{5,6},{6,5},{9,10},{10,9},{13,14},{14,13},{17,18},{18,... | collective-permute-start | bytes 196616 | tf_op jit(solution)/shard_map/ppermute | solution.py:351
  11.7 12.8 %collective-permute-start.4 = (bf16[17,64,128]{2,1,0:T(8,128)(2,1)S(1)}, bf16[17,64,128]{2,1,0:T(8,128)(2,1)S(1)}, u32[]{:S(2)}, u32[]{:S(2)}) collective-permute-start(bf16[17,64,128]{2,1,0:T(8,128)(2,1)S(1)} %shard_map.76), channel_id=1, source_target_pairs={{0,4},{12,8},{1,5},{13,9},{2,6},{14,10},{3,7},{15,11},{16,20},{28,... | collective-permute-start | bytes 835592 | tf_op jit(solution)/shard_map/ppermute | solution.py:369
  15.0 13.7 %collective-permute-start.2 = (bf16[17,64,128]{2,1,0:T(8,128)(2,1)S(1)}, bf16[17,64,128]{2,1,0:T(8,128)(2,1)S(1)}, u32[]{:S(2)}, u32[]{:S(2)}) collective-permute-start(bf16[17,64,128]{2,1,0:T(8,128)(2,1)S(1)} %shard_map.76), channel_id=1, source_target_pairs={{4,8},{8,4},{5,9},{9,5},{6,10},{10,6},{7,11},{11,7},{20,24},{24,20... | collective-permute-start | bytes 835592 | tf_op jit(solution)/shard_map/ppermute | solution.py:370
  19.2 9.5 %collective-permute-start.3 = (bf16[17,64,128]{2,1,0:T(8,128)(2,1)S(1)}, bf16[17,64,128]{2,1,0:T(8,128)(2,1)S(1)}, u32[]{:S(2)}, u32[]{:S(2)}) collective-permute-start(bf16[17,64,128]{2,1,0:T(8,128)(2,1)S(1)} %shard_map.77), channel_id=1, source_target_pairs={{0,8},{12,4},{4,0},{8,12},{1,9},{13,5},{5,1},{9,13},{2,10},{14,6},... | collective-permute-start | bytes 835592 | tf_op jit(solution)/shard_map/ppermute | solution.py:372
  24.9 9.7 %collective-permute-start.5 = (bf16[17,64,128]{2,1,0:T(8,128)(2,1)S(1)}, bf16[17,64,128]{2,1,0:T(8,128)(2,1)S(1)}, u32[]{:S(2)}, u32[]{:S(2)}) collective-permute-start(bf16[17,64,128]{2,1,0:T(8,128)(2,1)S(1)} %shard_map.79), channel_id=1, source_target_pairs={{0,4},{12,8},{4,12},{8,0},{1,5},{13,9},{5,13},{9,1},{2,6},{14,10},... | collective-permute-start | bytes 835592 | tf_op jit(solution)/shard_map/ppermute | solution.py:373

commit v4 on v3

v4 whole, which is shorter than its diff:
```python
import functools

import jax
import jax.numpy as jnp
from jax import lax
from jax.experimental import pallas as pl
from jax.experimental.pallas import tpu as pltpu
from jax.sharding import PartitionSpec as P

VM = pl.BlockSpec(memory_space=pltpu.VMEM)
HBM = pl.BlockSpec(memory_space=pltpu.HBM)
F32 = jnp.float32
BF16 = jnp.bfloat16

PIECE = ((3, 2, 1, 0), (2, 0, 3, 1), (1, 3, 0, 2), (0, 1, 2, 3))
FAR = [(0, 1), (3, 2)]
NEAR = [(1, 2), (2, 1)]
SECOND = [(0, 2), (3, 1), (1, 0), (2, 3)]
THIRD = [(0, 1), (3, 2), (1, 3), (2, 0)]
MERGE = (0, 1, 2, 0)
KEYS = ((0, 1, 2, 3), (9, 2, 1, 9), (1, 3, 0, 2))
LAST_IN_FRONT = (0, 1, 0, 1)


def gelu(x):
    c = 0.7978845608028654
    half = 0.5 * x
    return half + half * jnp.tanh(x * (c + (c * 0.044715) * (x * x)))


def pair_weights(w_ref):
    zero = jnp.zeros((w_ref.shape[2], w_ref.shape[3]), w_ref.dtype)
    blocks = []
    for j in range(4):
        for d in range(3):
            first = w_ref[j, d] if j < 3 else zero
            second = w_ref[j - 1, d] if j > 0 else zero
            blocks.append(jnp.concatenate([first, second], axis=1))
    return jnp.concatenate(blocks, axis=0)


def odd_row():
    return lax.rem(lax.axis_index("rows"), 2) == 1


def edges_kernel(x_hbm, one_ref, two_ref, buf, sem):
    rows = x_hbm.shape[2]
    a = pltpu.make_async_copy(x_hbm.at[:, :, pl.ds(0, 8)], buf.at[0], sem.at[0])
    b = pltpu.make_async_copy(x_hbm.at[:, :, pl.ds(rows - 8, 8)], buf.at[1], sem.at[1])
    a.start()
    b.start()
    a.wait()
    b.wait()

    @pl.when(odd_row())
    def _():
        one_ref[...] = buf[0, :, :, 0:2]
        two_ref[...] = buf[1, :, :, 6:8]

    @pl.when(jnp.logical_not(odd_row()))
    def _():
        one_ref[...] = buf[1, :, :, 6:8]
        two_ref[...] = buf[0, :, :, 0:2]


def edges(x):
    planes, cols, rows, ch = x.shape
    shape = jax.ShapeDtypeStruct((planes, cols, 2, ch), x.dtype)
    return pl.pallas_call(
        edges_kernel,
        out_shape=(shape, shape),
        in_specs=[HBM],
        out_specs=(VM, VM),
        scratch_shapes=[
            pltpu.VMEM((2, planes, cols, 8, ch), x.dtype),
            pltpu.SemaphoreType.DMA((2,)),
        ],
        compiler_params=pltpu.CompilerParams(vmem_limit_bytes=8 << 20),
    )(pltpu.with_memory_space_constraint(x, pltpu.HBM))


def first_conv(xs, w1_ref, bias, c0, cols, emit):
    planes, wide, ext, ch = xs.shape[1:]
    count = wide - 2
    weights = pair_weights(w1_ref)
    for p in range(planes):
        taps = []
        for j in range(4):
            for d in range(3):
                taps.append(jnp.concatenate([xs[d, p, g + j] for g in range(0, count, 2)], axis=0))
        y = jnp.dot(jnp.concatenate(taps, axis=1), weights, preferred_element_type=F32)
        for c in range(count):
            g, o = divmod(c, 2)
            v = gelu(y[g * ext : (g + 1) * ext, o * ch : (o + 1) * ch] + bias)
            if c == 0:
                v = v * jnp.where(c0 > 0, 1.0, 0.0)
            if c == count - 1:
                v = v * jnp.where(c0 + count - 2 < cols, 1.0, 0.0)
            emit(p, c, v)


def row_masks():
    here = lax.axis_index("rows")
    above = jnp.where(here == 0, 0.0, 1.0)
    below = jnp.where(here == lax.axis_size("rows") - 1, 0.0, 1.0)
    return above, below


def column(c0, c, cols):
    at = c0 - 2 + c
    inside = jnp.logical_and(at >= 0, at < cols)
    return jnp.clip(at, 0, cols - 1), jnp.where(inside, 1.0, 0.0)


def halo_rows(one_ref, two_ref, p, at, odd):
    one = one_ref[p, at].astype(F32)
    two = two_ref[p, at].astype(F32)
    return jnp.where(odd, one, two), jnp.where(odd, two, one)


def second_half(hs, fs, w2_ref, par_ref, out_ref, trans_ref):
    planes, nc, rows, ch = fs.shape
    bias = par_ref[1:2]
    opacity = par_ref[2:3]
    lane = lax.broadcasted_iota(jnp.int32, (rows, ch), 1)
    logits = [jnp.zeros((rows, ch), F32) for _ in range(planes)]
    taps = []
    for j in range(4):
        for d in range(3):
            taps.append(
                jnp.concatenate(
                    [hs[d, p, g + j] for g in range(0, nc, 2) for p in range(planes)], axis=0
                )
            )
    y = jnp.dot(jnp.concatenate(taps, axis=1), pair_weights(w2_ref), preferred_element_type=F32)
    for c in range(nc):
        g, o = divmod(c, 2)
        for p in range(planes):
            r0 = (g * planes + p) * rows
            f = gelu(y[r0 : r0 + rows, o * ch : (o + 1) * ch] + bias)
            total = jnp.sum(f * opacity, axis=1, keepdims=True)
            logits[p] = jnp.where(lane == c, total, logits[p])
            fs[p, c] = f
    parts = []
    trans = None
    for p in range(planes):
        alpha = 1.0 / (1.0 + jnp.exp(-(logits[p] + par_ref[3 + p : 4 + p])))
        if p == 0:
            parts.append(alpha)
            trans = 1.0 - alpha
        else:
            parts.append(trans * alpha)
            trans = trans * (1.0 - alpha)
    for c in range(nc):
        color = sum(parts[p][:, c : c + 1] * fs[p, c] for p in range(planes))
        if trans_ref is None:
            out_ref[c * rows : (c + 1) * rows] = color.astype(BF16)
        else:
            out_ref[c] = color
    if trans_ref is None:
        out_ref[nc * rows :] = pack_trans(trans, nc)
    else:
        trans_ref[...] = trans


def outputs(nc, rows, ch, packed):
    if packed:
        return [jax.ShapeDtypeStruct((nc * rows + rows // folds(nc, rows, ch), ch), BF16)]
    return [jax.ShapeDtypeStruct((nc, rows, ch), F32), jax.ShapeDtypeStruct((rows, ch), F32)]


def call(kernel, args, in_specs, out_shape, scratch):
    return pl.pallas_call(
        kernel,
        out_shape=out_shape,
        in_specs=in_specs,
        out_specs=[VM] * len(out_shape),
        scratch_shapes=scratch,
        compiler_params=pltpu.CompilerParams(vmem_limit_bytes=16 << 20),
        cost_estimate=pl.CostEstimate(flops=5 * 10**9, transcendentals=0, bytes_accessed=10**6),
    )(*args)


def chunk_kernel(pick, packed, x_ref, one_ref, two_ref, w1_ref, w2_ref, par_ref, *refs):
    refs = list(refs)
    out_ref = refs.pop(0)
    trans_ref = None if packed else refs.pop(0)
    f_ref, xs, f2_ref, hs, fs = refs
    planes, cols, rows, ch = x_ref.shape
    nc = fs.shape[1]
    ext = xs.shape[3]
    c0 = pick() * nc
    odd = odd_row()
    for i in range(planes * (nc + 4)):
        p, c = divmod(i, nc + 4)
        at, keep = column(c0, c, cols)
        f = f_ref.at[i % f_ref.shape[0]]
        upper, lower = halo_rows(one_ref, two_ref, p, at, odd)
        f[16 : 16 + rows] = x_ref[p, at].astype(F32) * keep
        f[14:16] = upper * keep
        f[16 + rows : 18 + rows] = lower * keep
        for d in range(3):
            xs[d, p, c] = f[7 + d : 7 + d + ext].astype(BF16)
    above, below = row_masks()

    def emit(p, c, v):
        f2 = f2_ref.at[p, c]
        f2[...] = v
        f2[7:8] = f2[7:8] * above
        f2[8 + rows : 9 + rows] = f2[8 + rows : 9 + rows] * below
        for d in range(3):
            hs[d, p, c] = f2[7 + d : 7 + d + rows].astype(BF16)

    first_conv(xs, w1_ref, par_ref[0:1], c0, cols, emit)
    second_half(hs, fs, w2_ref, par_ref, out_ref, trans_ref)


def chunk(pick, nc, packed, x, one, two, w1, w2, par):
    planes, cols, rows, ch = x.shape
    ext = rows + 16
    scratch = [
        pltpu.VMEM((8, rows + 32, ch), F32),
        pltpu.VMEM((3, planes, nc + 4, ext, ch), BF16),
        pltpu.VMEM((planes, nc + 2, ext, ch), F32),
        pltpu.VMEM((3, planes, nc + 2, rows, ch), BF16),
        pltpu.VMEM((planes, nc, rows, ch), F32),
    ]
    kernel = functools.partial(chunk_kernel, pick, packed)
    args = (x, one, two, w1, w2, par)
    return call(kernel, args, [VM] * 6, outputs(nc, rows, ch, packed), scratch)


def head_kernel(pick, nc, x_ref, w1_hbm, w2_hbm, b1_hbm, b2_hbm, ow_hbm, ob_ref, *refs):
    hid_ref, w1_ref, w2_ref, par_ref, f_ref, xs, sem = refs
    planes, cols, rows, ch = x_ref.shape
    pairs = [
        (w1_hbm, w1_ref),
        (b1_hbm, par_ref.at[0]),
        (w2_hbm, w2_ref),
        (b2_hbm, par_ref.at[1]),
        (ow_hbm, par_ref.at[2]),
    ]
    copies = [pltpu.make_async_copy(src, dst, sem.at[i]) for i, (src, dst) in enumerate(pairs)]
    for copy in copies:
        copy.start()
    for p in range(planes):
        par_ref[3 + p : 4 + p] = jnp.full((1, ch), ob_ref[p])
    c0 = pick() * nc
    for i in range(planes * (nc + 4)):
        p, c = divmod(i, nc + 4)
        at, keep = column(c0, c, cols)
        f = f_ref.at[i % f_ref.shape[0]]
        f[16 : 16 + rows] = x_ref[p, at].astype(F32) * keep
        for d in range(3):
            xs[d, p, c] = f[15 + d : 15 + d + rows].astype(BF16)
    copies[0].wait()
    copies[1].wait()

    def emit(p, c, v):
        hid_ref[p, c, 8 : 8 + rows] = v

    first_conv(xs, w1_ref, par_ref[0:1], c0, cols, emit)
    for copy in copies[2:]:
        copy.wait()


def head(pick, nc, x, w1, w2, b1, b2, ow, ob):
    planes, cols, rows, ch = x.shape
    args = [pltpu.with_memory_space_constraint(a, pltpu.HBM) for a in (w1, w2, b1, b2, ow)]
    out_shape = [
        jax.ShapeDtypeStruct((planes, nc + 2, rows + 16, ch), F32),
        jax.ShapeDtypeStruct(w1.shape, w1.dtype),
        jax.ShapeDtypeStruct(w2.shape, w2.dtype),
        jax.ShapeDtypeStruct((3 + planes, ch), F32),
    ]
    scratch = [
        pltpu.VMEM((8, rows + 32, ch), F32),
        pltpu.VMEM((3, planes, nc + 4, rows, ch), BF16),
        pltpu.SemaphoreType.DMA((5,)),
    ]
    in_specs = [VM] + [HBM] * 5 + [pl.BlockSpec(memory_space=pltpu.SMEM)]
    kernel = functools.partial(head_kernel, pick, nc)
    return call(kernel, (x, *args, ob), in_specs, out_shape, scratch)


def tail_kernel(pick, x_ref, one_ref, two_ref, hid_ref, w1_ref, w2_ref, par_ref, out_ref, *refs):
    f_ref, xs, edge_ref, f2_ref, hs, fs = refs
    planes, cols, rows, ch = x_ref.shape
    nc = fs.shape[1]
    c0 = pick() * nc
    odd = odd_row()
    for i in range(planes * (nc + 4)):
        p, c = divmod(i, nc + 4)
        at, keep = column(c0, c, cols)
        f = f_ref.at[i % f_ref.shape[0]]
        upper, lower = halo_rows(one_ref, two_ref, p, at, odd)
        f[6:8] = upper * keep
        f[8:16] = x_ref[p, at, 0:8].astype(F32) * keep
        f[24:32] = x_ref[p, at, rows - 8 : rows].astype(F32) * keep
        f[32:34] = lower * keep
        for d in range(3):
            both = jnp.concatenate([f[3 + d : 11 + d], f[27 + d : 35 + d]], axis=0)
            xs[d, p, c] = both.astype(BF16)
    above, below = row_masks()

    def emit(p, c, v):
        edge = edge_ref.at[p, c]
        edge[...] = v
        f2 = f2_ref.at[p, c]
        f2[8 : 8 + rows] = hid_ref[p, c, 8 : 8 + rows]
        f2[7:8] = edge[3:4] * above
        f2[8:9] = edge[4:5]
        f2[7 + rows : 8 + rows] = edge[11:12]
        f2[8 + rows : 9 + rows] = edge[12:13] * below
        for d in range(3):
            hs[d, p, c] = f2[7 + d : 7 + d + rows].astype(BF16)

    first_conv(xs, w1_ref, par_ref[0:1], c0, cols, emit)
    second_half(hs, fs, w2_ref, par_ref, out_ref, None)


def tail(pick, nc, x, one, two, hid, w1, w2, par):
    planes, cols, rows, ch = x.shape
    scratch = [
        pltpu.VMEM((8, 40, ch), F32),
        pltpu.VMEM((3, planes, nc + 4, 16, ch), BF16),
        pltpu.VMEM((planes, nc + 2, 16, ch), F32),
        pltpu.VMEM((planes, nc + 2, rows + 16, ch), F32),
        pltpu.VMEM((3, planes, nc + 2, rows, ch), BF16),
        pltpu.VMEM((planes, nc, rows, ch), F32),
    ]
    args = (x, one, two, hid, w1, w2, par)
    kernel = functools.partial(tail_kernel, pick)
    return call(kernel, args, [VM] * 7, outputs(nc, rows, ch, True), scratch)[0]


def lookup(table):
    here = lax.axis_index("depth")
    value = jnp.int32(table[-1])
    for i in range(len(table) - 1):
        value = jnp.where(here == i, table[i], value)
    return value


def folds(nc, rows, ch):
    return min(rows // 16, ch // (2 * nc))


def unpack_trans(ref, nc, rows):
    ch = ref.shape[1]
    fold = folds(nc, rows, ch)
    block = ref[nc * rows :].astype(F32)
    block = block + pltpu.roll(block, ch - nc, axis=1)
    parts = [block] + [pltpu.roll(block, ch - 2 * nc * q, axis=1) for q in range(1, fold)]
    return jnp.concatenate(parts, axis=0)


def pack_trans(trans, nc):
    rows, ch = trans.shape
    fold = folds(nc, rows, ch)
    size = rows // fold
    lane = lax.broadcasted_iota(jnp.int32, trans.shape, 1)
    high = trans.astype(BF16).astype(F32)
    low = pltpu.roll(trans - high, nc, axis=1)
    both = jnp.where(lane < nc, high, jnp.where(lane < 2 * nc, low, 0.0))
    block = both[:size]
    for q in range(1, fold):
        block = block + pltpu.roll(both[q * size : (q + 1) * size], 2 * nc * q, axis=1)
    return block.astype(BF16)


def merge_kernel(own_ref, trans_ref, got_ref, out_ref):
    nc = own_ref.shape[0]
    mine = trans_ref[...]
    rows = own_ref.shape[1]
    theirs = unpack_trans(got_ref, nc, rows)
    role = lookup(MERGE)
    scale_own = jnp.where(role == 1, theirs, 1.0)
    scale_got = jnp.where(role == 2, mine, jnp.where(role == 1, 1.0, 0.0))
    for c in range(nc):
        color = scale_own[:, c : c + 1] * own_ref[c]
        at = slice(c * rows, (c + 1) * rows)
        color = color + scale_got[:, c : c + 1] * got_ref[at].astype(F32)
        out_ref[at] = color.astype(BF16)
    out_ref[nc * rows :] = pack_trans(jnp.where(role == 0, mine, mine * theirs), nc)


def merge(own, trans, got):
    return pl.pallas_call(
        merge_kernel,
        out_shape=jax.ShapeDtypeStruct(got.shape, BF16),
        in_specs=[VM] * 3,
        out_specs=VM,
        compiler_params=pltpu.CompilerParams(vmem_limit_bytes=8 << 20),
        cost_estimate=pl.CostEstimate(flops=10**9, transcendentals=0, bytes_accessed=10**6),
    )(own, trans, got)


def gather_kernel(own_ref, trans_ref, *refs):
    *got_refs, out_ref, out_trans_ref = refs
    nc, rows = own_ref.shape[:2]
    keys = [lookup(table) for table in KEYS]
    trans = [trans_ref[...]] + [unpack_trans(ref, nc, rows) for ref in got_refs]
    scale = []
    through = None
    for k in range(len(trans)):
        w = None
        for m in range(len(trans)):
            if m != k:
                term = jnp.where(keys[m] < keys[k], trans[m], 1.0)
                w = term if w is None else w * term
        scale.append(w)
        term = jnp.where(keys[k] == 9, 1.0, trans[k])
        through = term if through is None else through * term
    for c in range(nc):
        total = scale[0][:, c : c + 1] * own_ref[c]
        for k, ref in enumerate(got_refs):
            at = slice(c * rows, (c + 1) * rows)
            total = total + scale[k + 1][:, c : c + 1] * ref[at].astype(F32)
        out_ref[c] = total
    out_trans_ref[...] = through


def finish_kernel(near_ref, trans_ref, got_ref, out_hbm, out, sem):
    nc, rows = near_ref.shape[:2]
    front = lookup(LAST_IN_FRONT) == 1
    theirs = unpack_trans(got_ref, nc, rows)
    scale_near = jnp.where(front, theirs, 1.0)
    scale_got = jnp.where(front, 1.0, trans_ref[...])
    pieces = sem.shape[0]
    step = nc // pieces
    copies = []
    for i in range(pieces):
        for c in range(i * step, (i + 1) * step):
            got = got_ref[c * rows : (c + 1) * rows].astype(F32)
            out[c] = scale_near[:, c : c + 1] * near_ref[c] + scale_got[:, c : c + 1] * got
        at = pl.ds(i * step, step)
        copies.append(pltpu.make_async_copy(out.at[at], out_hbm.at[at], sem.at[i]))
        copies[-1].start()
    for copy in copies:
        copy.wait()


def combine(own, trans, got):
    color = jax.ShapeDtypeStruct(own.shape, F32)
    near, trans = pl.pallas_call(
        gather_kernel,
        out_shape=[color, jax.ShapeDtypeStruct(trans.shape, F32)],
        in_specs=[VM] * 4,
        out_specs=[VM] * 2,
        compiler_params=pltpu.CompilerParams(vmem_limit_bytes=8 << 20),
        cost_estimate=pl.CostEstimate(flops=10**9, transcendentals=0, bytes_accessed=10**6),
    )(own, trans, *got[:2])
    return pl.pallas_call(
        finish_kernel,
        out_shape=color,
        in_specs=[VM] * 3,
        out_specs=HBM,
        scratch_shapes=[pltpu.VMEM(own.shape, F32), pltpu.SemaphoreType.DMA((4,))],
        compiler_params=pltpu.CompilerParams(vmem_limit_bytes=8 << 20),
    )(near, trans, got[2])


def exchange(value, axis, mask):
    pairs = [(i, i ^ mask) for i in range(lax.axis_size(axis))]
    return lax.ppermute(value, axis, pairs)


def pick_half(array, remaining, bit_set):
    shaped = array.reshape((remaining // 2, 2, -1) + array.shape[1:])
    first_half = shaped[:, 0].reshape((-1,) + array.shape[1:])
    second_half = shaped[:, 1].reshape((-1,) + array.shape[1:])
    keep = jnp.where(bit_set, second_half, first_half)
    other = jnp.where(bit_set, first_half, second_half)
    return (keep, other)


def butterfly(color, trans):
    position = lax.axis_index("depth")
    slabs = lax.axis_size("depth")
    for level in range(slabs.bit_length() - 1):
        remaining = slabs >> level
        bit_set = jnp.right_shift(position, level) % 2 == 1
        keep_color, send_color = pick_half(color, remaining, bit_set)
        keep_trans, send_trans = pick_half(trans, remaining, bit_set)
        got_color = exchange(send_color, "depth", 2**level)
        got_trans = exchange(send_trans, "depth", 2**level)
        color = jnp.where(
            bit_set,
            got_color + got_trans[..., None] * keep_color,
            keep_color + keep_trans[..., None] * got_color,
        )
        trans = keep_trans * got_trans
    return color


def per_device(volume, conv_one, bias_one, conv_two, bias_two, opacity_weight, opacity_bias):
    planes, cols, rows, ch = volume.shape
    slabs = lax.axis_size("depth")
    size = lax.axis_size("rows")
    one, two = edges(volume)
    one = lax.ppermute(one, "rows", [(i, i ^ 1) for i in range(size)])
    inner = [(i, i + 1) for i in range(1, size - 1, 2)]
    two = lax.ppermute(two, "rows", inner + [(j, i) for i, j in inner])
    if slabs != 4:
        par = jnp.concatenate(
            [
                jnp.stack([bias_one, bias_two, opacity_weight]),
                jnp.broadcast_to(opacity_bias[:, None], (planes, ch)),
            ]
        )
        args = (16, False, volume, one, two, conv_one, conv_two, par)
        done = [chunk(functools.partial(jnp.int32, i), *args) for i in range(cols // 16)]
        color = jnp.concatenate([c for c, _ in done])
        trans = jnp.concatenate([jnp.transpose(t[:, :16]) for _, t in done])
        return butterfly(color, trans)
    nc = cols // slabs
    picks = [functools.partial(lookup, [order[slot] for order in PIECE]) for slot in range(4)]
    hid, w1, w2, par = head(
        picks[0], nc, volume, conv_one, conv_two, bias_one, bias_two, opacity_weight, opacity_bias
    )

    def piece(slot, packed):
        return chunk(picks[slot], nc, packed, volume, one, two, w1, w2, par)

    first = tail(picks[0], nc, volume, one, two, hid, w1, w2, par)
    far = lax.ppermute(first, "depth", FAR)
    near = lax.ppermute(first, "depth", NEAR)
    (second,) = piece(1, True)
    second = lax.ppermute(second, "depth", SECOND)
    third = lax.ppermute(merge(*piece(2, False), far), "depth", THIRD)
    own, trans = piece(3, False)
    return combine(own, trans, [near, second, third])


def solution(mesh):
    in_specs = (P(("grp", "depth"), None, "rows", None), P(), P(), P(), P(), P(), P("depth"))
    out_specs = P(("grp", "depth"), "rows", None)
    return jax.shard_map(
        per_device, mesh=mesh, in_specs=in_specs, out_specs=out_specs, check_vma=False
    )
```

time: 36.3 us -> 35.1 us (0.967)
  waiting for transfers between devices: 5.83 us -> 4.65 us
    ppermute x1, waiting for transfers between devices: 5.82 us -> 4.64 us  [per_device(): third = lax.ppermute(merge(*piece(2, False), far), 'depth', THIRD)]
    pallas_call x6 -> x7, Pallas kernels: 17.7 us -> 17.5 us  [the longest x5 15.8 us: call(): pl.pallas_call(kernel, out_shape=out_shape, in_specs=in_specs, out_specs=...]
  transfers between devices with their start and end apart: 6 -> 6, of which waited for: 1 -> 1; matrix products, arithmetic and copies ran while one was open for 0% -> 0% of each run, Pallas kernels for 36% -> 42%
where the time goes in v4:
time: 35.1 us; the launch traced here: 34.9 us
  Pallas kernels  19.3 us (55%)
  starting transfers between devices  10.6 us (30%)
  waiting for transfers between devices  4.65 us (13%)
    pallas_call x5, Pallas kernels, call(): pl.pallas_call(kernel, out_shape=out_shape, in_specs=in_specs, out_specs=...  15.8 us
    ppermute x1, waiting for transfers between devices, per_device(): third = lax.ppermute(merge(*piece(2, False), far), 'depth', THIRD)  4.64 us
    ppermute x1, starting transfers between devices, per_device(): two = lax.ppermute(two, 'rows', inner + [(j, i) for i, j in inner])  4.47 us
    ppermute x1, starting transfers between devices, per_device(): far = lax.ppermute(first, 'depth', FAR)  3.22 us
    ppermute x1, starting transfers between devices, per_device(): second = lax.ppermute(second, 'depth', SECOND)  1.81 us
    pallas_call x1, Pallas kernels, edges(): pl.pallas_call(edges_kernel, out_shape=(shape, shape), in_specs=[HBM], ou...  1.32 us
    pallas_call x1, Pallas kernels, combine(): pl.pallas_call(finish_kernel, out_shape=color, in_specs=[VM] * 3, out_spe...  1.12 us
  transfers between devices with their start and end apart: 6, of which 1 were waited for; matrix products, arithmetic and copies ran while one was open for 0% of the time, Pallas kernels for 42%

profile of v4, /device:TPU:1, one launch (start us, length us, event | category | flops | bytes accessed | tf_op | source)
XLA Modules:
  0.0 34.9 jit_solution(8989925564593778010)
XLA Ops:
  0.0 0.0 copy-start
  0.0 0.0 copy-start.1
  0.0 1.3 %shard_map.73 = (bf16[2,64,2,128]{3,2,1,0:T(2,128)(2,1)S(1)}, bf16[2,64,2,128]{3,2,1,0:T(2,128)(2,1)S(1)}) custom-call(bf16[2,64,64,128]{3,2,1,0:T(8,128)(2,1)} %x_ref.9), custom_call_target="tpu_custom_call" | custom-call | tf_op jit(solution)/shard_map/pallas_call | solution.py:69
  1.3 0.1 collective-permute-start
  1.5 4.5 %collective-permute-start.1 = (bf16[2,64,2,128]{3,2,1,0:T(2,128)(2,1)S(1)}, bf16[2,64,2,128]{3,2,1,0:T(2,128)(2,1)S(1)}, u32[]{:S(2)}, u32[]{:S(2)}) collective-permute-start(bf16[2,64,2,128]{3,2,1,0:T(2,128)(2,1)S(1)} %get-tuple-element.18), channel_id=1, source_target_pairs={{1,2},{2,1},{5,6},{6,5},{9,10},{10,9},{13,14},{14,13},{17,18},{18,... | collective-permute-start | bytes 196616 | tf_op jit(solution)/shard_map/ppermute | solution.py:504
  5.9 0.0 copy-done
  5.9 0.0 copy-done.1
  5.9 2.9 %shard_map.74 = (f32[2,18,80,128]{3,2,1,0:T(8,128)S(1)}, bf16[3,3,128,128]{3,2,1,0:T(8,128)(2,1)S(1)}, bf16[3,3,128,128]{3,2,1,0:T(8,128)(2,1)S(1)}, f32[5,128]{1,0:T(8,128)S(1)}) custom-call(bf16[2,64,64,128]{3,2,1,0:T(8,128)(2,1)S(1)} %copy-done, bf16[3,3,128,128]{3,2,1,0:T(8,128)(2,1)} %w1_hbm.1, bf16[3,3,128,128]{3,2,1,0:T(8,128)(2,1)} %w2_hbm.1, ...), custom_call_target="tpu_custom_call" | custom-call | flops 5000000000 | bytes 1000000 | tf_op jit(solution)/shard_map/pallas_call | solution.py:173
  8.8 0.0 collective-permute-done.one_ref
  8.8 0.0 collective-permute-done.1.two_ref
  8.8 2.4 %shard_map.76 = bf16[1040,128]{1,0:T(8,128)(2,1)S(1)} custom-call(bf16[2,64,64,128]{3,2,1,0:T(8,128)(2,1)S(1)} %copy-done, bf16[2,64,2,128]{3,2,1,0:T(2,128)(2,1)S(1)} %collective-permute-done.one_ref, bf16[2,64,2,128]{3,2,1,0:T(2,128)(2,1)S(1)} %collective-permute-done.1.two_ref, f32[2,18,80,128]{3,2,1,0:T(8,128)S(1)} %get-tuple-element.24.hid_ref, ...), custom_call_target="tpu_custom_call" | custom-call | flops 5000000000 | bytes 1000000 | tf_op jit(solution)/shard_map/pallas_call | solution.py:173
  11.2 3.2 %collective-permute-start.4 = (bf16[1040,128]{1,0:T(8,128)(2,1)S(1)}, bf16[1040,128]{1,0:T(8,128)(2,1)S(1)}, u32[]{:S(2)}, u32[]{:S(2)}) collective-permute-start(bf16[1040,128]{1,0:T(8,128)(2,1)S(1)} %shard_map.76), channel_id=1, source_target_pairs={{0,4},{12,8},{1,5},{13,9},{2,6},{14,10},{3,7},{15,11},{16,20},{28,... | collective-permute-start | bytes 798728 | tf_op jit(solution)/shard_map/ppermute | solution.py:527
  14.4 0.7 %collective-permute-start.2 = (bf16[1040,128]{1,0:T(8,128)(2,1)S(1)}, bf16[1040,128]{1,0:T(8,128)(2,1)S(1)}, u32[]{:S(2)}, u32[]{:S(2)}) collective-permute-start(bf16[1040,128]{1,0:T(8,128)(2,1)S(1)} %shard_map.76), channel_id=1, source_target_pairs={{4,8},{8,4},{5,9},{9,5},{6,10},{10,6},{7,11},{11,7},{20,24},{24,20... | collective-permute-start | bytes 798728 | tf_op jit(solution)/shard_map/ppermute | solution.py:528
  15.1 3.6 %shard_map.77 = bf16[1040,128]{1,0:T(8,128)(2,1)S(1)} custom-call(bf16[2,64,64,128]{3,2,1,0:T(8,128)(2,1)S(1)} %copy-done, bf16[2,64,2,128]{3,2,1,0:T(2,128)(2,1)S(1)} %collective-permute-done.one_ref, bf16[2,64,2,128]{3,2,1,0:T(2,128)(2,1)S(1)} %collective-permute-done.1.two_ref, bf16[3,3,128,128]{3,2,1,0:T(8,128)(2,1)S(1)} %get-tuple-element.19.w1_ref, ...), custom_call_target="tpu_custom_call" | custom-call | flops 5000000000 | bytes 1000000 | tf_op jit(solution)/shard_map/pallas_call | solution.py:173
  18.7 1.8 %collective-permute-start.3 = (bf16[1040,128]{1,0:T(8,128)(2,1)S(1)}, bf16[1040,128]{1,0:T(8,128)(2,1)S(1)}, u32[]{:S(2)}, u32[]{:S(2)}) collective-permute-start(bf16[1040,128]{1,0:T(8,128)(2,1)S(1)} %shard_map.77), channel_id=1, source_target_pairs={{0,8},{12,4},{4,0},{8,12},{1,9},{13,5},{5,1},{9,13},{2,10},{14,6},... | collective-permute-start | bytes 798728 | tf_op jit(solution)/shard_map/ppermute | solution.py:530
  20.5 3.5 %shard_map.79 = (f32[16,64,128]{2,1,0:T(8,128)S(1)}, f32[64,128]{1,0:T(8,128)S(1)}) custom-call(bf16[2,64,64,128]{3,2,1,0:T(8,128)(2,1)S(1)} %copy-done, bf16[2,64,2,128]{3,2,1,0:T(2,128)(2,1)S(1)} %collective-permute-done.one_ref, bf16[2,64,2,128]{3,2,1,0:T(2,128)(2,1)S(1)} %collective-permute-done.1.two_ref, ...), custom_call_target="tpu_custom_call" | custom-call | flops 5000000000 | bytes 1000000 | tf_op jit(solution)/shard_map/pallas_call | solution.py:173
  24.0 0.0 collective-permute-done.4.got_ref
  24.0 0.5 %shard_map.80 = bf16[1040,128]{1,0:T(8,128)(2,1)S(1)} custom-call(f32[16,64,128]{2,1,0:T(8,128)S(1)} %get-tuple-element.27.own_ref, f32[64,128]{1,0:T(8,128)S(1)} %get-tuple-element.28.trans_ref, bf16[1040,128]{1,0:T(8,128)(2,1)S(1)} %collective-permute-done.4.got_ref), custom_call_target="tpu_custom_call" | custom-call | flops 1000000000 | bytes 1000000 | tf_op jit(solution)/shard_map/pallas_call | solution.py:389
  24.5 0.4 %collective-permute-start.5 = (bf16[1040,128]{1,0:T(8,128)(2,1)S(1)}, bf16[1040,128]{1,0:T(8,128)(2,1)S(1)}, u32[]{:S(2)}, u32[]{:S(2)}) collective-permute-start(bf16[1040,128]{1,0:T(8,128)(2,1)S(1)} %shard_map.80), channel_id=1, source_target_pairs={{0,4},{12,8},{4,12},{8,0},{1,5},{13,9},{5,13},{9,1},{2,6},{14,10},... | collective-permute-start | bytes 798728 | tf_op jit(solution)/shard_map/ppermute | solution.py:531
  24.8 3.5 %shard_map.75 = (f32[16,64,128]{2,1,0:T(8,128)S(1)}, f32[64,128]{1,0:T(8,128)S(1)}) custom-call(bf16[2,64,64,128]{3,2,1,0:T(8,128)(2,1)S(1)} %copy-done, bf16[2,64,2,128]{3,2,1,0:T(2,128)(2,1)S(1)} %collective-permute-done.one_ref, bf16[2,64,2,128]{3,2,1,0:T(2,128)(2,1)S(1)} %collective-permute-done.1.two_ref, ...), custom_call_target="tpu_custom_call" | custom-call | flops 5000000000 | bytes 1000000 | tf_op jit(solution)/shard_map/pallas_call | solution.py:173
  28.3 0.0 collective-permute-done.2.refs_0_
  28.3 0.0 collective-permute-done.3.refs_1_
  28.4 0.6 %shard_map.78 = (f32[16,64,128]{2,1,0:T(8,128)S(1)}, f32[64,128]{1,0:T(8,128)S(1)}) custom-call(f32[16,64,128]{2,1,0:T(8,128)S(1)} %get-tuple-element.22.own_ref, f32[64,128]{1,0:T(8,128)S(1)} %get-tuple-element.23.trans_ref, bf16[1040,128]{1,0:T(8,128)(2,1)S(1)} %collective-permute-done.2.refs_0_, bf16[1040,128]{1,0:T(8,128)(2,1)S(1)} %collective-permute-done.3.refs_1_), custom_call_target="tpu_custom_call" | custom-call | flops 1000000000 | bytes 1000000 | tf_op jit(solution)/shard_map/pallas_call | solution.py:446
  29.0 4.6 %collective-permute-done.5.got_ref = bf16[1040,128]{1,0:T(8,128)(2,1)S(1)} collective-permute-done((bf16[1040,128]{1,0:T(8,128)(2,1)S(1)}, bf16[1040,128]{1,0:T(8,128)(2,1)S(1)}, u32[]{:S(2)}, u32[]{:S(2)}) %collective-permute-start.5) | collective-permute-done | bytes 266272 | tf_op jit(solution)/shard_map/ppermute | solution.py:531
  33.6 1.1 %shard_map.81 = f32[16,64,128]{2,1,0:T(8,128)} custom-call(f32[16,64,128]{2,1,0:T(8,128)S(1)} %get-tuple-element.25.near_ref, f32[64,128]{1,0:T(8,128)S(1)} %get-tuple-element.26.trans_ref, bf16[1040,128]{1,0:T(8,128)(2,1)S(1)} %collective-permute-done.5.got_ref), custom_call_target="tpu_custom_call" | custom-call | tf_op jit(solution)/shard_map/pallas_call | solution.py:454
Async XLA Ops:
  0.0 5.9 %copy-start = (bf16[2,64,64,128]{3,2,1,0:T(8,128)(2,1)S(1)}, bf16[2,64,64,128]{3,2,1,0:T(8,128)(2,1)}, u32[]{:S(2)}) copy-start(bf16[2,64,64,128]{3,2,1,0:T(8,128)(2,1)} %x_ref.9) | copy-start | bytes 6291460
  0.0 5.9 %copy-start.1 = (f32[2]{0:T(128)S(1)}, f32[2]{0:T(128)}, u32[]{:S(2)}) copy-start(f32[2]{0:T(128)} %ob_ref.1) | copy-start | bytes 28
  1.3 7.5 %collective-permute-start = (bf16[2,64,2,128]{3,2,1,0:T(2,128)(2,1)S(1)}, bf16[2,64,2,128]{3,2,1,0:T(2,128)(2,1)S(1)}, u32[]{:S(2)}, u32[]{:S(2)}) collective-permute-start(bf16[2,64,2,128]{3,2,1,0:T(2,128)(2,1)S(1)} %get-tuple-element.17), channel_id=1, source_target_pairs={{0,1},{1,0},{2,3},{3,2},{4,5},{5,4},{6,7},{7,6},{8,9},{9,8},{10,11... | collective-permute-start | bytes 196616 | tf_op jit(solution)/shard_map/ppermute | solution.py:502
  1.5 7.4 %collective-permute-start.1 = (bf16[2,64,2,128]{3,2,1,0:T(2,128)(2,1)S(1)}, bf16[2,64,2,128]{3,2,1,0:T(2,128)(2,1)S(1)}, u32[]{:S(2)}, u32[]{:S(2)}) collective-permute-start(bf16[2,64,2,128]{3,2,1,0:T(2,128)(2,1)S(1)} %get-tuple-element.18), channel_id=1, source_target_pairs={{1,2},{2,1},{5,6},{6,5},{9,10},{10,9},{13,14},{14,13},{17,18},{18,... | collective-permute-start | bytes 196616 | tf_op jit(solution)/shard_map/ppermute | solution.py:504
  11.2 12.8 %collective-permute-start.4 = (bf16[1040,128]{1,0:T(8,128)(2,1)S(1)}, bf16[1040,128]{1,0:T(8,128)(2,1)S(1)}, u32[]{:S(2)}, u32[]{:S(2)}) collective-permute-start(bf16[1040,128]{1,0:T(8,128)(2,1)S(1)} %shard_map.76), channel_id=1, source_target_pairs={{0,4},{12,8},{1,5},{13,9},{2,6},{14,10},{3,7},{15,11},{16,20},{28,... | collective-permute-start | bytes 798728 | tf_op jit(solution)/shard_map/ppermute | solution.py:527
  14.4 13.9 %collective-permute-start.2 = (bf16[1040,128]{1,0:T(8,128)(2,1)S(1)}, bf16[1040,128]{1,0:T(8,128)(2,1)S(1)}, u32[]{:S(2)}, u32[]{:S(2)}) collective-permute-start(bf16[1040,128]{1,0:T(8,128)(2,1)S(1)} %shard_map.76), channel_id=1, source_target_pairs={{4,8},{8,4},{5,9},{9,5},{6,10},{10,6},{7,11},{11,7},{20,24},{24,20... | collective-permute-start | bytes 798728 | tf_op jit(solution)/shard_map/ppermute | solution.py:528
  18.7 9.7 %collective-permute-start.3 = (bf16[1040,128]{1,0:T(8,128)(2,1)S(1)}, bf16[1040,128]{1,0:T(8,128)(2,1)S(1)}, u32[]{:S(2)}, u32[]{:S(2)}) collective-permute-start(bf16[1040,128]{1,0:T(8,128)(2,1)S(1)} %shard_map.77), channel_id=1, source_target_pairs={{0,8},{12,4},{4,0},{8,12},{1,9},{13,5},{5,1},{9,13},{2,10},{14,6},... | collective-permute-start | bytes 798728 | tf_op jit(solution)/shard_map/ppermute | solution.py:530
  24.5 9.1 %collective-permute-start.5 = (bf16[1040,128]{1,0:T(8,128)(2,1)S(1)}, bf16[1040,128]{1,0:T(8,128)(2,1)S(1)}, u32[]{:S(2)}, u32[]{:S(2)}) collective-permute-start(bf16[1040,128]{1,0:T(8,128)(2,1)S(1)} %shard_map.80), channel_id=1, source_target_pairs={{0,4},{12,8},{4,12},{8,0},{1,5},{13,9},{5,13},{9,1},{2,6},{14,10},... | collective-permute-start | bytes 798728 | tf_op jit(solution)/shard_map/ppermute | solution.py:531

commit v5 on v4

--- a/solution.py
+++ b/solution.py
@@ -43,24 +43,19 @@
     return lax.rem(lax.axis_index("rows"), 2) == 1
 
 
-def edges_kernel(x_hbm, one_ref, two_ref, buf, sem):
+def edges_kernel(x_hbm, one_ref, two_ref, sem):
     rows = x_hbm.shape[2]
-    a = pltpu.make_async_copy(x_hbm.at[:, :, pl.ds(0, 8)], buf.at[0], sem.at[0])
-    b = pltpu.make_async_copy(x_hbm.at[:, :, pl.ds(rows - 8, 8)], buf.at[1], sem.at[1])
-    a.start()
-    b.start()
-    a.wait()
-    b.wait()
-
-    @pl.when(odd_row())
-    def _():
-        one_ref[...] = buf[0, :, :, 0:2]
-        two_ref[...] = buf[1, :, :, 6:8]
-
-    @pl.when(jnp.logical_not(odd_row()))
-    def _():
-        one_ref[...] = buf[1, :, :, 6:8]
-        two_ref[...] = buf[0, :, :, 0:2]
+
+    def send(near, far):
+        a = pltpu.make_async_copy(x_hbm.at[:, :, pl.ds(near, 2)], one_ref, sem.at[0])
+        b = pltpu.make_async_copy(x_hbm.at[:, :, pl.ds(far, 2)], two_ref, sem.at[1])
+        a.start()
+        b.start()
+        a.wait()
+        b.wait()
+
+    pl.when(odd_row())(functools.partial(send, 0, rows - 2))
+    pl.when(jnp.logical_not(odd_row()))(functools.partial(send, rows - 2, 0))
 
 
 def edges(x):
@@ -71,26 +66,24 @@
         out_shape=(shape, shape),
         in_specs=[HBM],
         out_specs=(VM, VM),
-        scratch_shapes=[
-            pltpu.VMEM((2, planes, cols, 8, ch), x.dtype),
-            pltpu.SemaphoreType.DMA((2,)),
-        ],
+        scratch_shapes=[pltpu.SemaphoreType.DMA((2,))],
         compiler_params=pltpu.CompilerParams(vmem_limit_bytes=8 << 20),
     )(pltpu.with_memory_space_constraint(x, pltpu.HBM))
 
 
 def first_conv(xs, w1_ref, bias, c0, cols, emit):
-    planes, wide, ext, ch = xs.shape[1:]
+    blocks, wide, ext, ch = xs.shape[1:]
     count = wide - 2
     weights = pair_weights(w1_ref)
-    for p in range(planes):
+    cuts = [count // 2 * i // 2 for i in range(2 + 1)]
+    for p, lo, hi in [(p, a, b) for p in range(blocks) for a, b in zip(cuts, cuts[1:])]:
         taps = []
         for j in range(4):
             for d in range(3):
-                taps.append(jnp.concatenate([xs[d, p, g + j] for g in range(0, count, 2)], axis=0))
+                taps.append(jnp.concatenate([xs[d, p, 2 * g + j] for g in range(lo, hi)], axis=0))
         y = jnp.dot(jnp.concatenate(taps, axis=1), weights, preferred_element_type=F32)
-        for c in range(count):
-            g, o = divmod(c, 2)
+        for c in range(2 * lo, 2 * hi):
+            g, o = divmod(c - 2 * lo, 2)
             v = gelu(y[g * ext : (g + 1) * ext, o * ch : (o + 1) * ch] + bias)
             if c == 0:
                 v = v * jnp.where(c0 > 0, 1.0, 0.0)
@@ -123,44 +116,47 @@
     bias = par_ref[1:2]
     opacity = par_ref[2:3]
     lane = lax.broadcasted_iota(jnp.int32, (rows, ch), 1)
-    logits = [jnp.zeros((rows, ch), F32) for _ in range(planes)]
-    taps = []
-    for j in range(4):
-        for d in range(3):
-            taps.append(
-                jnp.concatenate(
-                    [hs[d, p, g + j] for g in range(0, nc, 2) for p in range(planes)], axis=0
-                )
-            )
-    y = jnp.dot(jnp.concatenate(taps, axis=1), pair_weights(w2_ref), preferred_element_type=F32)
-    for c in range(nc):
-        g, o = divmod(c, 2)
+    weights = pair_weights(w2_ref)
+    through = jnp.zeros((rows, ch), F32)
+    cuts = [nc // 2 * i // 4 for i in range(4 + 1)]
+    for lo, hi in zip(cuts, cuts[1:]):
+        logits = [jnp.zeros((rows, ch), F32) for _ in range(planes)]
+        taps = []
+        for j in range(4):
+            for d in range(3):
+                cells = [hs[d, p, 2 * g + j] for g in range(lo, hi) for p in range(planes)]
+                taps.append(jnp.concatenate(cells, axis=0))
+        y = jnp.dot(jnp.concatenate(taps, axis=1), weights, preferred_element_type=F32)
+        for c in range(2 * lo, 2 * hi):
+            g, o = divmod(c - 2 * lo, 2)
+            for p in range(planes):
+                r0 = (g * planes + p) * rows
+                f = gelu(y[r0 : r0 + rows, o * ch : (o + 1) * ch] + bias)
+                total = jnp.sum(f * opacity, axis=1, keepdims=True)
+                logits[p] = jnp.where(lane == c, total, logits[p])
+                fs[p, c] = f
+        parts = []
+        trans = None
         for p in range(planes):
-            r0 = (g * planes + p) * rows
-            f = gelu(y[r0 : r0 + rows, o * ch : (o + 1) * ch] + bias)
-            total = jnp.sum(f * opacity, axis=1, keepdims=True)
-            logits[p] = jnp.where(lane == c, total, logits[p])
-            fs[p, c] = f
-    parts = []
-    trans = None
-    for p in range(planes):
-        alpha = 1.0 / (1.0 + jnp.exp(-(logits[p] + par_ref[3 + p : 4 + p])))
-        if p == 0:
-            parts.append(alpha)
-            trans = 1.0 - alpha
-        else:
-            parts.append(trans * alpha)
-            trans = trans * (1.0 - alpha)
-    for c in range(nc):
-        color = sum(parts[p][:, c : c + 1] * fs[p, c] for p in range(planes))
-        if trans_ref is None:
-            out_ref[c * rows : (c + 1) * rows] = color.astype(BF16)
-        else:
-            out_ref[c] = color
+            alpha = 1.0 / (1.0 + jnp.exp(-(logits[p] + par_ref[3 + p : 4 + p])))
+            if p == 0:
+                parts.append(alpha)
+                trans = 1.0 - alpha
+            else:
+                parts.append(trans * alpha)
+                trans = trans * (1.0 - alpha)
+        for c in range(2 * lo, 2 * hi):
+            color = sum(parts[p][:, c : c + 1] * fs[p, c] for p in range(planes))
+            if trans_ref is None:
+                out_ref[c * rows : (c + 1) * rows] = color.astype(BF16)
+            else:
+                out_ref[c] = color
+        mine = jnp.logical_and(lane >= 2 * lo, lane < 2 * hi)
+        through = jnp.where(mine, trans, through)
     if trans_ref is None:
-        out_ref[nc * rows :] = pack_trans(trans, nc)
+        out_ref[nc * rows :] = pack_trans(through, nc)
     else:
-        trans_ref[...] = trans
+        trans_ref[...] = through
 
 
 def outputs(nc, rows, ch, packed):
@@ -189,27 +185,31 @@
     planes, cols, rows, ch = x_ref.shape
     nc = fs.shape[1]
     ext = xs.shape[3]
+    gap = rows + 8
     c0 = pick() * nc
     odd = odd_row()
-    for i in range(planes * (nc + 4)):
-        p, c = divmod(i, nc + 4)
+    for c in range(nc + 4):
         at, keep = column(c0, c, cols)
-        f = f_ref.at[i % f_ref.shape[0]]
-        upper, lower = halo_rows(one_ref, two_ref, p, at, odd)
-        f[16 : 16 + rows] = x_ref[p, at].astype(F32) * keep
-        f[14:16] = upper * keep
-        f[16 + rows : 18 + rows] = lower * keep
+        f = f_ref.at[c % f_ref.shape[0]]
+        for p in range(planes):
+            upper, lower = halo_rows(one_ref, two_ref, p, at, odd)
+            r0 = 8 + p * gap
+            f[r0 : r0 + rows] = x_ref[p, at].astype(F32) * keep
+            f[r0 - 2 : r0] = upper * keep
+            f[r0 + rows : r0 + rows + 2] = lower * keep
         for d in range(3):
-            xs[d, p, c] = f[7 + d : 7 + d + ext].astype(BF16)
+            xs[d, 0, c] = f[6 + d : 6 + d + ext].astype(BF16)
     above, below = row_masks()
 
-    def emit(p, c, v):
-        f2 = f2_ref.at[p, c]
+    def emit(_, c, v):
+        f2 = f2_ref.at[c]
         f2[...] = v
-        f2[7:8] = f2[7:8] * above
-        f2[8 + rows : 9 + rows] = f2[8 + rows : 9 + rows] * below
-        for d in range(3):
-            hs[d, p, c] = f2[7 + d : 7 + d + rows].astype(BF16)
+        for p in range(planes):
+            r0 = p * gap
+            f2[r0 : r0 + 1] = f2[r0 : r0 + 1] * above
+            f2[r0 + rows + 1 : r0 + rows + 2] = f2[r0 + rows + 1 : r0 + rows + 2] * below
+            for d in range(3):
+                hs[d, p, c] = f2[r0 + d : r0 + d + rows].astype(BF16)
 
     first_conv(xs, w1_ref, par_ref[0:1], c0, cols, emit)
     second_half(hs, fs, w2_ref, par_ref, out_ref, trans_ref)
@@ -217,11 +217,11 @@
 
 def chunk(pick, nc, packed, x, one, two, w1, w2, par):
     planes, cols, rows, ch = x.shape
-    ext = rows + 16
+    ext = -(-((planes - 1) * (rows + 8) + rows + 2) // 16) * 16
     scratch = [
-        pltpu.VMEM((8, rows + 32, ch), F32),
-        pltpu.VMEM((3, planes, nc + 4, ext, ch), BF16),
-        pltpu.VMEM((planes, nc + 2, ext, ch), F32),
+        pltpu.VMEM((4, ext + 16, ch), F32),
+        pltpu.VMEM((3, 1, nc + 4, ext, ch), BF16),
+        pltpu.VMEM((nc + 2, ext, ch), F32),
         pltpu.VMEM((3, planes, nc + 2, rows, ch), BF16),
         pltpu.VMEM((planes, nc, rows, ch), F32),
     ]

time: 35.1 us -> 34.4 us (0.980)
  Pallas kernels: 19.3 us -> 18.1 us
  waiting for transfers between devices: 4.65 us -> 5.14 us
    pallas_call x5, Pallas kernels: 15.8 us -> 14.9 us  [call(): pl.pallas_call(kernel, out_shape=out_shape, in_specs=in_specs, out_specs=...]
    ppermute x1, waiting for transfers between devices: 4.64 us -> 5.13 us  [per_device(): third = lax.ppermute(merge(*piece(2, False), far), 'depth', THIRD)]
  transfers between devices with their start and end apart: 6 -> 6, of which waited for: 1 -> 1; matrix products, arithmetic and copies ran while one was open for 0% -> 0% of each run, Pallas kernels for 42% -> 40%
where the time goes in v5:
time: 34.4 us; the launch traced here: 34.2 us
  Pallas kernels  18.1 us (53%)
  starting transfers between devices  10.7 us (31%)
  waiting for transfers between devices  5.14 us (15%)
    pallas_call x5, Pallas kernels, call(): pl.pallas_call(kernel, out_shape=out_shape, in_specs=in_specs, out_specs=...  14.9 us
    ppermute x1, waiting for transfers between devices, per_device(): third = lax.ppermute(merge(*piece(2, False), far), 'depth', THIRD)  5.13 us
    ppermute x1, starting transfers between devices, per_device(): two = lax.ppermute(two, 'rows', inner + [(j, i) for i, j in inner])  4.47 us
    ppermute x1, starting transfers between devices, per_device(): far = lax.ppermute(first, 'depth', FAR)  3.21 us
    ppermute x1, starting transfers between devices, per_device(): second = lax.ppermute(second, 'depth', SECOND)  1.82 us
    pallas_call x1, Pallas kernels, combine(): pl.pallas_call(finish_kernel, out_shape=color, in_specs=[VM] * 3, out_spe...  1.12 us
    pallas_call x1, Pallas kernels, edges(): pl.pallas_call(edges_kernel, out_shape=(shape, shape), in_specs=[HBM], ou...  1.04 us
  transfers between devices with their start and end apart: 6, of which 1 were waited for; matrix products, arithmetic and copies ran while one was open for 0% of the time, Pallas kernels for 40%

profile of v5, /device:TPU:1, one launch (start us, length us, event | category | flops | bytes accessed | tf_op | source)
XLA Modules:
  0.0 34.2 jit_solution(7032415066645281708)
XLA Ops:
  0.0 0.0 copy-start
  0.0 0.0 copy-start.1
  0.0 1.0 %shard_map.73 = (bf16[2,64,2,128]{3,2,1,0:T(2,128)(2,1)S(1)}, bf16[2,64,2,128]{3,2,1,0:T(2,128)(2,1)S(1)}) custom-call(bf16[2,64,64,128]{3,2,1,0:T(8,128)(2,1)} %x_ref.9), custom_call_target="tpu_custom_call" | custom-call | tf_op jit(solution)/shard_map/pallas_call | solution.py:64
  1.1 0.1 collective-permute-start
  1.2 4.5 %collective-permute-start.1 = (bf16[2,64,2,128]{3,2,1,0:T(2,128)(2,1)S(1)}, bf16[2,64,2,128]{3,2,1,0:T(2,128)(2,1)S(1)}, u32[]{:S(2)}, u32[]{:S(2)}) collective-permute-start(bf16[2,64,2,128]{3,2,1,0:T(2,128)(2,1)S(1)} %get-tuple-element.18), channel_id=1, source_target_pairs={{1,2},{2,1},{5,6},{6,5},{9,10},{10,9},{13,14},{14,13},{17,18},{18,... | collective-permute-start | bytes 196616 | tf_op jit(solution)/shard_map/ppermute | solution.py:504
  5.7 0.0 copy-done
  5.7 0.0 copy-done.1
  5.7 2.7 %shard_map.74 = (f32[2,18,80,128]{3,2,1,0:T(8,128)S(1)}, bf16[3,3,128,128]{3,2,1,0:T(8,128)(2,1)S(1)}, bf16[3,3,128,128]{3,2,1,0:T(8,128)(2,1)S(1)}, f32[5,128]{1,0:T(8,128)S(1)}) custom-call(bf16[2,64,64,128]{3,2,1,0:T(8,128)(2,1)S(1)} %copy-done, bf16[3,3,128,128]{3,2,1,0:T(8,128)(2,1)} %w1_hbm.1, bf16[3,3,128,128]{3,2,1,0:T(8,128)(2,1)} %w2_hbm.1, ...), custom_call_target="tpu_custom_call" | custom-call | flops 5000000000 | bytes 1000000 | tf_op jit(solution)/shard_map/pallas_call | solution.py:169
  8.4 0.0 collective-permute-done.one_ref
  8.4 0.0 collective-permute-done.1.two_ref
  8.4 2.3 %shard_map.76 = bf16[1040,128]{1,0:T(8,128)(2,1)S(1)} custom-call(bf16[2,64,64,128]{3,2,1,0:T(8,128)(2,1)S(1)} %copy-done, bf16[2,64,2,128]{3,2,1,0:T(2,128)(2,1)S(1)} %collective-permute-done.one_ref, bf16[2,64,2,128]{3,2,1,0:T(2,128)(2,1)S(1)} %collective-permute-done.1.two_ref, f32[2,18,80,128]{3,2,1,0:T(8,128)S(1)} %get-tuple-element.24.hid_ref, ...), custom_call_target="tpu_custom_call" | custom-call | flops 5000000000 | bytes 1000000 | tf_op jit(solution)/shard_map/pallas_call | solution.py:169
  10.7 3.2 %collective-permute-start.4 = (bf16[1040,128]{1,0:T(8,128)(2,1)S(1)}, bf16[1040,128]{1,0:T(8,128)(2,1)S(1)}, u32[]{:S(2)}, u32[]{:S(2)}) collective-permute-start(bf16[1040,128]{1,0:T(8,128)(2,1)S(1)} %shard_map.76), channel_id=1, source_target_pairs={{0,4},{12,8},{1,5},{13,9},{2,6},{14,10},{3,7},{15,11},{16,20},{28,... | collective-permute-start | bytes 798728 | tf_op jit(solution)/shard_map/ppermute | solution.py:527
  14.0 0.7 %collective-permute-start.2 = (bf16[1040,128]{1,0:T(8,128)(2,1)S(1)}, bf16[1040,128]{1,0:T(8,128)(2,1)S(1)}, u32[]{:S(2)}, u32[]{:S(2)}) collective-permute-start(bf16[1040,128]{1,0:T(8,128)(2,1)S(1)} %shard_map.76), channel_id=1, source_target_pairs={{4,8},{8,4},{5,9},{9,5},{6,10},{10,6},{7,11},{11,7},{20,24},{24,20... | collective-permute-start | bytes 798728 | tf_op jit(solution)/shard_map/ppermute | solution.py:528
  14.6 3.3 %shard_map.77 = bf16[1040,128]{1,0:T(8,128)(2,1)S(1)} custom-call(bf16[2,64,64,128]{3,2,1,0:T(8,128)(2,1)S(1)} %copy-done, bf16[2,64,2,128]{3,2,1,0:T(2,128)(2,1)S(1)} %collective-permute-done.one_ref, bf16[2,64,2,128]{3,2,1,0:T(2,128)(2,1)S(1)} %collective-permute-done.1.two_ref, bf16[3,3,128,128]{3,2,1,0:T(8,128)(2,1)S(1)} %get-tuple-element.19.w1_ref, ...), custom_call_target="tpu_custom_call" | custom-call | flops 5000000000 | bytes 1000000 | tf_op jit(solution)/shard_map/pallas_call | solution.py:169
  18.0 1.8 %collective-permute-start.3 = (bf16[1040,128]{1,0:T(8,128)(2,1)S(1)}, bf16[1040,128]{1,0:T(8,128)(2,1)S(1)}, u32[]{:S(2)}, u32[]{:S(2)}) collective-permute-start(bf16[1040,128]{1,0:T(8,128)(2,1)S(1)} %shard_map.77), channel_id=1, source_target_pairs={{0,8},{12,4},{4,0},{8,12},{1,9},{13,5},{5,1},{9,13},{2,10},{14,6},... | collective-permute-start | bytes 798728 | tf_op jit(solution)/shard_map/ppermute | solution.py:530
  19.8 3.3 %shard_map.79 = (f32[16,64,128]{2,1,0:T(8,128)S(1)}, f32[64,128]{1,0:T(8,128)S(1)}) custom-call(bf16[2,64,64,128]{3,2,1,0:T(8,128)(2,1)S(1)} %copy-done, bf16[2,64,2,128]{3,2,1,0:T(2,128)(2,1)S(1)} %collective-permute-done.one_ref, bf16[2,64,2,128]{3,2,1,0:T(2,128)(2,1)S(1)} %collective-permute-done.1.two_ref, ...), custom_call_target="tpu_custom_call" | custom-call | flops 5000000000 | bytes 1000000 | tf_op jit(solution)/shard_map/pallas_call | solution.py:169
  23.0 0.0 collective-permute-done.4.got_ref
  23.1 0.5 %shard_map.80 = bf16[1040,128]{1,0:T(8,128)(2,1)S(1)} custom-call(f32[16,64,128]{2,1,0:T(8,128)S(1)} %get-tuple-element.27.own_ref, f32[64,128]{1,0:T(8,128)S(1)} %get-tuple-element.28.trans_ref, bf16[1040,128]{1,0:T(8,128)(2,1)S(1)} %collective-permute-done.4.got_ref), custom_call_target="tpu_custom_call" | custom-call | flops 1000000000 | bytes 1000000 | tf_op jit(solution)/shard_map/pallas_call | solution.py:389
  23.5 0.4 %collective-permute-start.5 = (bf16[1040,128]{1,0:T(8,128)(2,1)S(1)}, bf16[1040,128]{1,0:T(8,128)(2,1)S(1)}, u32[]{:S(2)}, u32[]{:S(2)}) collective-permute-start(bf16[1040,128]{1,0:T(8,128)(2,1)S(1)} %shard_map.80), channel_id=1, source_target_pairs={{0,4},{12,8},{4,12},{8,0},{1,5},{13,9},{5,13},{9,1},{2,6},{14,10},... | collective-permute-start | bytes 798728 | tf_op jit(solution)/shard_map/ppermute | solution.py:531
  23.9 3.3 %shard_map.75 = (f32[16,64,128]{2,1,0:T(8,128)S(1)}, f32[64,128]{1,0:T(8,128)S(1)}) custom-call(bf16[2,64,64,128]{3,2,1,0:T(8,128)(2,1)S(1)} %copy-done, bf16[2,64,2,128]{3,2,1,0:T(2,128)(2,1)S(1)} %collective-permute-done.one_ref, bf16[2,64,2,128]{3,2,1,0:T(2,128)(2,1)S(1)} %collective-permute-done.1.two_ref, ...), custom_call_target="tpu_custom_call" | custom-call | flops 5000000000 | bytes 1000000 | tf_op jit(solution)/shard_map/pallas_call | solution.py:169
  27.2 0.0 collective-permute-done.2.refs_0_
  27.2 0.0 collective-permute-done.3.refs_1_
  27.2 0.6 %shard_map.78 = (f32[16,64,128]{2,1,0:T(8,128)S(1)}, f32[64,128]{1,0:T(8,128)S(1)}) custom-call(f32[16,64,128]{2,1,0:T(8,128)S(1)} %get-tuple-element.22.own_ref, f32[64,128]{1,0:T(8,128)S(1)} %get-tuple-element.23.trans_ref, bf16[1040,128]{1,0:T(8,128)(2,1)S(1)} %collective-permute-done.2.refs_0_, bf16[1040,128]{1,0:T(8,128)(2,1)S(1)} %collective-permute-done.3.refs_1_), custom_call_target="tpu_custom_call" | custom-call | flops 1000000000 | bytes 1000000 | tf_op jit(solution)/shard_map/pallas_call | solution.py:446
  27.8 5.1 %collective-permute-done.5.got_ref = bf16[1040,128]{1,0:T(8,128)(2,1)S(1)} collective-permute-done((bf16[1040,128]{1,0:T(8,128)(2,1)S(1)}, bf16[1040,128]{1,0:T(8,128)(2,1)S(1)}, u32[]{:S(2)}, u32[]{:S(2)}) %collective-permute-start.5) | collective-permute-done | bytes 266272 | tf_op jit(solution)/shard_map/ppermute | solution.py:531
  32.9 1.1 %shard_map.81 = f32[16,64,128]{2,1,0:T(8,128)} custom-call(f32[16,64,128]{2,1,0:T(8,128)S(1)} %get-tuple-element.25.near_ref, f32[64,128]{1,0:T(8,128)S(1)} %get-tuple-element.26.trans_ref, bf16[1040,128]{1,0:T(8,128)(2,1)S(1)} %collective-permute-done.5.got_ref), custom_call_target="tpu_custom_call" | custom-call | tf_op jit(solution)/shard_map/pallas_call | solution.py:454
Async XLA Ops:
  0.0 5.7 %copy-start = (bf16[2,64,64,128]{3,2,1,0:T(8,128)(2,1)S(1)}, bf16[2,64,64,128]{3,2,1,0:T(8,128)(2,1)}, u32[]{:S(2)}) copy-start(bf16[2,64,64,128]{3,2,1,0:T(8,128)(2,1)} %x_ref.9) | copy-start | bytes 6291460
  0.0 5.7 %copy-start.1 = (f32[2]{0:T(128)S(1)}, f32[2]{0:T(128)}, u32[]{:S(2)}) copy-start(f32[2]{0:T(128)} %ob_ref.1) | copy-start | bytes 28
  1.1 7.3 %collective-permute-start = (bf16[2,64,2,128]{3,2,1,0:T(2,128)(2,1)S(1)}, bf16[2,64,2,128]{3,2,1,0:T(2,128)(2,1)S(1)}, u32[]{:S(2)}, u32[]{:S(2)}) collective-permute-start(bf16[2,64,2,128]{3,2,1,0:T(2,128)(2,1)S(1)} %get-tuple-element.17), channel_id=1, source_target_pairs={{0,1},{1,0},{2,3},{3,2},{4,5},{5,4},{6,7},{7,6},{8,9},{9,8},{10,11... | collective-permute-start | bytes 196616 | tf_op jit(solution)/shard_map/ppermute | solution.py:502
  1.2 7.2 %collective-permute-start.1 = (bf16[2,64,2,128]{3,2,1,0:T(2,128)(2,1)S(1)}, bf16[2,64,2,128]{3,2,1,0:T(2,128)(2,1)S(1)}, u32[]{:S(2)}, u32[]{:S(2)}) collective-permute-start(bf16[2,64,2,128]{3,2,1,0:T(2,128)(2,1)S(1)} %get-tuple-element.18), channel_id=1, source_target_pairs={{1,2},{2,1},{5,6},{6,5},{9,10},{10,9},{13,14},{14,13},{17,18},{18,... | collective-permute-start | bytes 196616 | tf_op jit(solution)/shard_map/ppermute | solution.py:504
  10.7 12.3 %collective-permute-start.4 = (bf16[1040,128]{1,0:T(8,128)(2,1)S(1)}, bf16[1040,128]{1,0:T(8,128)(2,1)S(1)}, u32[]{:S(2)}, u32[]{:S(2)}) collective-permute-start(bf16[1040,128]{1,0:T(8,128)(2,1)S(1)} %shard_map.76), channel_id=1, source_target_pairs={{0,4},{12,8},{1,5},{13,9},{2,6},{14,10},{3,7},{15,11},{16,20},{28,... | collective-permute-start | bytes 798728 | tf_op jit(solution)/shard_map/ppermute | solution.py:527
  14.0 13.2 %collective-permute-start.2 = (bf16[1040,128]{1,0:T(8,128)(2,1)S(1)}, bf16[1040,128]{1,0:T(8,128)(2,1)S(1)}, u32[]{:S(2)}, u32[]{:S(2)}) collective-permute-start(bf16[1040,128]{1,0:T(8,128)(2,1)S(1)} %shard_map.76), channel_id=1, source_target_pairs={{4,8},{8,4},{5,9},{9,5},{6,10},{10,6},{7,11},{11,7},{20,24},{24,20... | collective-permute-start | bytes 798728 | tf_op jit(solution)/shard_map/ppermute | solution.py:528
  18.0 9.2 %collective-permute-start.3 = (bf16[1040,128]{1,0:T(8,128)(2,1)S(1)}, bf16[1040,128]{1,0:T(8,128)(2,1)S(1)}, u32[]{:S(2)}, u32[]{:S(2)}) collective-permute-start(bf16[1040,128]{1,0:T(8,128)(2,1)S(1)} %shard_map.77), channel_id=1, source_target_pairs={{0,8},{12,4},{4,0},{8,12},{1,9},{13,5},{5,1},{9,13},{2,10},{14,6},... | collective-permute-start | bytes 798728 | tf_op jit(solution)/shard_map/ppermute | solution.py:530
  23.5 9.4 %collective-permute-start.5 = (bf16[1040,128]{1,0:T(8,128)(2,1)S(1)}, bf16[1040,128]{1,0:T(8,128)(2,1)S(1)}, u32[]{:S(2)}, u32[]{:S(2)}) collective-permute-start(bf16[1040,128]{1,0:T(8,128)(2,1)S(1)} %shard_map.80), channel_id=1, source_target_pairs={{0,4},{12,8},{4,12},{8,0},{1,5},{13,9},{5,13},{9,1},{2,6},{14,10},... | collective-permute-start | bytes 798728 | tf_op jit(solution)/shard_map/ppermute | solution.py:531

commit v6 on v5

--- a/solution.py
+++ b/solution.py
@@ -43,32 +43,43 @@
     return lax.rem(lax.axis_index("rows"), 2) == 1
 
 
-def edges_kernel(x_hbm, one_ref, two_ref, sem):
+def edges_kernel(x_hbm, w_hbm, b_hbm, one_ref, two_ref, w_ref, b_ref, sem):
     rows = x_hbm.shape[2]
+    weights = pltpu.make_async_copy(w_hbm, w_ref, sem.at[2])
+    bias = pltpu.make_async_copy(b_hbm, b_ref.at[0], sem.at[3])
 
     def send(near, far):
         a = pltpu.make_async_copy(x_hbm.at[:, :, pl.ds(near, 2)], one_ref, sem.at[0])
         b = pltpu.make_async_copy(x_hbm.at[:, :, pl.ds(far, 2)], two_ref, sem.at[1])
         a.start()
         b.start()
+        weights.start()
+        bias.start()
         a.wait()
         b.wait()
+        weights.wait()
+        bias.wait()
 
     pl.when(odd_row())(functools.partial(send, 0, rows - 2))
     pl.when(jnp.logical_not(odd_row()))(functools.partial(send, rows - 2, 0))
 
 
-def edges(x):
+def edges(x, w, b):
     planes, cols, rows, ch = x.shape
     shape = jax.ShapeDtypeStruct((planes, cols, 2, ch), x.dtype)
     return pl.pallas_call(
         edges_kernel,
-        out_shape=(shape, shape),
-        in_specs=[HBM],
-        out_specs=(VM, VM),
-        scratch_shapes=[pltpu.SemaphoreType.DMA((2,))],
+        out_shape=(
+            shape,
+            shape,
+            jax.ShapeDtypeStruct(w.shape, w.dtype),
+            jax.ShapeDtypeStruct((1, ch), F32),
+        ),
+        in_specs=[HBM] * 3,
+        out_specs=(VM,) * 4,
+        scratch_shapes=[pltpu.SemaphoreType.DMA((4,))],
         compiler_params=pltpu.CompilerParams(vmem_limit_bytes=8 << 20),
-    )(pltpu.with_memory_space_constraint(x, pltpu.HBM))
+    )(*[pltpu.with_memory_space_constraint(a, pltpu.HBM) for a in (x, w, b)])
 
 
 def first_conv(xs, w1_ref, bias, c0, cols, emit):
@@ -230,12 +241,10 @@
     return call(kernel, args, [VM] * 6, outputs(nc, rows, ch, packed), scratch)
 
 
-def head_kernel(pick, nc, x_ref, w1_hbm, w2_hbm, b1_hbm, b2_hbm, ow_hbm, ob_ref, *refs):
-    hid_ref, w1_ref, w2_ref, par_ref, f_ref, xs, sem = refs
+def head_kernel(pick, nc, x_ref, w1_ref, b1_ref, w2_hbm, b2_hbm, ow_hbm, ob_ref, *refs):
+    hid_ref, w2_ref, par_ref, f_ref, xs, sem = refs
     planes, cols, rows, ch = x_ref.shape
     pairs = [
-        (w1_hbm, w1_ref),
-        (b1_hbm, par_ref.at[0]),
         (w2_hbm, w2_ref),
         (b2_hbm, par_ref.at[1]),
         (ow_hbm, par_ref.at[2]),
@@ -243,8 +252,7 @@
     copies = [pltpu.make_async_copy(src, dst, sem.at[i]) for i, (src, dst) in enumerate(pairs)]
     for copy in copies:
         copy.start()
-    for p in range(planes):
-        par_ref[3 + p : 4 + p] = jnp.full((1, ch), ob_ref[p])
+    par_ref[3:] = ob_ref[...]
     c0 = pick() * nc
     for i in range(planes * (nc + 4)):
         p, c = divmod(i, nc + 4)
@@ -253,34 +261,32 @@
         f[16 : 16 + rows] = x_ref[p, at].astype(F32) * keep
         for d in range(3):
             xs[d, p, c] = f[15 + d : 15 + d + rows].astype(BF16)
-    copies[0].wait()
-    copies[1].wait()
+    par_ref[0:1] = b1_ref[...]
 
     def emit(p, c, v):
         hid_ref[p, c, 8 : 8 + rows] = v
 
-    first_conv(xs, w1_ref, par_ref[0:1], c0, cols, emit)
-    for copy in copies[2:]:
+    first_conv(xs, w1_ref, b1_ref[...], c0, cols, emit)
+    for copy in copies:
         copy.wait()
 
 
 def head(pick, nc, x, w1, w2, b1, b2, ow, ob):
     planes, cols, rows, ch = x.shape
-    args = [pltpu.with_memory_space_constraint(a, pltpu.HBM) for a in (w1, w2, b1, b2, ow)]
+    args = [pltpu.with_memory_space_constraint(a, pltpu.HBM) for a in (w2, b2, ow)]
     out_shape = [
         jax.ShapeDtypeStruct((planes, nc + 2, rows + 16, ch), F32),
-        jax.ShapeDtypeStruct(w1.shape, w1.dtype),
         jax.ShapeDtypeStruct(w2.shape, w2.dtype),
         jax.ShapeDtypeStruct((3 + planes, ch), F32),
     ]
     scratch = [
         pltpu.VMEM((8, rows + 32, ch), F32),
         pltpu.VMEM((3, planes, nc + 4, rows, ch), BF16),
-        pltpu.SemaphoreType.DMA((5,)),
+        pltpu.SemaphoreType.DMA((3,)),
     ]
-    in_specs = [VM] + [HBM] * 5 + [pl.BlockSpec(memory_space=pltpu.SMEM)]
+    in_specs = [VM] * 3 + [HBM] * 3 + [VM]
     kernel = functools.partial(head_kernel, pick, nc)
-    return call(kernel, (x, *args, ob), in_specs, out_shape, scratch)
+    return call(kernel, (x, w1, b1, *args, ob), in_specs, out_shape, scratch)
 
 
 def tail_kernel(pick, x_ref, one_ref, two_ref, hid_ref, w1_ref, w2_ref, par_ref, out_ref, *refs):
@@ -498,10 +504,10 @@
     planes, cols, rows, ch = volume.shape
     slabs = lax.axis_size("depth")
     size = lax.axis_size("rows")
-    one, two = edges(volume)
-    one = lax.ppermute(one, "rows", [(i, i ^ 1) for i in range(size)])
+    one, two, w1, b1 = edges(volume, conv_one, bias_one)
     inner = [(i, i + 1) for i in range(1, size - 1, 2)]
     two = lax.ppermute(two, "rows", inner + [(j, i) for i, j in inner])
+    one = lax.ppermute(one, "rows", [(i, i ^ 1) for i in range(size)])
     if slabs != 4:
         par = jnp.concatenate(
             [
@@ -509,15 +515,16 @@
                 jnp.broadcast_to(opacity_bias[:, None], (planes, ch)),
             ]
         )
-        args = (16, False, volume, one, two, conv_one, conv_two, par)
+        args = (16, False, volume, one, two, w1, conv_two, par)
         done = [chunk(functools.partial(jnp.int32, i), *args) for i in range(cols // 16)]
         color = jnp.concatenate([c for c, _ in done])
         trans = jnp.concatenate([jnp.transpose(t[:, :16]) for _, t in done])
         return butterfly(color, trans)
     nc = cols // slabs
     picks = [functools.partial(lookup, [order[slot] for order in PIECE]) for slot in range(4)]
-    hid, w1, w2, par = head(
-        picks[0], nc, volume, conv_one, conv_two, bias_one, bias_two, opacity_weight, opacity_bias
+    offsets = jnp.broadcast_to(opacity_bias[:, None], (planes, ch))
+    hid, w2, par = head(
+        picks[0], nc, volume, w1, conv_two, b1, bias_two, opacity_weight, offsets
     )
 
     def piece(slot, packed):

time: 34.4 us -> 33.3 us (0.968)
  Pallas kernels: 18.1 us -> 16.9 us
  starting transfers between devices: 10.7 us -> 11.3 us
  waiting for transfers between devices: 5.14 us -> 4.56 us
    pallas_call x5, Pallas kernels: 14.9 us -> 13.5 us  [call(): pl.pallas_call(kernel, out_shape=out_shape, in_specs=in_specs, out_specs=...]
    ppermute x1, waiting for transfers between devices: 5.13 us -> 4.09 us  [per_device(): third = lax.ppermute(merge(*piece(2, False), far), 'depth', THIRD)]
    ppermute x1, starting transfers between devices: 3.21 us -> 3.82 us  [per_device(): far = lax.ppermute(first, 'depth', FAR)]
    ppermute x1, waiting for transfers between devices: 0.01 us -> 0.46 us  [per_device(): two = lax.ppermute(two, 'rows', inner + [(j, i) for i, j in inner])]
  transfers between devices with their start and end apart: 6 -> 6, of which waited for: 1 -> 2; matrix products, arithmetic and copies ran while one was open for 0% -> 0% of each run, Pallas kernels for 40% -> 37%
where the time goes in v6:
time: 33.3 us; the launch traced here: 33.1 us
  Pallas kernels  16.9 us (51%)
  starting transfers between devices  11.3 us (34%)
  waiting for transfers between devices  4.56 us (14%)
    pallas_call x5, Pallas kernels, call(): pl.pallas_call(kernel, out_shape=out_shape, in_specs=in_specs, out_specs=...  13.5 us
    ppermute x1, starting transfers between devices, per_device(): two = lax.ppermute(two, 'rows', inner + [(j, i) for i, j in inner])  4.47 us
    ppermute x1, waiting for transfers between devices, per_device(): third = lax.ppermute(merge(*piece(2, False), far), 'depth', THIRD)  4.09 us
    ppermute x1, starting transfers between devices, per_device(): far = lax.ppermute(first, 'depth', FAR)  3.82 us
    ppermute x1, starting transfers between devices, per_device(): second = lax.ppermute(second, 'depth', SECOND)  1.81 us
    pallas_call x1, Pallas kernels, edges(): pl.pallas_call(edges_kernel, out_shape=(shape, shape, jax.ShapeDtypeStruc...  1.24 us
    pallas_call x1, Pallas kernels, combine(): pl.pallas_call(finish_kernel, out_shape=color, in_specs=[VM] * 3, out_spe...  1.12 us
    ppermute x1, starting transfers between devices, per_device(): near = lax.ppermute(first, 'depth', NEAR)  0.68 us
  transfers between devices with their start and end apart: 6, of which 2 were waited for; matrix products, arithmetic and copies ran while one was open for 0% of the time, Pallas kernels for 37%

profile of v6, /device:TPU:1, one launch (start us, length us, event | category | flops | bytes accessed | tf_op | source)
XLA Modules:
  0.0 33.1 jit_solution(9895566602676970866)
XLA Ops:
  0.0 0.0 copy-start
  0.0 0.0 copy-start.1
  0.0 1.2 %shard_map.73 = (bf16[2,64,2,128]{3,2,1,0:T(2,128)(2,1)S(1)}, bf16[2,64,2,128]{3,2,1,0:T(2,128)(2,1)S(1)}, bf16[3,3,128,128]{3,2,1,0:T(8,128)(2,1)S(1)}, f32[1,128]{1,0:T(1,128)S(1)}) custom-call(bf16[2,64,64,128]{3,2,1,0:T(8,128)(2,1)} %x_ref.9, bf16[3,3,128,128]{3,2,1,0:T(8,128)(2,1)} %w_hbm.1, f32[128]{0:T(128)} %b_hbm.1), custom_call_target="tpu_custom_call" | custom-call | tf_op jit(solution)/shard_map/pallas_call | solution.py:70
  1.3 0.1 collective-permute-start
  1.4 4.5 %collective-permute-start.1 = (bf16[2,64,2,128]{3,2,1,0:T(2,128)(2,1)S(1)}, bf16[2,64,2,128]{3,2,1,0:T(2,128)(2,1)S(1)}, u32[]{:S(2)}, u32[]{:S(2)}) collective-permute-start(bf16[2,64,2,128]{3,2,1,0:T(2,128)(2,1)S(1)} %get-tuple-element.19), channel_id=1, source_target_pairs={{1,2},{2,1},{5,6},{6,5},{9,10},{10,9},{13,14},{14,13},{17,18},{18,... | collective-permute-start | bytes 196616 | tf_op jit(solution)/shard_map/ppermute | solution.py:509
  5.8 0.0 copy-done.1
  5.9 0.1 broadcast_in_dim.2.ob_ref
  5.9 0.0 copy-done
  5.9 1.4 %shard_map.74 = (f32[2,18,80,128]{3,2,1,0:T(8,128)S(1)}, bf16[3,3,128,128]{3,2,1,0:T(8,128)(2,1)S(1)}, f32[5,128]{1,0:T(8,128)S(1)}) custom-call(bf16[2,64,64,128]{3,2,1,0:T(8,128)(2,1)S(1)} %copy-done, bf16[3,3,128,128]{3,2,1,0:T(8,128)(2,1)S(1)} %get-tuple-element.20.w1_ref, f32[1,128]{1,0:T(1,128)S(1)} %get-tuple-element.21.b1_ref, ...), custom_call_target="tpu_custom_call" | custom-call | flops 5000000000 | bytes 1000000 | tf_op jit(solution)/shard_map/pallas_call | solution.py:180
  7.3 0.0 collective-permute-done.one_ref
  7.3 0.5 %collective-permute-done.1.two_ref = bf16[2,64,2,128]{3,2,1,0:T(2,128)(2,1)S(1)} collective-permute-done((bf16[2,64,2,128]{3,2,1,0:T(2,128)(2,1)S(1)}, bf16[2,64,2,128]{3,2,1,0:T(2,128)(2,1)S(1)}, u32[]{:S(2)}, u32[]{:S(2)}) %collective-permute-start.1) | collective-permute-done | bytes 65568 | tf_op jit(solution)/shard_map/ppermute | solution.py:509
  7.8 2.3 %shard_map.76 = bf16[1040,128]{1,0:T(8,128)(2,1)S(1)} custom-call(bf16[2,64,64,128]{3,2,1,0:T(8,128)(2,1)S(1)} %copy-done, bf16[2,64,2,128]{3,2,1,0:T(2,128)(2,1)S(1)} %collective-permute-done.one_ref, bf16[2,64,2,128]{3,2,1,0:T(2,128)(2,1)S(1)} %collective-permute-done.1.two_ref, f32[2,18,80,128]{3,2,1,0:T(8,128)S(1)} %get-tuple-element.26.hid_ref, ...), custom_call_target="tpu_custom_call" | custom-call | flops 5000000000 | bytes 1000000 | tf_op jit(solution)/shard_map/pallas_call | solution.py:180
  10.1 3.8 %collective-permute-start.4 = (bf16[1040,128]{1,0:T(8,128)(2,1)S(1)}, bf16[1040,128]{1,0:T(8,128)(2,1)S(1)}, u32[]{:S(2)}, u32[]{:S(2)}) collective-permute-start(bf16[1040,128]{1,0:T(8,128)(2,1)S(1)} %shard_map.76), channel_id=1, source_target_pairs={{0,4},{12,8},{1,5},{13,9},{2,6},{14,10},{3,7},{15,11},{16,20},{28,... | collective-permute-start | bytes 798728 | tf_op jit(solution)/shard_map/ppermute | solution.py:534
  13.9 0.7 %collective-permute-start.2 = (bf16[1040,128]{1,0:T(8,128)(2,1)S(1)}, bf16[1040,128]{1,0:T(8,128)(2,1)S(1)}, u32[]{:S(2)}, u32[]{:S(2)}) collective-permute-start(bf16[1040,128]{1,0:T(8,128)(2,1)S(1)} %shard_map.76), channel_id=1, source_target_pairs={{4,8},{8,4},{5,9},{9,5},{6,10},{10,6},{7,11},{11,7},{20,24},{24,20... | collective-permute-start | bytes 798728 | tf_op jit(solution)/shard_map/ppermute | solution.py:535
  14.6 3.3 %shard_map.77 = bf16[1040,128]{1,0:T(8,128)(2,1)S(1)} custom-call(bf16[2,64,64,128]{3,2,1,0:T(8,128)(2,1)S(1)} %copy-done, bf16[2,64,2,128]{3,2,1,0:T(2,128)(2,1)S(1)} %collective-permute-done.one_ref, bf16[2,64,2,128]{3,2,1,0:T(2,128)(2,1)S(1)} %collective-permute-done.1.two_ref, bf16[3,3,128,128]{3,2,1,0:T(8,128)(2,1)S(1)} %get-tuple-element.20.w1_ref, ...), custom_call_target="tpu_custom_call" | custom-call | flops 5000000000 | bytes 1000000 | tf_op jit(solution)/shard_map/pallas_call | solution.py:180
  17.9 1.8 %collective-permute-start.3 = (bf16[1040,128]{1,0:T(8,128)(2,1)S(1)}, bf16[1040,128]{1,0:T(8,128)(2,1)S(1)}, u32[]{:S(2)}, u32[]{:S(2)}) collective-permute-start(bf16[1040,128]{1,0:T(8,128)(2,1)S(1)} %shard_map.77), channel_id=1, source_target_pairs={{0,8},{12,4},{4,0},{8,12},{1,9},{13,5},{5,1},{9,13},{2,10},{14,6},... | collective-permute-start | bytes 798728 | tf_op jit(solution)/shard_map/ppermute | solution.py:537
  19.7 3.3 %shard_map.79 = (f32[16,64,128]{2,1,0:T(8,128)S(1)}, f32[64,128]{1,0:T(8,128)S(1)}) custom-call(bf16[2,64,64,128]{3,2,1,0:T(8,128)(2,1)S(1)} %copy-done, bf16[2,64,2,128]{3,2,1,0:T(2,128)(2,1)S(1)} %collective-permute-done.one_ref, bf16[2,64,2,128]{3,2,1,0:T(2,128)(2,1)S(1)} %collective-permute-done.1.two_ref, ...), custom_call_target="tpu_custom_call" | custom-call | flops 5000000000 | bytes 1000000 | tf_op jit(solution)/shard_map/pallas_call | solution.py:180
  23.0 0.0 collective-permute-done.4.got_ref
  23.0 0.5 %shard_map.80 = bf16[1040,128]{1,0:T(8,128)(2,1)S(1)} custom-call(f32[16,64,128]{2,1,0:T(8,128)S(1)} %get-tuple-element.29.own_ref, f32[64,128]{1,0:T(8,128)S(1)} %get-tuple-element.30.trans_ref, bf16[1040,128]{1,0:T(8,128)(2,1)S(1)} %collective-permute-done.4.got_ref), custom_call_target="tpu_custom_call" | custom-call | flops 1000000000 | bytes 1000000 | tf_op jit(solution)/shard_map/pallas_call | solution.py:395
  23.5 0.4 %collective-permute-start.5 = (bf16[1040,128]{1,0:T(8,128)(2,1)S(1)}, bf16[1040,128]{1,0:T(8,128)(2,1)S(1)}, u32[]{:S(2)}, u32[]{:S(2)}) collective-permute-start(bf16[1040,128]{1,0:T(8,128)(2,1)S(1)} %shard_map.80), channel_id=1, source_target_pairs={{0,4},{12,8},{4,12},{8,0},{1,5},{13,9},{5,13},{9,1},{2,6},{14,10},... | collective-permute-start | bytes 798728 | tf_op jit(solution)/shard_map/ppermute | solution.py:538
  23.8 3.2 %shard_map.75 = (f32[16,64,128]{2,1,0:T(8,128)S(1)}, f32[64,128]{1,0:T(8,128)S(1)}) custom-call(bf16[2,64,64,128]{3,2,1,0:T(8,128)(2,1)S(1)} %copy-done, bf16[2,64,2,128]{3,2,1,0:T(2,128)(2,1)S(1)} %collective-permute-done.one_ref, bf16[2,64,2,128]{3,2,1,0:T(2,128)(2,1)S(1)} %collective-permute-done.1.two_ref, ...), custom_call_target="tpu_custom_call" | custom-call | flops 5000000000 | bytes 1000000 | tf_op jit(solution)/shard_map/pallas_call | solution.py:180
  27.1 0.0 collective-permute-done.3.refs_1_
  27.1 0.0 collective-permute-done.2.refs_0_
  27.1 0.6 %shard_map.78 = (f32[16,64,128]{2,1,0:T(8,128)S(1)}, f32[64,128]{1,0:T(8,128)S(1)}) custom-call(f32[16,64,128]{2,1,0:T(8,128)S(1)} %get-tuple-element.24.own_ref, f32[64,128]{1,0:T(8,128)S(1)} %get-tuple-element.25.trans_ref, bf16[1040,128]{1,0:T(8,128)(2,1)S(1)} %collective-permute-done.2.refs_0_, bf16[1040,128]{1,0:T(8,128)(2,1)S(1)} %collective-permute-done.3.refs_1_), custom_call_target="tpu_custom_call" | custom-call | flops 1000000000 | bytes 1000000 | tf_op jit(solution)/shard_map/pallas_call | solution.py:452
  27.7 4.1 %collective-permute-done.5.got_ref = bf16[1040,128]{1,0:T(8,128)(2,1)S(1)} collective-permute-done((bf16[1040,128]{1,0:T(8,128)(2,1)S(1)}, bf16[1040,128]{1,0:T(8,128)(2,1)S(1)}, u32[]{:S(2)}, u32[]{:S(2)}) %collective-permute-start.5) | collective-permute-done | bytes 266272 | tf_op jit(solution)/shard_map/ppermute | solution.py:538
  31.8 1.1 %shard_map.81 = f32[16,64,128]{2,1,0:T(8,128)} custom-call(f32[16,64,128]{2,1,0:T(8,128)S(1)} %get-tuple-element.27.near_ref, f32[64,128]{1,0:T(8,128)S(1)} %get-tuple-element.28.trans_ref, bf16[1040,128]{1,0:T(8,128)(2,1)S(1)} %collective-permute-done.5.got_ref), custom_call_target="tpu_custom_call" | custom-call | tf_op jit(solution)/shard_map/pallas_call | solution.py:460
Async XLA Ops:
  0.0 5.9 %copy-start = (bf16[2,64,64,128]{3,2,1,0:T(8,128)(2,1)S(1)}, bf16[2,64,64,128]{3,2,1,0:T(8,128)(2,1)}, u32[]{:S(2)}) copy-start(bf16[2,64,64,128]{3,2,1,0:T(8,128)(2,1)} %x_ref.9) | copy-start | bytes 6291460
  0.0 5.8 %copy-start.1 = (f32[2]{0:T(128)S(1)}, f32[2]{0:T(128)}, u32[]{:S(2)}) copy-start(f32[2]{0:T(128)} %param.13) | copy-start | bytes 28
  1.3 6.1 %collective-permute-start = (bf16[2,64,2,128]{3,2,1,0:T(2,128)(2,1)S(1)}, bf16[2,64,2,128]{3,2,1,0:T(2,128)(2,1)S(1)}, u32[]{:S(2)}, u32[]{:S(2)}) collective-permute-start(bf16[2,64,2,128]{3,2,1,0:T(2,128)(2,1)S(1)} %get-tuple-element.18), channel_id=1, source_target_pairs={{0,1},{1,0},{2,3},{3,2},{4,5},{5,4},{6,7},{7,6},{8,9},{9,8},{10,11... | collective-permute-start | bytes 196616 | tf_op jit(solution)/shard_map/ppermute | solution.py:510
  1.4 6.4 %collective-permute-start.1 = (bf16[2,64,2,128]{3,2,1,0:T(2,128)(2,1)S(1)}, bf16[2,64,2,128]{3,2,1,0:T(2,128)(2,1)S(1)}, u32[]{:S(2)}, u32[]{:S(2)}) collective-permute-start(bf16[2,64,2,128]{3,2,1,0:T(2,128)(2,1)S(1)} %get-tuple-element.19), channel_id=1, source_target_pairs={{1,2},{2,1},{5,6},{6,5},{9,10},{10,9},{13,14},{14,13},{17,18},{18,... | collective-permute-start | bytes 196616 | tf_op jit(solution)/shard_map/ppermute | solution.py:509
  10.1 12.9 %collective-permute-start.4 = (bf16[1040,128]{1,0:T(8,128)(2,1)S(1)}, bf16[1040,128]{1,0:T(8,128)(2,1)S(1)}, u32[]{:S(2)}, u32[]{:S(2)}) collective-permute-start(bf16[1040,128]{1,0:T(8,128)(2,1)S(1)} %shard_map.76), channel_id=1, source_target_pairs={{0,4},{12,8},{1,5},{13,9},{2,6},{14,10},{3,7},{15,11},{16,20},{28,... | collective-permute-start | bytes 798728 | tf_op jit(solution)/shard_map/ppermute | solution.py:534
  13.9 13.2 %collective-permute-start.2 = (bf16[1040,128]{1,0:T(8,128)(2,1)S(1)}, bf16[1040,128]{1,0:T(8,128)(2,1)S(1)}, u32[]{:S(2)}, u32[]{:S(2)}) collective-permute-start(bf16[1040,128]{1,0:T(8,128)(2,1)S(1)} %shard_map.76), channel_id=1, source_target_pairs={{4,8},{8,4},{5,9},{9,5},{6,10},{10,6},{7,11},{11,7},{20,24},{24,20... | collective-permute-start | bytes 798728 | tf_op jit(solution)/shard_map/ppermute | solution.py:535
  17.9 9.2 %collective-permute-start.3 = (bf16[1040,128]{1,0:T(8,128)(2,1)S(1)}, bf16[1040,128]{1,0:T(8,128)(2,1)S(1)}, u32[]{:S(2)}, u32[]{:S(2)}) collective-permute-start(bf16[1040,128]{1,0:T(8,128)(2,1)S(1)} %shard_map.77), channel_id=1, source_target_pairs={{0,8},{12,4},{4,0},{8,12},{1,9},{13,5},{5,1},{9,13},{2,10},{14,6},... | collective-permute-start | bytes 798728 | tf_op jit(solution)/shard_map/ppermute | solution.py:537
  23.5 8.3 %collective-permute-start.5 = (bf16[1040,128]{1,0:T(8,128)(2,1)S(1)}, bf16[1040,128]{1,0:T(8,128)(2,1)S(1)}, u32[]{:S(2)}, u32[]{:S(2)}) collective-permute-start(bf16[1040,128]{1,0:T(8,128)(2,1)S(1)} %shard_map.80), channel_id=1, source_target_pairs={{0,4},{12,8},{4,12},{8,0},{1,5},{13,9},{5,13},{9,1},{2,6},{14,10},... | collective-permute-start | bytes 798728 | tf_op jit(solution)/shard_map/ppermute | solution.py:538

commit v7 on v6

--- a/solution.py
+++ b/solution.py
@@ -129,7 +129,7 @@
     lane = lax.broadcasted_iota(jnp.int32, (rows, ch), 1)
     weights = pair_weights(w2_ref)
     through = jnp.zeros((rows, ch), F32)
-    cuts = [nc // 2 * i // 4 for i in range(4 + 1)]
+    cuts = [nc // 2 * i // 3 for i in range(3 + 1)]
     for lo, hi in zip(cuts, cuts[1:]):
         logits = [jnp.zeros((rows, ch), F32) for _ in range(planes)]
         taps = []

time: 33.3 us -> 33.3 us (level)
  transfers between devices with their start and end apart: 6 -> 6, of which waited for: 2 -> 2; matrix products, arithmetic and copies ran while one was open for 0% -> 0% of each run, Pallas kernels for 37% -> 36%
where the time goes in v7:
time: 33.3 us; the launch traced here: 33.1 us
  Pallas kernels  16.8 us (50%)
  starting transfers between devices  11.3 us (34%)
  waiting for transfers between devices  4.7 us (14%)
    pallas_call x5, Pallas kernels, call(): pl.pallas_call(kernel, out_shape=out_shape, in_specs=in_specs, out_specs=...  13.3 us
    ppermute x1, starting transfers between devices, per_device(): two = lax.ppermute(two, 'rows', inner + [(j, i) for i, j in inner])  4.47 us
    ppermute x1, waiting for transfers between devices, per_device(): third = lax.ppermute(merge(*piece(2, False), far), 'depth', THIRD)  4.24 us
    ppermute x1, starting transfers between devices, per_device(): far = lax.ppermute(first, 'depth', FAR)  3.83 us
    ppermute x1, starting transfers between devices, per_device(): second = lax.ppermute(second, 'depth', SECOND)  1.81 us
    pallas_call x1, Pallas kernels, edges(): pl.pallas_call(edges_kernel, out_shape=(shape, shape, jax.ShapeDtypeStruc...  1.24 us
    pallas_call x1, Pallas kernels, combine(): pl.pallas_call(finish_kernel, out_shape=color, in_specs=[VM] * 3, out_spe...  1.12 us
    ppermute x1, starting transfers between devices, per_device(): near = lax.ppermute(first, 'depth', NEAR)  0.68 us
  transfers between devices with their start and end apart: 6, of which 2 were waited for; matrix products, arithmetic and copies ran while one was open for 0% of the time, Pallas kernels for 36%

profile of v7, /device:TPU:1, one launch (start us, length us, event | category | flops | bytes accessed | tf_op | source)
XLA Modules:
  0.0 33.1 jit_solution(15069600058508196271)
XLA Ops:
  0.0 0.0 copy-start
  0.0 0.0 copy-start.1
  0.0 1.2 %shard_map.73 = (bf16[2,64,2,128]{3,2,1,0:T(2,128)(2,1)S(1)}, bf16[2,64,2,128]{3,2,1,0:T(2,128)(2,1)S(1)}, bf16[3,3,128,128]{3,2,1,0:T(8,128)(2,1)S(1)}, f32[1,128]{1,0:T(1,128)S(1)}) custom-call(bf16[2,64,64,128]{3,2,1,0:T(8,128)(2,1)} %x_ref.9, bf16[3,3,128,128]{3,2,1,0:T(8,128)(2,1)} %w_hbm.1, f32[128]{0:T(128)} %b_hbm.1), custom_call_target="tpu_custom_call" | custom-call | tf_op jit(solution)/shard_map/pallas_call | solution.py:70
  1.3 0.1 collective-permute-start
  1.4 4.5 %collective-permute-start.1 = (bf16[2,64,2,128]{3,2,1,0:T(2,128)(2,1)S(1)}, bf16[2,64,2,128]{3,2,1,0:T(2,128)(2,1)S(1)}, u32[]{:S(2)}, u32[]{:S(2)}) collective-permute-start(bf16[2,64,2,128]{3,2,1,0:T(2,128)(2,1)S(1)} %get-tuple-element.19), channel_id=1, source_target_pairs={{1,2},{2,1},{5,6},{6,5},{9,10},{10,9},{13,14},{14,13},{17,18},{18,... | collective-permute-start | bytes 196616 | tf_op jit(solution)/shard_map/ppermute | solution.py:509
  5.8 0.0 copy-done.1
  5.9 0.1 broadcast_in_dim.2.ob_ref
  5.9 0.0 copy-done
  5.9 1.4 %shard_map.74 = (f32[2,18,80,128]{3,2,1,0:T(8,128)S(1)}, bf16[3,3,128,128]{3,2,1,0:T(8,128)(2,1)S(1)}, f32[5,128]{1,0:T(8,128)S(1)}) custom-call(bf16[2,64,64,128]{3,2,1,0:T(8,128)(2,1)S(1)} %copy-done, bf16[3,3,128,128]{3,2,1,0:T(8,128)(2,1)S(1)} %get-tuple-element.20.w1_ref, f32[1,128]{1,0:T(1,128)S(1)} %get-tuple-element.21.b1_ref, ...), custom_call_target="tpu_custom_call" | custom-call | flops 5000000000 | bytes 1000000 | tf_op jit(solution)/shard_map/pallas_call | solution.py:180
  7.3 0.0 collective-permute-done.one_ref
  7.3 0.5 %collective-permute-done.1.two_ref = bf16[2,64,2,128]{3,2,1,0:T(2,128)(2,1)S(1)} collective-permute-done((bf16[2,64,2,128]{3,2,1,0:T(2,128)(2,1)S(1)}, bf16[2,64,2,128]{3,2,1,0:T(2,128)(2,1)S(1)}, u32[]{:S(2)}, u32[]{:S(2)}) %collective-permute-start.1) | collective-permute-done | bytes 65568 | tf_op jit(solution)/shard_map/ppermute | solution.py:509
  7.8 2.3 %shard_map.76 = bf16[1040,128]{1,0:T(8,128)(2,1)S(1)} custom-call(bf16[2,64,64,128]{3,2,1,0:T(8,128)(2,1)S(1)} %copy-done, bf16[2,64,2,128]{3,2,1,0:T(2,128)(2,1)S(1)} %collective-permute-done.one_ref, bf16[2,64,2,128]{3,2,1,0:T(2,128)(2,1)S(1)} %collective-permute-done.1.two_ref, f32[2,18,80,128]{3,2,1,0:T(8,128)S(1)} %get-tuple-element.26.hid_ref, ...), custom_call_target="tpu_custom_call" | custom-call | flops 5000000000 | bytes 1000000 | tf_op jit(solution)/shard_map/pallas_call | solution.py:180
  10.1 3.8 %collective-permute-start.4 = (bf16[1040,128]{1,0:T(8,128)(2,1)S(1)}, bf16[1040,128]{1,0:T(8,128)(2,1)S(1)}, u32[]{:S(2)}, u32[]{:S(2)}) collective-permute-start(bf16[1040,128]{1,0:T(8,128)(2,1)S(1)} %shard_map.76), channel_id=1, source_target_pairs={{0,4},{12,8},{1,5},{13,9},{2,6},{14,10},{3,7},{15,11},{16,20},{28,... | collective-permute-start | bytes 798728 | tf_op jit(solution)/shard_map/ppermute | solution.py:534
  14.0 0.7 %collective-permute-start.2 = (bf16[1040,128]{1,0:T(8,128)(2,1)S(1)}, bf16[1040,128]{1,0:T(8,128)(2,1)S(1)}, u32[]{:S(2)}, u32[]{:S(2)}) collective-permute-start(bf16[1040,128]{1,0:T(8,128)(2,1)S(1)} %shard_map.76), channel_id=1, source_target_pairs={{4,8},{8,4},{5,9},{9,5},{6,10},{10,6},{7,11},{11,7},{20,24},{24,20... | collective-permute-start | bytes 798728 | tf_op jit(solution)/shard_map/ppermute | solution.py:535
  14.7 3.2 %shard_map.77 = bf16[1040,128]{1,0:T(8,128)(2,1)S(1)} custom-call(bf16[2,64,64,128]{3,2,1,0:T(8,128)(2,1)S(1)} %copy-done, bf16[2,64,2,128]{3,2,1,0:T(2,128)(2,1)S(1)} %collective-permute-done.one_ref, bf16[2,64,2,128]{3,2,1,0:T(2,128)(2,1)S(1)} %collective-permute-done.1.two_ref, bf16[3,3,128,128]{3,2,1,0:T(8,128)(2,1)S(1)} %get-tuple-element.20.w1_ref, ...), custom_call_target="tpu_custom_call" | custom-call | flops 5000000000 | bytes 1000000 | tf_op jit(solution)/shard_map/pallas_call | solution.py:180
  17.9 1.8 %collective-permute-start.3 = (bf16[1040,128]{1,0:T(8,128)(2,1)S(1)}, bf16[1040,128]{1,0:T(8,128)(2,1)S(1)}, u32[]{:S(2)}, u32[]{:S(2)}) collective-permute-start(bf16[1040,128]{1,0:T(8,128)(2,1)S(1)} %shard_map.77), channel_id=1, source_target_pairs={{0,8},{12,4},{4,0},{8,12},{1,9},{13,5},{5,1},{9,13},{2,10},{14,6},... | collective-permute-start | bytes 798728 | tf_op jit(solution)/shard_map/ppermute | solution.py:537
  19.7 3.2 %shard_map.79 = (f32[16,64,128]{2,1,0:T(8,128)S(1)}, f32[64,128]{1,0:T(8,128)S(1)}) custom-call(bf16[2,64,64,128]{3,2,1,0:T(8,128)(2,1)S(1)} %copy-done, bf16[2,64,2,128]{3,2,1,0:T(2,128)(2,1)S(1)} %collective-permute-done.one_ref, bf16[2,64,2,128]{3,2,1,0:T(2,128)(2,1)S(1)} %collective-permute-done.1.two_ref, ...), custom_call_target="tpu_custom_call" | custom-call | flops 5000000000 | bytes 1000000 | tf_op jit(solution)/shard_map/pallas_call | solution.py:180
  22.9 0.0 collective-permute-done.4.got_ref
  22.9 0.5 %shard_map.80 = bf16[1040,128]{1,0:T(8,128)(2,1)S(1)} custom-call(f32[16,64,128]{2,1,0:T(8,128)S(1)} %get-tuple-element.29.own_ref, f32[64,128]{1,0:T(8,128)S(1)} %get-tuple-element.30.trans_ref, bf16[1040,128]{1,0:T(8,128)(2,1)S(1)} %collective-permute-done.4.got_ref), custom_call_target="tpu_custom_call" | custom-call | flops 1000000000 | bytes 1000000 | tf_op jit(solution)/shard_map/pallas_call | solution.py:395
  23.4 0.3 %collective-permute-start.5 = (bf16[1040,128]{1,0:T(8,128)(2,1)S(1)}, bf16[1040,128]{1,0:T(8,128)(2,1)S(1)}, u32[]{:S(2)}, u32[]{:S(2)}) collective-permute-start(bf16[1040,128]{1,0:T(8,128)(2,1)S(1)} %shard_map.80), channel_id=1, source_target_pairs={{0,4},{12,8},{4,12},{8,0},{1,5},{13,9},{5,13},{9,1},{2,6},{14,10},... | collective-permute-start | bytes 798728 | tf_op jit(solution)/shard_map/ppermute | solution.py:538
  23.7 3.2 %shard_map.75 = (f32[16,64,128]{2,1,0:T(8,128)S(1)}, f32[64,128]{1,0:T(8,128)S(1)}) custom-call(bf16[2,64,64,128]{3,2,1,0:T(8,128)(2,1)S(1)} %copy-done, bf16[2,64,2,128]{3,2,1,0:T(2,128)(2,1)S(1)} %collective-permute-done.one_ref, bf16[2,64,2,128]{3,2,1,0:T(2,128)(2,1)S(1)} %collective-permute-done.1.two_ref, ...), custom_call_target="tpu_custom_call" | custom-call | flops 5000000000 | bytes 1000000 | tf_op jit(solution)/shard_map/pallas_call | solution.py:180
  26.9 0.0 collective-permute-done.3.refs_1_
  26.9 0.0 collective-permute-done.2.refs_0_
  26.9 0.6 %shard_map.78 = (f32[16,64,128]{2,1,0:T(8,128)S(1)}, f32[64,128]{1,0:T(8,128)S(1)}) custom-call(f32[16,64,128]{2,1,0:T(8,128)S(1)} %get-tuple-element.24.own_ref, f32[64,128]{1,0:T(8,128)S(1)} %get-tuple-element.25.trans_ref, bf16[1040,128]{1,0:T(8,128)(2,1)S(1)} %collective-permute-done.2.refs_0_, bf16[1040,128]{1,0:T(8,128)(2,1)S(1)} %collective-permute-done.3.refs_1_), custom_call_target="tpu_custom_call" | custom-call | flops 1000000000 | bytes 1000000 | tf_op jit(solution)/shard_map/pallas_call | solution.py:452
  27.6 4.2 %collective-permute-done.5.got_ref = bf16[1040,128]{1,0:T(8,128)(2,1)S(1)} collective-permute-done((bf16[1040,128]{1,0:T(8,128)(2,1)S(1)}, bf16[1040,128]{1,0:T(8,128)(2,1)S(1)}, u32[]{:S(2)}, u32[]{:S(2)}) %collective-permute-start.5) | collective-permute-done | bytes 266272 | tf_op jit(solution)/shard_map/ppermute | solution.py:538
  31.8 1.1 %shard_map.81 = f32[16,64,128]{2,1,0:T(8,128)} custom-call(f32[16,64,128]{2,1,0:T(8,128)S(1)} %get-tuple-element.27.near_ref, f32[64,128]{1,0:T(8,128)S(1)} %get-tuple-element.28.trans_ref, bf16[1040,128]{1,0:T(8,128)(2,1)S(1)} %collective-permute-done.5.got_ref), custom_call_target="tpu_custom_call" | custom-call | tf_op jit(solution)/shard_map/pallas_call | solution.py:460
Async XLA Ops:
  0.0 5.9 %copy-start = (bf16[2,64,64,128]{3,2,1,0:T(8,128)(2,1)S(1)}, bf16[2,64,64,128]{3,2,1,0:T(8,128)(2,1)}, u32[]{:S(2)}) copy-start(bf16[2,64,64,128]{3,2,1,0:T(8,128)(2,1)} %x_ref.9) | copy-start | bytes 6291460
  0.0 5.8 %copy-start.1 = (f32[2]{0:T(128)S(1)}, f32[2]{0:T(128)}, u32[]{:S(2)}) copy-start(f32[2]{0:T(128)} %param.13) | copy-start | bytes 28
  1.3 6.1 %collective-permute-start = (bf16[2,64,2,128]{3,2,1,0:T(2,128)(2,1)S(1)}, bf16[2,64,2,128]{3,2,1,0:T(2,128)(2,1)S(1)}, u32[]{:S(2)}, u32[]{:S(2)}) collective-permute-start(bf16[2,64,2,128]{3,2,1,0:T(2,128)(2,1)S(1)} %get-tuple-element.18), channel_id=1, source_target_pairs={{0,1},{1,0},{2,3},{3,2},{4,5},{5,4},{6,7},{7,6},{8,9},{9,8},{10,11... | collective-permute-start | bytes 196616 | tf_op jit(solution)/shard_map/ppermute | solution.py:510
  1.4 6.4 %collective-permute-start.1 = (bf16[2,64,2,128]{3,2,1,0:T(2,128)(2,1)S(1)}, bf16[2,64,2,128]{3,2,1,0:T(2,128)(2,1)S(1)}, u32[]{:S(2)}, u32[]{:S(2)}) collective-permute-start(bf16[2,64,2,128]{3,2,1,0:T(2,128)(2,1)S(1)} %get-tuple-element.19), channel_id=1, source_target_pairs={{1,2},{2,1},{5,6},{6,5},{9,10},{10,9},{13,14},{14,13},{17,18},{18,... | collective-permute-start | bytes 196616 | tf_op jit(solution)/shard_map/ppermute | solution.py:509
  10.1 12.8 %collective-permute-start.4 = (bf16[1040,128]{1,0:T(8,128)(2,1)S(1)}, bf16[1040,128]{1,0:T(8,128)(2,1)S(1)}, u32[]{:S(2)}, u32[]{:S(2)}) collective-permute-start(bf16[1040,128]{1,0:T(8,128)(2,1)S(1)} %shard_map.76), channel_id=1, source_target_pairs={{0,4},{12,8},{1,5},{13,9},{2,6},{14,10},{3,7},{15,11},{16,20},{28,... | collective-permute-start | bytes 798728 | tf_op jit(solution)/shard_map/ppermute | solution.py:534
  14.0 13.0 %collective-permute-start.2 = (bf16[1040,128]{1,0:T(8,128)(2,1)S(1)}, bf16[1040,128]{1,0:T(8,128)(2,1)S(1)}, u32[]{:S(2)}, u32[]{:S(2)}) collective-permute-start(bf16[1040,128]{1,0:T(8,128)(2,1)S(1)} %shard_map.76), channel_id=1, source_target_pairs={{4,8},{8,4},{5,9},{9,5},{6,10},{10,6},{7,11},{11,7},{20,24},{24,20... | collective-permute-start | bytes 798728 | tf_op jit(solution)/shard_map/ppermute | solution.py:535
  17.9 9.0 %collective-permute-start.3 = (bf16[1040,128]{1,0:T(8,128)(2,1)S(1)}, bf16[1040,128]{1,0:T(8,128)(2,1)S(1)}, u32[]{:S(2)}, u32[]{:S(2)}) collective-permute-start(bf16[1040,128]{1,0:T(8,128)(2,1)S(1)} %shard_map.77), channel_id=1, source_target_pairs={{0,8},{12,4},{4,0},{8,12},{1,9},{13,5},{5,1},{9,13},{2,10},{14,6},... | collective-permute-start | bytes 798728 | tf_op jit(solution)/shard_map/ppermute | solution.py:537
  23.4 8.4 %collective-permute-start.5 = (bf16[1040,128]{1,0:T(8,128)(2,1)S(1)}, bf16[1040,128]{1,0:T(8,128)(2,1)S(1)}, u32[]{:S(2)}, u32[]{:S(2)}) collective-permute-start(bf16[1040,128]{1,0:T(8,128)(2,1)S(1)} %shard_map.80), channel_id=1, source_target_pairs={{0,4},{12,8},{4,12},{8,0},{1,5},{13,9},{5,13},{9,1},{2,6},{14,10},... | collective-permute-start | bytes 798728 | tf_op jit(solution)/shard_map/ppermute | solution.py:538
